TPU v7x, 32 devices: a whole 2x2x4 slice. The times are simulated.
32 devices in a mesh: aux: 32 (over z, y, x, core).
Axes of the slice: x: 2, y: 2, z: 4, core: 2. Of those that a mesh axis runs over, the one named last changes fastest.
Arguments:
- state: float32 [32, 2, 256, 256], P('aux'), may hold values from -6 to 6
- h_static: float32 [2, 256, 256], replicated, may hold values from -0.375 to 0.375
- drive_op: float32 [2, 256, 256], replicated, may hold values from -0.375 to 0.375
- couple: float32 [3, 256, 256], replicated, may hold values from -0.375 to 0.375
- bath_coef: float32 [2, 3], replicated, may hold values from -2 to 2
- damping: float32 [3], replicated, may hold values from 0.3 to 3
- occupation: int32 [32, 3], P('aux'), may hold values from 1 to 3
- raise_nbr: int32 [32, 3], P('aux'), may hold values from -1 to 31, as said below
- lower_nbr: int32 [32, 3], P('aux'), may hold values from -1 to 31, as said below
Outputs:
- new_state: float32 [32, 2, 256, 256], P('aux')
Inputs may be any that keep to these rules, and one draw needn't show every extreme that they name: `raise_nbr`: each entry is -1 or the index of an auxiliary matrix held on a device 1 to 2 after its own holder (auxiliary a is held by device a); the first mode's entry is -1 only on the last 2 devices. `lower_nbr`: each entry is -1 or the index of an auxiliary matrix held on a device 1 to 2 before its own holder (auxiliary a is held by device a); the first mode's entry is -1 only on the first 2 devices.
All inputs are finite; a program needn't handle non-finite values.
Results may differ from a plain program's by a relative error of at most 0.0003.
Values sent between devices are 32-bit elements; how exact they have to be, the bound alone decides.
No kernel may reach another device: no remote copies, remote signals or barrier semaphores. Data moves between devices by JAX's collectives and lax.ppermute only.
A program may use at most 64 MiB of HBM per device.

v0:
```python
import math
from functools import partial

import jax
import jax.numpy as jnp
from jax import lax
from jax.experimental import pallas as pl
from jax.experimental.pallas import tpu as pltpu
from jax.sharding import PartitionSpec as P


time_step = 0.05
drive_amp = 2.0
drive_freq = 20.0
META = 8
F32 = jnp.float32
BF16 = jnp.bfloat16
VMEM = pl.BlockSpec(memory_space=pltpu.VMEM)
SMEM = pl.BlockSpec(memory_space=pltpu.SMEM)


def chip_of(problem, block):
    group, odd = block >> 1, block & 1
    return group * 4 + problem * 2 + (odd ^ (group & 1))


def device_of(problem, block, pair):
    return chip_of(problem, block) * 2 + ((block & 1) ^ pair)


def role_of(device):
    core, x, problem, group = device & 1, (device >> 1) & 1, (device >> 2) & 1, device >> 3
    odd = x ^ (group & 1)
    return problem, 2 * group + odd, core ^ odd


def permutations(count):
    blocks = count // 4
    first, second, link = [], [], []
    for device in range(count):
        block, half, slot = device >> 2, (device >> 1) & 1, device & 1
        first.append((device, device_of(slot, block, half)))
        second.append((device, device_of(1 - slot, block, half)))
    for problem in range(2):
        for block in range(blocks - 1):
            here, there = device_of(problem, block, 1), device_of(problem, block + 1, 0)
            link += [(here, there), (there, here)]
    for block, pair in ((0, 0), (blocks - 1, 1)):
        here, there = device_of(0, block, pair), device_of(1, block, pair)
        link += [(here, there), (there, here)]
    core = [(device, device ^ 1) for device in range(count)]
    return full(first), full(second), sorted(link), core


def full(pairs):
    fixed = [a for a, b in pairs if a == b]
    swaps = dict(zip(fixed[::2], fixed[1::2]))
    swaps.update({b: a for a, b in swaps.items()})
    return [(a, swaps.get(a, b)) for a, b in pairs]


def kept(device):
    block, half, slot = device >> 2, (device >> 1) & 1, device & 1
    return device_of(slot, block, half) == device, device_of(1 - slot, block, half) == device


def flipped(pairs):
    return sorted((b, a) for a, b in pairs)


def split(value):
    high = value.astype(BF16)
    return high, (value - high.astype(F32)).astype(BF16)


def store_stack(ref, index, w_re, w_im=None):
    size = w_re.shape[0]
    for place, value in enumerate((w_re,) if w_im is None else (w_re, w_im, w_re + w_im)):
        high, low = split(value)
        ref[index, 2 * place * size : (2 * place + 1) * size] = high
        ref[index, (2 * place + 1) * size : (2 * place + 2) * size] = low


def dot_nn(a, b):
    return lax.dot_general(a, b, (((1,), (0,)), ((), ())), preferred_element_type=F32)


def dot_nt(a, b):
    return lax.dot_general(a, b, (((1,), (1,)), ((), ())), preferred_element_type=F32)


def three(stack, place, source, dot):
    high, low = source
    size = high.shape[0]
    both = stack[2 * place * size : (2 * place + 2) * size]
    wide = dot(both, high)
    return wide[:size] + wide[size:] + dot(both[:size], low)


def forms(source, full):
    if not full:
        return (split(source),)
    turned = source.T
    return split(source), split(source + turned), split(source - turned)


def products(stack, source):
    if len(source) == 1:
        return -three(stack, 0, source[0], dot_nt), three(stack, 0, source[0], dot_nn)
    shared = three(stack, 2, source[0], dot_nn)
    return shared - three(stack, 0, source[1], dot_nn), shared - three(stack, 1, source[2], dot_nn)


def role(axis):
    return role_of(lax.axis_index(axis))


def by_type(lower, body):
    @pl.when(lower)
    def _():
        body(True)

    @pl.when(jnp.logical_not(lower))
    def _():
        body(False)


def convert_kernel(state_hbm, occ_hbm, up_hbm, low_hbm, first, second, state, occ, up, low, sems):
    copies = [
        pltpu.make_async_copy(src, dst, sems.at[index])
        for index, (src, dst) in enumerate(((state_hbm, state), (occ_hbm, occ), (up_hbm, up), (low_hbm, low)))
    ]
    for copy in copies:
        copy.start()
    for copy in copies:
        copy.wait()
    slot = lax.axis_index("aux") & 1
    re, im = state[0, 0], state[0, 1]
    size = re.shape[0]
    total, diff = re + im, re - im
    herm = 0.5 * (total + diff.T)
    anti = 0.5 * (total.T - diff)
    first[0:size] = jnp.where(slot == 0, herm, anti)
    second[0:size] = jnp.where(slot == 0, anti, herm)
    lane = lax.broadcasted_iota(jnp.int32, (META, size), 1)
    modes = occ.shape[1]
    row = jnp.zeros((META, size), F32)
    for mode in range(modes):
        for place, table in enumerate((occ, up, low)):
            row = jnp.where(lane == place * modes + mode, table[0, mode].astype(F32), row)
    first[size : size + META] = row
    second[size : size + META] = row


def prepare_kernel(h_static, drive_op, couple, bath_coef, damping, h_a, h_b, h_c, q_out, damp_out):
    h_re = (h_static[0] + h_static[0].T) * 0.5
    h_im = (h_static[1] - h_static[1].T) * 0.5
    v_re = (drive_op[0] + drive_op[0].T) * 0.5
    v_im = (drive_op[1] - drive_op[1].T) * 0.5
    for h_out, moment in ((h_a, 0.0), (h_b, time_step / 2), (h_c, time_step)):
        drive = drive_amp * math.cos(drive_freq * moment)
        store_stack(h_out, 0, h_re + drive * v_re, h_im + drive * v_im)
    for mode in range(couple.shape[0]):
        q = (couple[mode] + couple[mode].T) * 0.5
        q_out[3 * mode] = q
        q_out[3 * mode + 1] = bath_coef[0, mode] * q
        q_out[3 * mode + 2] = bath_coef[1, mode] * q
        damp_out[mode] = jnp.full(damp_out.shape[1:], damping[mode], F32)


def arrive_kernel(which, array, q_ref, damp, h_ref, *refs):
    weights, base, rate, early = refs[-4:]
    problem, block, pair = role("aux")
    part = pair ^ problem ^ which
    size = q_ref.shape[1]
    modes = damp.shape[0]
    meta = array[size : size + 1]

    def entry(place, mode):
        column = place * modes + mode
        return meta[:, column : column + 1]

    total = jnp.zeros((1, 1), F32)
    for mode in range(modes):
        total = total + entry(0, mode) * damp[mode][0:1, 0:1]
    rate[part] = jnp.broadcast_to(total, rate.shape[1:])
    value = array[0:size]
    base[part] = value
    m, p = products(h_ref.at[0], forms(value, True))
    early[part] = m - total * value + p.T

    near = 4 * block + 3 * pair
    inward = 1 - 2 * pair
    twin = near + (1 - part) * inward
    last = jnp.where(part == 0, near + 2 * inward, near + 3 * inward)
    third = jnp.where(part == 0, near - 2 * inward, near + 2 * inward)
    for kind, source in enumerate((twin, near - inward, third, last)):
        source = jnp.where(source < 0, -9, source).astype(F32)
        w_re = jnp.zeros((size, size), F32)
        w_im = jnp.zeros((size, size), F32)
        for mode in range(modes):
            up = jnp.where(entry(1, mode) == source, 1.0, 0.0)
            down = jnp.where(entry(2, mode) == source, entry(0, mode), 0.0)
            w_re = w_re + (up * q_ref[3 * mode] + down * q_ref[3 * mode + 1])
            w_im = w_im + down * q_ref[3 * mode + 2]
        store_stack(weights, 4 * part + kind, w_re, w_im)


N_OWN, N_LINK_N, N_LINK_F, N_PARTNER_F, F_OWN, F_LINK_N, F_PARTNER_F, F_PARTNER_N = range(8)


def term(weights, row, source):
    m, p = products(weights.at[row], source)
    return m + p.T


def cross_kernel(base, weights, early, near_out, far_out):
    _, _, pair = role("aux")

    def body(lower):
        near_out[...] = early[0] + term(weights, N_OWN, forms(base[1], lower))
        far_out[...] = early[1] + term(weights, F_OWN, forms(base[0], not lower))

    by_type(pair == 1, body)


def own_kernel(near, far, h_ref, weights, rate, near_out, far_out):
    _, _, pair = role("aux")
    x_n, x_f = near[...], far[...]
    f_n, f_f = forms(x_n, True), forms(x_f, True)
    m_n, p_n = products(h_ref.at[0], f_n)
    m_f, p_f = products(h_ref.at[0], f_f)
    m_n = m_n - rate[0][0:1, 0:1] * x_n
    m_f = m_f - rate[1][0:1, 0:1] * x_f

    def body(lower):
        m_nf, p_nf = products(weights.at[N_OWN], f_f if lower else f_f[:1])
        m_fn, p_fn = products(weights.at[F_OWN], f_n[:1] if lower else f_n)
        near_out[...] = m_n + m_nf + (p_n + p_nf).T
        far_out[...] = m_f + m_fn + (p_f + p_fn).T

    by_type(pair == 1, body)


def pick(one, two, pair, sorted_already):
    if sorted_already:
        return one[...], two[...]
    problem, _, _ = role("aux")
    size = one.shape[1]
    near_first = pair == problem
    one, two = one[0:size], two[0:size]
    return jnp.where(near_first, one, two), jnp.where(near_first, two, one)


def partner_kernel(sorted_already, one, two, weights, near, far, near_out, far_out):
    _, _, pair = role("aux")
    x_n, x_f = pick(one, two, 1 - pair, sorted_already)

    def body(lower):
        f_n, f_f = forms(x_n, lower), forms(x_f, lower)
        near_out[...] = near[...] + term(weights, N_PARTNER_F, f_f)
        m_a, p_a = products(weights.at[F_PARTNER_F], f_f)
        m_b, p_b = products(weights.at[F_PARTNER_N], f_n)
        far_out[...] = far[...] + m_a + m_b + (p_a + p_b).T

    by_type(pair == 1, body)


def part_kernel(row, source, weights, early, out):
    _, _, pair = role("aux")

    def body(lower):
        out[...] = early[...] + term(weights, row, forms(source[...], lower))

    by_type(pair == 0, body)


def finish_kernel(row, part, step, weight, source, weights, early, base, acc, out, acc_out):
    _, _, pair = role("aux")

    def body(lower):
        slope = early[...] + term(weights, row, forms(source[...], lower))
        out[...] = base[part] + step * slope
        acc_out[...] = (acc[part] if len(acc.shape) == 3 else acc[...]) + weight * slope

    by_type(pair == 0, body)


def first_near_kernel(step, weight, one, two, weights, early, base, out, acc_out):
    _, _, pair = role("aux")
    x_n, x_f = pick(one, two, 1 - pair, False)

    def body(lower):
        m_a, p_a = products(weights.at[N_LINK_N], forms(x_n, lower))
        m_b, p_b = products(weights.at[N_LINK_F], forms(x_f, lower))
        slope = early[...] + m_a + m_b + (p_a + p_b).T
        out[...] = base[0] + step * slope
        acc_out[...] = base[0] + weight * slope

    by_type(pair == 0, body)


def first_far_kernel(step, weight, one, two, weights, early, base, out, acc_out):
    _, _, pair = role("aux")
    x_n, _ = pick(one, two, 1 - pair, False)

    def body(lower):
        slope = early[...] + term(weights, F_LINK_N, forms(x_n, lower))
        out[...] = base[1] + step * slope
        acc_out[...] = base[1] + weight * slope

    by_type(pair == 0, body)


def last_far_kernel(weight, source, weights, early, acc, out):
    _, _, pair = role("aux")

    def body(lower):
        out[...] = acc[...] + weight * (early[...] + term(weights, F_LINK_N, forms(source[...], lower)))

    by_type(pair == 0, body)


def last_near_kernel(weight, source, weights, early, acc, far, first, second):
    problem, _, pair = role("aux")
    near_first = pair == problem

    def body(lower):
        near = acc[...] + weight * (early[...] + term(weights, N_LINK_F, forms(source[...], lower)))
        first[...] = jnp.where(near_first, near, far[...])
        second[...] = jnp.where(near_first, far[...], near)

    by_type(pair == 0, body)


def restore_kernel(first, second, first_sent, second_sent, out):
    device = lax.axis_index("aux")
    slot = device & 1
    keep_first, keep_second = kept(device)
    one = jnp.where(keep_first, first_sent[...], first[...])
    two = jnp.where(keep_second, second_sent[...], second[...])
    herm = jnp.where(slot == 0, one, two)
    anti = jnp.where(slot == 0, two, one)
    total = herm + anti.T
    diff = herm.T - anti
    out[0, 0] = 0.5 * (total + diff)
    out[0, 1] = 0.5 * (total - diff)


def call(kernel, out_shapes, args, smem=(), flops=0, space=None, scratch=(), grant=32, aliases=None):
    shapes = [jax.ShapeDtypeStruct(shape, dtype) for shape, dtype in out_shapes]
    moved = sum(math.prod(a.shape) * a.dtype.itemsize for a in list(args) + shapes)
    single = len(shapes) == 1
    return pl.pallas_call(
        kernel,
        out_shape=shapes[0] if single else shapes,
        in_specs=[space or (SMEM if index in smem else VMEM) for index in range(len(args))],
        out_specs=VMEM if single else [VMEM] * len(shapes),
        scratch_shapes=scratch,
        input_output_aliases=aliases or {},
        cost_estimate=pl.CostEstimate(flops=flops, bytes_accessed=moved, transcendentals=0),
        compiler_params=pltpu.CompilerParams(vmem_limit_bytes=grant * 1024 * 1024),
    )(*args)


def on_device(state, h_static, drive_op, couple, bath_coef, damping, occupation, raise_nbr, lower_nbr):
    count = lax.axis_size("aux")
    size = state.shape[-1]
    modes = couple.shape[0]
    first_to, second_to, link_to, core_to = permutations(count)
    pair_shape = (2, size, size)
    unit = 2 * size**3

    def send(value, pairs):
        return lax.ppermute(value, "aux", pairs)

    tall = ((size + META, size), F32)
    tables = [occupation, raise_nbr, lower_nbr]
    first, second = call(
        convert_kernel,
        [tall, tall],
        [state] + tables,
        space=pl.BlockSpec(memory_space=pltpu.HBM),
        grant=60,
        scratch=[pltpu.VMEM(state.shape, F32)]
        + [pltpu.SMEM(table.shape, jnp.int32) for table in tables]
        + [pltpu.SemaphoreType.DMA((4,))],
    )
    keep_first, keep_second = kept(lax.axis_index("aux"))
    first = jnp.where(keep_first, first, send(first, first_to))
    second = jnp.where(keep_second, second, send(second, second_to))
    *h_now, q_all, damp = call(
        prepare_kernel,
        [((1, 6 * size, size), BF16)] * 3 + [((3 * modes, size, size), F32), ((modes, 8, 128), F32)],
        [h_static, drive_op, couple, bath_coef, damping],
        smem=(3, 4),
    )
    flat = ((size, size), F32)

    held = [((8, 6 * size, size), BF16), (pair_shape, F32), ((2, 8, 128), F32), (pair_shape, F32)]
    state_now = call(partial(arrive_kernel, 0), held, [first, q_all, damp, h_now[0]], flops=9 * unit)
    link = [send(first, link_to)]
    partner = [send(first, core_to)]
    weights, base, rate, early = call(
        partial(arrive_kernel, 1),
        held,
        [second, q_all, damp, h_now[0], *state_now],
        flops=9 * unit,
        aliases={4 + index: index for index in range(4)},
    )
    link.append(send(second, link_to))
    partner.append(send(second, core_to))
    near_e, far_e = call(cross_kernel, [flat, flat], [base, weights, early], flops=15 * unit)
    steps = (time_step / 2, time_step / 2, time_step)
    shares = (time_step / 6, time_step / 3, time_step / 3, time_step / 6)

    def with_partner(stage, near_e, far_e):
        return call(
            partial(partner_kernel, stage > 0), [flat, flat], [*partner, weights, near_e, far_e], flops=27 * unit
        )

    def own(stage, near, far):
        args = [near, far, h_now[(0, 1, 1, 2)[stage]], weights, rate]
        return call(own_kernel, [flat, flat], args, flops=33 * unit)

    def part(row, source, early):
        return call(partial(part_kernel, row), [flat], [source, weights, early], flops=9 * unit)

    def finish(stage, row, which, source, early, acc):
        return call(
            partial(finish_kernel, row, which, steps[stage], shares[stage]),
            [flat, flat],
            [source, weights, early, base, acc],
            flops=9 * unit,
        )

    near_e, far_e = with_partner(0, near_e, far_e)
    near, near_acc = call(
        partial(first_near_kernel, steps[0], shares[0]), [flat, flat], [*link, weights, near_e, base], flops=18 * unit
    )
    far, far_acc = call(
        partial(first_far_kernel, steps[0], shares[0]), [flat, flat], [*link, weights, far_e, base], flops=9 * unit
    )
    link_n, link_f = send(near, link_to), send(far, link_to)
    partner = [send(near, core_to), send(far, core_to)]
    near_e, far_e = with_partner(1, *own(1, near, far))
    far, far_acc = finish(1, F_LINK_N, 1, link_n, far_e, far_acc)
    next_f = send(far, link_to)
    near_e = part(N_LINK_N, link_n, near_e)
    near, near_acc = finish(1, N_LINK_F, 0, link_f, near_e, near_acc)
    link_n, link_f = send(near, link_to), next_f
    partner = [send(near, core_to), send(far, core_to)]
    near_e, far_e = with_partner(2, *own(2, near, far))
    near_e = part(N_LINK_F, link_f, near_e)
    near, near_acc = finish(2, N_LINK_N, 0, link_n, near_e, near_acc)
    far, far_acc = finish(2, F_LINK_N, 1, link_n, far_e, far_acc)
    link_n, link_f = send(near, link_to), send(far, link_to)
    partner = [send(near, core_to), send(far, core_to)]
    near_e, far_e = with_partner(3, *own(3, near, far))
    far = call(partial(last_far_kernel, shares[3]), [flat], [link_n, weights, far_e, far_acc], flops=9 * unit)
    near_e = part(N_LINK_N, link_n, near_e)
    first, second = call(
        partial(last_near_kernel, shares[3]), [flat, flat], [link_f, weights, near_e, near_acc, far], flops=9 * unit
    )
    back = [send(first, flipped(first_to)), send(second, flipped(second_to)), first, second]
    return call(restore_kernel, [((1, 2, size, size), F32)], back)


def solution(mesh):
    return jax.shard_map(
        on_device,
        mesh=mesh,
        in_specs=(
            P("aux", None, None, None),
            P(),
            P(),
            P(),
            P(),
            P(),
            P("aux", None),
            P("aux", None),
            P("aux", None),
        ),
        out_specs=P("aux", None, None, None),
        check_vma=False,
    )
```

profile of v0, /device:TPU:0, one launch (start us, length us, event | category | flops | bytes accessed | tf_op | source)
XLA Modules:
  0.0 79.3 jit_solution(6062840837772737880)
XLA Ops:
  0.0 2.1 %shard_map.91 = (f32[264,256]{1,0:T(8,128)}, f32[264,256]{1,0:T(8,128)}) custom-call(f32[1,2,256,256]{3,2,1,0:T(8,128)} %state_hbm.1, s32[1,3]{1,0:T(1,128)} %occ_hbm.1, s32[1,3]{1,0:T(1,128)} %up_hbm.1, s32[1,3]{1,0:T(1,128)} %low_hbm.1), custom_call_target="tpu_custom_call" | custom-call | bytes 1064996 | tf_op jit(solution)/shard_map/pallas_call | solution.py:354
  2.1 3.1 %collective-permute-start.2 = (f32[264,256]{1,0:T(8,128)}, f32[264,256]{1,0:T(8,128)S(1)}, u32[]{:S(2)}, u32[]{:S(2)}) collective-permute-start(f32[264,256]{1,0:T(8,128)} %get-tuple-element.51), channel_id=1, source_target_pairs={{0,4},{1,0},{2,5},{3,1},{4,7},{5,3},{6,11},{7,2},{8,14},{9,10},{10... | collective-permute-start | bytes 811016 | tf_op jit(solution)/shard_map/ppermute | solution.py:375
  5.8 12.0 %collective-permute-done.2 = f32[264,256]{1,0:T(8,128)S(1)} collective-permute-done((f32[264,256]{1,0:T(8,128)}, f32[264,256]{1,0:T(8,128)S(1)}, u32[]{:S(2)}, u32[]{:S(2)}) %collective-permute-start.2) | collective-permute-done | bytes 270368 | tf_op jit(solution)/shard_map/ppermute | solution.py:375
  17.9 1.0 %broadcast_select_fusion.1.array = f32[264,256]{1,0:T(8,128)S(1)} fusion(f32[264,256]{1,0:T(8,128)} %get-tuple-element.50, f32[264,256]{1,0:T(8,128)S(1)} %collective-permute-done, pred[]{:T(512)S(6)} %eq.6), kind=kLoop, calls=%fused_computation.1 | loop fusion | flops 67584 | bytes 811009 | tf_op jit(solution)/shard_map/jit(_where)/select_n | solution.py:390
  19.0 1.9 %collective-permute-start.3 = (f32[264,256]{1,0:T(8,128)S(1)}, f32[264,256]{1,0:T(8,128)S(1)}, u32[]{:S(2)}, u32[]{:S(2)}) collective-permute-start(f32[264,256]{1,0:T(8,128)S(1)} %broadcast_select_fusion.array), channel_id=1, source_target_pairs={{0,4},{1,3},{2,10},{3,1},{4,0},{5,7},{6,14},{7,5},{8,16},{9,11},{1... | collective-permute-start | bytes 811016 | tf_op jit(solution)/shard_map/ppermute | solution.py:375
  21.1 1.1 %copy-done = f32[3,256,256]{2,1,0:T(8,128)S(1)} copy-done((f32[3,256,256]{2,1,0:T(8,128)S(1)}, f32[3,256,256]{2,1,0:T(8,128)}, u32[]{:S(2)}) %copy-start) | copy-done | bytes 786456
  22.2 1.0 %copy-done.1 = f32[2,256,256]{2,1,0:T(8,128)S(1)} copy-done((f32[2,256,256]{2,1,0:T(8,128)S(1)}, f32[2,256,256]{2,1,0:T(8,128)}, u32[]{:S(2)}) %copy-start.1) | copy-done | bytes 524312
  23.3 1.0 %copy-done.2 = f32[2,256,256]{2,1,0:T(8,128)S(1)} copy-done((f32[2,256,256]{2,1,0:T(8,128)S(1)}, f32[2,256,256]{2,1,0:T(8,128)}, u32[]{:S(2)}) %copy-start.2) | copy-done | bytes 524312
  25.7 1.5 %shard_map.92 = (bf16[1,1536,256]{2,1,0:T(8,128)(2,1)S(1)}, bf16[1,1536,256]{2,1,0:T(8,128)(2,1)S(1)}, bf16[1,1536,256]{2,1,0:T(8,128)(2,1)S(1)}, f32[9,256,256]{2,1,0:T(8,128)S(1)}, f32[3,8,128]{2,1,0:T(8,128)S(1)}) custom-call(f32[2,256,256]{2,1,0:T(8,128)S(1)} %copy-done.1, f32[2,256,256]{2,1,0:T(8,128)S(1)} %copy-done.2, f32[3,256,256]{2,1,0:T(8,128)S(1)} %copy-done, ...), custom_call_target="tpu_custom_call" | custom-call | bytes 6565924 | tf_op jit(solution)/shard_map/pallas_call | solution.py:354
  27.1 2.3 %shard_map.93 = (bf16[8,1536,256]{2,1,0:T(8,128)(2,1)S(1)}, f32[2,256,256]{2,1,0:T(8,128)S(1)}, f32[2,8,128]{2,1,0:T(8,128)S(1)}, f32[2,256,256]{2,1,0:T(8,128)S(1)}) custom-call(f32[264,256]{1,0:T(8,128)S(1)} %broadcast_select_fusion.1.array, f32[9,256,256]{2,1,0:T(8,128)S(1)} %get-tuple-element.52.q_ref, f32[3,8,128]{2,1,0:T(8,128)S(1)} %get-tuple-element.53.damp, ...), custom_call_target="tpu_custom_call" | custom-call | flops 301989888 | bytes 10776576 | tf_op jit(solution)/shard_map/pallas_call | solution.py:354
  29.4 2.3 %shard_map.94 = (bf16[8,1536,256]{2,1,0:T(8,128)(2,1)S(1)}, f32[2,256,256]{2,1,0:T(8,128)S(1)}, f32[2,8,128]{2,1,0:T(8,128)S(1)}, f32[2,256,256]{2,1,0:T(8,128)S(1)}) custom-call(f32[264,256]{1,0:T(8,128)S(1)} %broadcast_select_fusion.array, ...), custom_call_target="tpu_custom_call", output_to_operand_aliasing={{0}: (4, {}), {1}: (5, {}), {2}: (6, {}), {3}: (7, {})} | custom-call | flops 301989888 | bytes 18124800 | tf_op jit(solution)/shard_map/pallas_call | solution.py:354
  32.6 0.9 %shard_map.96 = (f32[256,256]{1,0:T(8,128)S(1)}, f32[256,256]{1,0:T(8,128)S(1)}) custom-call(f32[264,256]{1,0:T(8,128)S(1)} %collective-permute-done.4.one, f32[264,256]{1,0:T(8,128)S(1)} %collective-permute-done.5.two, bf16[8,1536,256]{2,1,0:T(8,128)(2,1)S(1)} %get-tuple-element.59.weights, f32[256,256]{1,0:T(8,128)S(1)} %get-tuple-element.62.near, ...), custom_call_target="tpu_custom_call" | custom-call | flops 905969664 | bytes 7880704 | tf_op jit(solution)/shard_map/pallas_call | solution.py:354
  33.5 1.0 %shard_map.98 = (f32[256,256]{1,0:T(8,128)S(1)}, f32[256,256]{1,0:T(8,128)S(1)}) custom-call(f32[264,256]{1,0:T(8,128)S(1)} %collective-permute-done.1.one, f32[264,256]{1,0:T(8,128)S(1)} %collective-permute-done.3.two, bf16[8,1536,256]{2,1,0:T(8,128)(2,1)S(1)} %get-tuple-element.59.weights, f32[256,256]{1,0:T(8,128)S(1)} %get-tuple-element.66.early, ...), custom_call_target="tpu_custom_call" | custom-call | flops 603979776 | bytes 8142848 | tf_op jit(solution)/shard_map/pallas_call | solution.py:354
  35.9 1.8 %collective-permute-start.7 = (f32[256,256]{1,0:T(8,128)S(1)}, f32[256,256]{1,0:T(8,128)S(1)}, u32[]{:S(2)}, u32[]{:S(2)}) collective-permute-start(f32[256,256]{1,0:T(8,128)S(1)} %get-tuple-element.67.near), channel_id=1, source_target_pairs={{0,4},{1,3},{2,10},{3,1},{4,0},{5,7},{6,14},{7,5},{8,16},{9,11},{1... | collective-permute-start | bytes 786440 | tf_op jit(solution)/shard_map/ppermute | solution.py:375
  37.9 1.7 %shard_map.99 = (f32[256,256]{1,0:T(8,128)S(1)}, f32[256,256]{1,0:T(8,128)S(1)}) custom-call(f32[256,256]{1,0:T(8,128)S(1)} %get-tuple-element.67.near, f32[256,256]{1,0:T(8,128)S(1)} %get-tuple-element.65.far, bf16[1,1536,256]{2,1,0:T(8,128)(2,1)S(1)} %get-tuple-element.68.h_ref, bf16[8,1536,256]{2,1,0:T(8,128)(2,1)S(1)} %get-tuple-element.59.weights, ...), custom_call_target="tpu_custom_call" | custom-call | flops 1107296256 | bytes 8134656 | tf_op jit(solution)/shard_map/pallas_call | solution.py:354
  39.6 0.9 %shard_map.100 = (f32[256,256]{1,0:T(8,128)S(1)}, f32[256,256]{1,0:T(8,128)S(1)}) custom-call(f32[256,256]{1,0:T(8,128)S(1)} %collective-permute-done.8.one, f32[256,256]{1,0:T(8,128)S(1)} %collective-permute-done.9.two, bf16[8,1536,256]{2,1,0:T(8,128)(2,1)S(1)} %get-tuple-element.59.weights, f32[256,256]{1,0:T(8,128)S(1)} %get-tuple-element.70.near, ...), custom_call_target="tpu_custom_call" | custom-call | flops 905969664 | bytes 7864320 | tf_op jit(solution)/shard_map/pallas_call | solution.py:354
  40.5 1.7 %collective-permute-done.7.source = f32[256,256]{1,0:T(8,128)S(1)} collective-permute-done((f32[256,256]{1,0:T(8,128)S(1)}, f32[256,256]{1,0:T(8,128)S(1)}, u32[]{:S(2)}, u32[]{:S(2)}) %collective-permute-start.7) | collective-permute-done | bytes 262176 | tf_op jit(solution)/shard_map/ppermute | solution.py:375
  43.5 1.5 %collective-permute-done.6.source = f32[256,256]{1,0:T(8,128)S(1)} collective-permute-done((f32[256,256]{1,0:T(8,128)S(1)}, f32[256,256]{1,0:T(8,128)S(1)}, u32[]{:S(2)}, u32[]{:S(2)}) %collective-permute-start.6) | collective-permute-done | bytes 262176 | tf_op jit(solution)/shard_map/ppermute | solution.py:375
  45.7 1.9 %collective-permute-start.14 = (f32[256,256]{1,0:T(8,128)S(1)}, f32[256,256]{1,0:T(8,128)S(1)}, u32[]{:S(2)}, u32[]{:S(2)}) collective-permute-start(f32[256,256]{1,0:T(8,128)S(1)} %get-tuple-element.77.far), channel_id=1, source_target_pairs={{0,4},{1,3},{2,10},{3,1},{4,0},{5,7},{6,14},{7,5},{8,16},{9,11},{1... | collective-permute-start | bytes 786440 | tf_op jit(solution)/shard_map/ppermute | solution.py:375
  47.8 1.7 %shard_map.104 = (f32[256,256]{1,0:T(8,128)S(1)}, f32[256,256]{1,0:T(8,128)S(1)}) custom-call(f32[256,256]{1,0:T(8,128)S(1)} %get-tuple-element.74.near, f32[256,256]{1,0:T(8,128)S(1)} %get-tuple-element.77.far, bf16[1,1536,256]{2,1,0:T(8,128)(2,1)S(1)} %get-tuple-element.68.h_ref, bf16[8,1536,256]{2,1,0:T(8,128)(2,1)S(1)} %get-tuple-element.59.weights, ...), custom_call_target="tpu_custom_call" | custom-call | flops 1107296256 | bytes 8134656 | tf_op jit(solution)/shard_map/pallas_call | solution.py:354
  49.5 0.9 %shard_map.105 = (f32[256,256]{1,0:T(8,128)S(1)}, f32[256,256]{1,0:T(8,128)S(1)}) custom-call(f32[256,256]{1,0:T(8,128)S(1)} %collective-permute-done.11.one, f32[256,256]{1,0:T(8,128)S(1)} %collective-permute-done.12.two, bf16[8,1536,256]{2,1,0:T(8,128)(2,1)S(1)} %get-tuple-element.59.weights, f32[256,256]{1,0:T(8,128)S(1)} %get-tuple-element.78.near, ...), custom_call_target="tpu_custom_call" | custom-call | flops 905969664 | bytes 7864320 | tf_op jit(solution)/shard_map/pallas_call | solution.py:354
  50.4 1.7 %collective-permute-done.14.source = f32[256,256]{1,0:T(8,128)S(1)} collective-permute-done((f32[256,256]{1,0:T(8,128)S(1)}, f32[256,256]{1,0:T(8,128)S(1)}, u32[]{:S(2)}, u32[]{:S(2)}) %collective-permute-start.14) | collective-permute-done | bytes 262176 | tf_op jit(solution)/shard_map/ppermute | solution.py:375
  52.7 2.2 %collective-permute-done.10.source = f32[256,256]{1,0:T(8,128)S(1)} collective-permute-done((f32[256,256]{1,0:T(8,128)S(1)}, f32[256,256]{1,0:T(8,128)S(1)}, u32[]{:S(2)}, u32[]{:S(2)}) %collective-permute-start.10) | collective-permute-done | bytes 262176 | tf_op jit(solution)/shard_map/ppermute | solution.py:375
  56.6 1.8 %collective-permute-start.15 = (f32[256,256]{1,0:T(8,128)S(1)}, f32[256,256]{1,0:T(8,128)S(1)}, u32[]{:S(2)}, u32[]{:S(2)}) collective-permute-start(f32[256,256]{1,0:T(8,128)S(1)} %get-tuple-element.85.near), channel_id=1, source_target_pairs={{0,4},{1,3},{2,10},{3,1},{4,0},{5,7},{6,14},{7,5},{8,16},{9,11},{1... | collective-permute-start | bytes 786440 | tf_op jit(solution)/shard_map/ppermute | solution.py:375
  58.7 1.7 %shard_map.109 = (f32[256,256]{1,0:T(8,128)S(1)}, f32[256,256]{1,0:T(8,128)S(1)}) custom-call(f32[256,256]{1,0:T(8,128)S(1)} %get-tuple-element.85.near, f32[256,256]{1,0:T(8,128)S(1)} %get-tuple-element.82.far, bf16[1,1536,256]{2,1,0:T(8,128)(2,1)S(1)} %get-tuple-element.86.h_ref, bf16[8,1536,256]{2,1,0:T(8,128)(2,1)S(1)} %get-tuple-element.59.weights, ...), custom_call_target="tpu_custom_call" | custom-call | flops 1107296256 | bytes 8134656 | tf_op jit(solution)/shard_map/pallas_call | solution.py:354
  60.4 0.9 %shard_map.110 = (f32[256,256]{1,0:T(8,128)S(1)}, f32[256,256]{1,0:T(8,128)S(1)}) custom-call(f32[256,256]{1,0:T(8,128)S(1)} %collective-permute-done.16.one, f32[256,256]{1,0:T(8,128)S(1)} %collective-permute-done.17.two, bf16[8,1536,256]{2,1,0:T(8,128)(2,1)S(1)} %get-tuple-element.59.weights, f32[256,256]{1,0:T(8,128)S(1)} %get-tuple-element.87.near, ...), custom_call_target="tpu_custom_call" | custom-call | flops 905969664 | bytes 7864320 | tf_op jit(solution)/shard_map/pallas_call | solution.py:354
  61.3 1.7 %collective-permute-done.15.source = f32[256,256]{1,0:T(8,128)S(1)} collective-permute-done((f32[256,256]{1,0:T(8,128)S(1)}, f32[256,256]{1,0:T(8,128)S(1)}, u32[]{:S(2)}, u32[]{:S(2)}) %collective-permute-start.15) | collective-permute-done | bytes 262176 | tf_op jit(solution)/shard_map/ppermute | solution.py:375
  64.2 1.6 %collective-permute-done.13.source = f32[256,256]{1,0:T(8,128)S(1)} collective-permute-done((f32[256,256]{1,0:T(8,128)S(1)}, f32[256,256]{1,0:T(8,128)S(1)}, u32[]{:S(2)}, u32[]{:S(2)}) %collective-permute-start.13) | collective-permute-done | bytes 262176 | tf_op jit(solution)/shard_map/ppermute | solution.py:375
  66.4 1.6 %collective-permute-start.18 = (f32[256,256]{1,0:T(8,128)S(1)}, f32[256,256]{1,0:T(8,128)S(1)}, u32[]{:S(2)}, u32[]{:S(2)}) collective-permute-start(f32[256,256]{1,0:T(8,128)S(1)} %get-tuple-element.93.first_sent), channel_id=1, source_target_pairs={{0,13},{1,2},{2,6},{3,4},{4,1},{5,3},{6,7},{7,5},{8,14},{9,12},{10... | collective-permute-start | bytes 786440 | tf_op jit(solution)/shard_map/ppermute | solution.py:375
  68.0 5.3 %collective-permute-done.18.first = f32[256,256]{1,0:T(8,128)S(1)} collective-permute-done((f32[256,256]{1,0:T(8,128)S(1)}, f32[256,256]{1,0:T(8,128)S(1)}, u32[]{:S(2)}, u32[]{:S(2)}) %collective-permute-start.18) | collective-permute-done | bytes 262176 | tf_op jit(solution)/shard_map/ppermute | solution.py:375
  73.3 5.0 %collective-permute-done.19.second = f32[256,256]{1,0:T(8,128)S(1)} collective-permute-done((f32[256,256]{1,0:T(8,128)S(1)}, f32[256,256]{1,0:T(8,128)S(1)}, u32[]{:S(2)}, u32[]{:S(2)}) %collective-permute-start.19) | collective-permute-done | bytes 262176 | tf_op jit(solution)/shard_map/ppermute | solution.py:375
  78.3 1.0 %shard_map.114 = f32[1,2,256,256]{3,2,1,0:T(8,128)} custom-call(f32[256,256]{1,0:T(8,128)S(1)} %collective-permute-done.18.first, f32[256,256]{1,0:T(8,128)S(1)} %collective-permute-done.19.second, f32[256,256]{1,0:T(8,128)S(1)} %get-tuple-element.93.first_sent, f32[256,256]{1,0:T(8,128)S(1)} %get-tuple-element.94.second_sent), custom_call_target="tpu_custom_call" | custom-call | bytes 1572864 | tf_op jit(solution)/shard_map/pallas_call | solution.py:354
  (44 shorter events, 10.9 us)
Async XLA Ops:
  2.1 15.7 %collective-permute-start.2 = (f32[264,256]{1,0:T(8,128)}, f32[264,256]{1,0:T(8,128)S(1)}, u32[]{:S(2)}, u32[]{:S(2)}) collective-permute-start(f32[264,256]{1,0:T(8,128)} %get-tuple-element.51), channel_id=1, source_target_pairs={{0,4},{1,0},{2,5},{3,1},{4,7},{5,3},{6,11},{7,2},{8,14},{9,10},{10... | collective-permute-start | bytes 811016 | tf_op jit(solution)/shard_map/ppermute | solution.py:375
  5.2 12.8 %collective-permute-start = (f32[264,256]{1,0:T(8,128)}, f32[264,256]{1,0:T(8,128)S(1)}, u32[]{:S(2)}, u32[]{:S(2)}) collective-permute-start(f32[264,256]{1,0:T(8,128)} %get-tuple-element.50), channel_id=1, source_target_pairs={{0,13},{1,4},{2,1},{3,5},{4,3},{5,7},{6,2},{7,6},{8,10},{9,14},{10... | collective-permute-start | bytes 811016 | tf_op jit(solution)/shard_map/ppermute | solution.py:375
  17.8 14.7 %collective-permute-start.5 = (f32[264,256]{1,0:T(8,128)S(1)}, f32[264,256]{1,0:T(8,128)S(1)}, u32[]{:S(2)}, u32[]{:S(2)}) collective-permute-start(f32[264,256]{1,0:T(8,128)S(1)} %broadcast_select_fusion.array), channel_id=1, source_target_pairs={{0,1},{1,0},{2,3},{3,2},{4,5},{5,4},{6,7},{7,6},{8,9},{9,8},{10,11... | collective-permute-start | bytes 811016 | tf_op jit(solution)/shard_map/ppermute | solution.py:375
  18.9 13.7 %collective-permute-start.4 = (f32[264,256]{1,0:T(8,128)S(1)}, f32[264,256]{1,0:T(8,128)S(1)}, u32[]{:S(2)}, u32[]{:S(2)}) collective-permute-start(f32[264,256]{1,0:T(8,128)S(1)} %broadcast_select_fusion.1.array), channel_id=1, source_target_pairs={{0,1},{1,0},{2,3},{3,2},{4,5},{5,4},{6,7},{7,6},{8,9},{9,8},{10,11... | collective-permute-start | bytes 811016 | tf_op jit(solution)/shard_map/ppermute | solution.py:375
  19.0 14.5 %collective-permute-start.3 = (f32[264,256]{1,0:T(8,128)S(1)}, f32[264,256]{1,0:T(8,128)S(1)}, u32[]{:S(2)}, u32[]{:S(2)}) collective-permute-start(f32[264,256]{1,0:T(8,128)S(1)} %broadcast_select_fusion.array), channel_id=1, source_target_pairs={{0,4},{1,3},{2,10},{3,1},{4,0},{5,7},{6,14},{7,5},{8,16},{9,11},{1... | collective-permute-start | bytes 811016 | tf_op jit(solution)/shard_map/ppermute | solution.py:375
  20.9 12.6 %collective-permute-start.1 = (f32[264,256]{1,0:T(8,128)S(1)}, f32[264,256]{1,0:T(8,128)S(1)}, u32[]{:S(2)}, u32[]{:S(2)}) collective-permute-start(f32[264,256]{1,0:T(8,128)S(1)} %broadcast_select_fusion.1.array), channel_id=1, source_target_pairs={{0,4},{1,3},{2,10},{3,1},{4,0},{5,7},{6,14},{7,5},{8,16},{9,11},{1... | collective-permute-start | bytes 811016 | tf_op jit(solution)/shard_map/ppermute | solution.py:375
  21.1 1.1 %copy-start = (f32[3,256,256]{2,1,0:T(8,128)S(1)}, f32[3,256,256]{2,1,0:T(8,128)}, u32[]{:S(2)}) copy-start(f32[3,256,256]{2,1,0:T(8,128)} %couple.1) | copy-start | bytes 2359300
  22.2 1.0 %copy-start.1 = (f32[2,256,256]{2,1,0:T(8,128)S(1)}, f32[2,256,256]{2,1,0:T(8,128)}, u32[]{:S(2)}) copy-start(f32[2,256,256]{2,1,0:T(8,128)} %h_static.1) | copy-start | bytes 1572868
  23.3 1.0 %copy-start.2 = (f32[2,256,256]{2,1,0:T(8,128)S(1)}, f32[2,256,256]{2,1,0:T(8,128)}, u32[]{:S(2)}) copy-start(f32[2,256,256]{2,1,0:T(8,128)} %drive_op.1) | copy-start | bytes 1572868
  24.3 0.7 copy-start.3
  25.0 0.7 copy-start.4
  34.6 5.0 %collective-permute-start.8 = (f32[256,256]{1,0:T(8,128)S(1)}, f32[256,256]{1,0:T(8,128)S(1)}, u32[]{:S(2)}, u32[]{:S(2)}) collective-permute-start(f32[256,256]{1,0:T(8,128)S(1)} %get-tuple-element.67.near), channel_id=1, source_target_pairs={{0,1},{1,0},{2,3},{3,2},{4,5},{5,4},{6,7},{7,6},{8,9},{9,8},{10,11... | collective-permute-start | bytes 786440 | tf_op jit(solution)/shard_map/ppermute | solution.py:375
  35.4 4.1 %collective-permute-start.9 = (f32[256,256]{1,0:T(8,128)S(1)}, f32[256,256]{1,0:T(8,128)S(1)}, u32[]{:S(2)}, u32[]{:S(2)}) collective-permute-start(f32[256,256]{1,0:T(8,128)S(1)} %get-tuple-element.65.far), channel_id=1, source_target_pairs={{0,1},{1,0},{2,3},{3,2},{4,5},{5,4},{6,7},{7,6},{8,9},{9,8},{10,11... | collective-permute-start | bytes 786440 | tf_op jit(solution)/shard_map/ppermute | solution.py:375
  35.9 6.4 %collective-permute-start.7 = (f32[256,256]{1,0:T(8,128)S(1)}, f32[256,256]{1,0:T(8,128)S(1)}, u32[]{:S(2)}, u32[]{:S(2)}) collective-permute-start(f32[256,256]{1,0:T(8,128)S(1)} %get-tuple-element.67.near), channel_id=1, source_target_pairs={{0,4},{1,3},{2,10},{3,1},{4,0},{5,7},{6,14},{7,5},{8,16},{9,11},{1... | collective-permute-start | bytes 786440 | tf_op jit(solution)/shard_map/ppermute | solution.py:375
  37.7 7.4 %collective-permute-start.6 = (f32[256,256]{1,0:T(8,128)S(1)}, f32[256,256]{1,0:T(8,128)S(1)}, u32[]{:S(2)}, u32[]{:S(2)}) collective-permute-start(f32[256,256]{1,0:T(8,128)S(1)} %get-tuple-element.65.far), channel_id=1, source_target_pairs={{0,4},{1,3},{2,10},{3,1},{4,0},{5,7},{6,14},{7,5},{8,16},{9,11},{1... | collective-permute-start | bytes 786440 | tf_op jit(solution)/shard_map/ppermute | solution.py:375
  42.8 6.6 %collective-permute-start.12 = (f32[256,256]{1,0:T(8,128)S(1)}, f32[256,256]{1,0:T(8,128)S(1)}, u32[]{:S(2)}, u32[]{:S(2)}) collective-permute-start(f32[256,256]{1,0:T(8,128)S(1)} %get-tuple-element.77.far), channel_id=1, source_target_pairs={{0,1},{1,0},{2,3},{3,2},{4,5},{5,4},{6,7},{7,6},{8,9},{9,8},{10,11... | collective-permute-start | bytes 786440 | tf_op jit(solution)/shard_map/ppermute | solution.py:375
  45.6 3.9 %collective-permute-start.11 = (f32[256,256]{1,0:T(8,128)S(1)}, f32[256,256]{1,0:T(8,128)S(1)}, u32[]{:S(2)}, u32[]{:S(2)}) collective-permute-start(f32[256,256]{1,0:T(8,128)S(1)} %get-tuple-element.74.near), channel_id=1, source_target_pairs={{0,1},{1,0},{2,3},{3,2},{4,5},{5,4},{6,7},{7,6},{8,9},{9,8},{10,11... | collective-permute-start | bytes 786440 | tf_op jit(solution)/shard_map/ppermute | solution.py:375
  45.7 6.4 %collective-permute-start.14 = (f32[256,256]{1,0:T(8,128)S(1)}, f32[256,256]{1,0:T(8,128)S(1)}, u32[]{:S(2)}, u32[]{:S(2)}) collective-permute-start(f32[256,256]{1,0:T(8,128)S(1)} %get-tuple-element.77.far), channel_id=1, source_target_pairs={{0,4},{1,3},{2,10},{3,1},{4,0},{5,7},{6,14},{7,5},{8,16},{9,11},{1... | collective-permute-start | bytes 786440 | tf_op jit(solution)/shard_map/ppermute | solution.py:375
  47.6 7.4 %collective-permute-start.10 = (f32[256,256]{1,0:T(8,128)S(1)}, f32[256,256]{1,0:T(8,128)S(1)}, u32[]{:S(2)}, u32[]{:S(2)}) collective-permute-start(f32[256,256]{1,0:T(8,128)S(1)} %get-tuple-element.74.near), channel_id=1, source_target_pairs={{0,4},{1,3},{2,10},{3,1},{4,0},{5,7},{6,14},{7,5},{8,16},{9,11},{1... | collective-permute-start | bytes 786440 | tf_op jit(solution)/shard_map/ppermute | solution.py:375
  55.6 4.8 %collective-permute-start.16 = (f32[256,256]{1,0:T(8,128)S(1)}, f32[256,256]{1,0:T(8,128)S(1)}, u32[]{:S(2)}, u32[]{:S(2)}) collective-permute-start(f32[256,256]{1,0:T(8,128)S(1)} %get-tuple-element.85.near), channel_id=1, source_target_pairs={{0,1},{1,0},{2,3},{3,2},{4,5},{5,4},{6,7},{7,6},{8,9},{9,8},{10,11... | collective-permute-start | bytes 786440 | tf_op jit(solution)/shard_map/ppermute | solution.py:375
  56.5 3.9 %collective-permute-start.17 = (f32[256,256]{1,0:T(8,128)S(1)}, f32[256,256]{1,0:T(8,128)S(1)}, u32[]{:S(2)}, u32[]{:S(2)}) collective-permute-start(f32[256,256]{1,0:T(8,128)S(1)} %get-tuple-element.82.far), channel_id=1, source_target_pairs={{0,1},{1,0},{2,3},{3,2},{4,5},{5,4},{6,7},{7,6},{8,9},{9,8},{10,11... | collective-permute-start | bytes 786440 | tf_op jit(solution)/shard_map/ppermute | solution.py:375
  56.6 6.4 %collective-permute-start.15 = (f32[256,256]{1,0:T(8,128)S(1)}, f32[256,256]{1,0:T(8,128)S(1)}, u32[]{:S(2)}, u32[]{:S(2)}) collective-permute-start(f32[256,256]{1,0:T(8,128)S(1)} %get-tuple-element.85.near), channel_id=1, source_target_pairs={{0,4},{1,3},{2,10},{3,1},{4,0},{5,7},{6,14},{7,5},{8,16},{9,11},{1... | collective-permute-start | bytes 786440 | tf_op jit(solution)/shard_map/ppermute | solution.py:375
  58.5 7.4 %collective-permute-start.13 = (f32[256,256]{1,0:T(8,128)S(1)}, f32[256,256]{1,0:T(8,128)S(1)}, u32[]{:S(2)}, u32[]{:S(2)}) collective-permute-start(f32[256,256]{1,0:T(8,128)S(1)} %get-tuple-element.82.far), channel_id=1, source_target_pairs={{0,4},{1,3},{2,10},{3,1},{4,0},{5,7},{6,14},{7,5},{8,16},{9,11},{1... | collective-permute-start | bytes 786440 | tf_op jit(solution)/shard_map/ppermute | solution.py:375
  66.4 6.9 %collective-permute-start.18 = (f32[256,256]{1,0:T(8,128)S(1)}, f32[256,256]{1,0:T(8,128)S(1)}, u32[]{:S(2)}, u32[]{:S(2)}) collective-permute-start(f32[256,256]{1,0:T(8,128)S(1)} %get-tuple-element.93.first_sent), channel_id=1, source_target_pairs={{0,13},{1,2},{2,6},{3,4},{4,1},{5,3},{6,7},{7,5},{8,14},{9,12},{10... | collective-permute-start | bytes 786440 | tf_op jit(solution)/shard_map/ppermute | solution.py:375
  68.0 10.3 %collective-permute-start.19 = (f32[256,256]{1,0:T(8,128)S(1)}, f32[256,256]{1,0:T(8,128)S(1)}, u32[]{:S(2)}, u32[]{:S(2)}) collective-permute-start(f32[256,256]{1,0:T(8,128)S(1)} %get-tuple-element.94.second_sent), channel_id=1, source_target_pairs={{0,1},{1,3},{2,7},{3,5},{4,0},{5,2},{6,11},{7,4},{8,15},{9,13},{10... | collective-permute-start | bytes 786440 | tf_op jit(solution)/shard_map/ppermute | solution.py:375
where the time goes:
time: 79.6 us; the launch traced here: 79.3 us
  waiting for transfers between devices  32.9 us (41%)
  Pallas kernels  25.9 us (33%)
  starting transfers between devices  14.5 us (18%)
  local copies, waits for them, and re-layouts  4.55 us (6%)
  other arithmetic  1.04 us (1%)
    ppermute x20, waiting for transfers between devices, send(): return lax.ppermute(value, 'aux', pairs)  32.9 us
    pallas_call x24, Pallas kernels, call(): pl.pallas_call(kernel, out_shape=shapes[0] if single else shapes, in_spec...  25.9 us
    ppermute x20, starting transfers between devices, send(): return lax.ppermute(value, 'aux', pairs)  14.5 us
    unnamed x10, local copies, waits for them, and re-layouts  4.55 us
  transfers between devices with their start and end apart: 20, of which 9 were waited for; matrix products, arithmetic and copies ran while one was open for 1% of the time, Pallas kernels for 26%

commit v1 on v0

--- a/solution.py
+++ b/solution.py
@@ -13,6 +13,7 @@
 drive_amp = 2.0
 drive_freq = 20.0
 META = 8
+CHUNK = 32
 F32 = jnp.float32
 BF16 = jnp.bfloat16
 VMEM = pl.BlockSpec(memory_space=pltpu.VMEM)
@@ -79,6 +80,14 @@
         high, low = split(value)
         ref[index, 2 * place * size : (2 * place + 1) * size] = high
         ref[index, (2 * place + 1) * size : (2 * place + 2) * size] = low
+
+
+def store_rows(ref, index, row, size, values):
+    for place, value in enumerate(values):
+        high, low = split(value)
+        start = 2 * place * size + row
+        ref[index, start : start + value.shape[0]] = high
+        ref[index, start + size : start + size + value.shape[0]] = low
 
 
 def dot_nn(a, b):
@@ -161,11 +170,9 @@
         drive = drive_amp * math.cos(drive_freq * moment)
         store_stack(h_out, 0, h_re + drive * v_re, h_im + drive * v_im)
     for mode in range(couple.shape[0]):
-        q = (couple[mode] + couple[mode].T) * 0.5
-        q_out[3 * mode] = q
-        q_out[3 * mode + 1] = bath_coef[0, mode] * q
-        q_out[3 * mode + 2] = bath_coef[1, mode] * q
-        damp_out[mode] = jnp.full(damp_out.shape[1:], damping[mode], F32)
+        q_out[mode] = (couple[mode] + couple[mode].T) * 0.5
+        for place, value in enumerate((damping[mode], bath_coef[0, mode], bath_coef[1, mode])):
+            damp_out[3 * mode + place] = jnp.full(damp_out.shape[1:], value, F32)
 
 
 def arrive_kernel(which, array, q_ref, damp, h_ref, *refs):
@@ -173,16 +180,19 @@
     problem, block, pair = role("aux")
     part = pair ^ problem ^ which
     size = q_ref.shape[1]
-    modes = damp.shape[0]
+    modes = q_ref.shape[0]
     meta = array[size : size + 1]
 
     def entry(place, mode):
         column = place * modes + mode
         return meta[:, column : column + 1]
 
+    def constant(place, mode):
+        return damp[3 * mode + place][0:1, 0:1]
+
     total = jnp.zeros((1, 1), F32)
     for mode in range(modes):
-        total = total + entry(0, mode) * damp[mode][0:1, 0:1]
+        total = total + entry(0, mode) * constant(0, mode)
     rate[part] = jnp.broadcast_to(total, rate.shape[1:])
     value = array[0:size]
     base[part] = value
@@ -191,19 +201,39 @@
 
     near = 4 * block + 3 * pair
     inward = 1 - 2 * pair
-    twin = near + (1 - part) * inward
-    last = jnp.where(part == 0, near + 2 * inward, near + 3 * inward)
-    third = jnp.where(part == 0, near - 2 * inward, near + 2 * inward)
-    for kind, source in enumerate((twin, near - inward, third, last)):
-        source = jnp.where(source < 0, -9, source).astype(F32)
-        w_re = jnp.zeros((size, size), F32)
-        w_im = jnp.zeros((size, size), F32)
+    from_below = pair == 0
+    sources = (
+        jnp.where(part == 0, near + inward, near),
+        near - inward,
+        jnp.where(part == 0, near - 2 * inward, near + 2 * inward),
+        jnp.where(part == 0, near + 2 * inward, near + 3 * inward),
+    )
+    link_kinds = (1 - part, 2 - part)
+    partner_kinds = (2 * part, 3)
+    link_sources = (jnp.where(part == 0, sources[1], sources[0]), jnp.where(part == 0, sources[2], sources[1]))
+    partner_sources = (jnp.where(part == 0, sources[0], sources[2]), sources[3])
+
+    def marked(place, source, mode):
+        return entry(place, mode) == jnp.where(source < 0, -9, source).astype(F32)
+
+    for index in range(2):
+        kind = jnp.where(from_below, link_kinds[index], partner_kinds[index])
+        source = jnp.where(from_below, link_sources[index], partner_sources[index])
+        factors = []
         for mode in range(modes):
-            up = jnp.where(entry(1, mode) == source, 1.0, 0.0)
-            down = jnp.where(entry(2, mode) == source, entry(0, mode), 0.0)
-            w_re = w_re + (up * q_ref[3 * mode] + down * q_ref[3 * mode + 1])
-            w_im = w_im + down * q_ref[3 * mode + 2]
-        store_stack(weights, 4 * part + kind, w_re, w_im)
+            down = jnp.where(marked(2, source, mode), entry(0, mode), 0.0)
+            factors.append((down * constant(1, mode), down * constant(2, mode)))
+        for row in range(0, size, CHUNK):
+            w_re = sum(factors[mode][0] * q_ref[mode, row : row + CHUNK] for mode in range(modes))
+            w_im = sum(factors[mode][1] * q_ref[mode, row : row + CHUNK] for mode in range(modes))
+            store_rows(weights, 4 * part + kind, row, size, (w_re, w_im, w_re + w_im))
+    for index in range(2):
+        kind = jnp.where(from_below, partner_kinds[index], link_kinds[index])
+        source = jnp.where(from_below, partner_sources[index], link_sources[index])
+        factors = [jnp.where(marked(1, source, mode), 1.0, 0.0) for mode in range(modes)]
+        for row in range(0, size, CHUNK):
+            w_re = sum(factors[mode] * q_ref[mode, row : row + CHUNK] for mode in range(modes))
+            store_rows(weights, 4 * part + kind, row, size, (w_re,))
 
 
 N_OWN, N_LINK_N, N_LINK_F, N_PARTNER_F, F_OWN, F_LINK_N, F_PARTNER_F, F_PARTNER_N = range(8)
@@ -391,7 +421,7 @@
     second = jnp.where(keep_second, second, send(second, second_to))
     *h_now, q_all, damp = call(
         prepare_kernel,
-        [((1, 6 * size, size), BF16)] * 3 + [((3 * modes, size, size), F32), ((modes, 8, 128), F32)],
+        [((1, 6 * size, size), BF16)] * 3 + [((modes, size, size), F32), ((3 * modes, 8, 128), F32)],
         [h_static, drive_op, couple, bath_coef, damping],
         smem=(3, 4),
     )

time: 79.6 us -> 77.2 us (0.970)
  Pallas kernels: 25.9 us -> 23.8 us
    pallas_call x24, Pallas kernels: 25.9 us -> 23.8 us  [call(): pl.pallas_call(kernel, out_shape=shapes[0] if single else shapes, in_spec...]
  transfers between devices with their start and end apart: 20 -> 20, of which waited for: 9 -> 9; matrix products, arithmetic and copies ran while one was open for 1% -> 1% of each run, Pallas kernels for 26% -> 24%
where the time goes in v1:
time: 77.2 us; the launch traced here: 76.9 us
  waiting for transfers between devices  32.6 us (42%)
  Pallas kernels  23.8 us (31%)
  starting transfers between devices  14.6 us (19%)
  local copies, waits for them, and re-layouts  4.55 us (6%)
  other arithmetic  1.04 us (1%)
    ppermute x20, waiting for transfers between devices, send(): return lax.ppermute(value, 'aux', pairs)  32.6 us
    pallas_call x24, Pallas kernels, call(): pl.pallas_call(kernel, out_shape=shapes[0] if single else shapes, in_spec...  23.8 us
    ppermute x20, starting transfers between devices, send(): return lax.ppermute(value, 'aux', pairs)  14.6 us
    unnamed x10, local copies, waits for them, and re-layouts  4.55 us
  transfers between devices with their start and end apart: 20, of which 9 were waited for; matrix products, arithmetic and copies ran while one was open for 1% of the time, Pallas kernels for 24%

profile of v1, /device:TPU:0, one launch (start us, length us, event | category | flops | bytes accessed | tf_op | source)
XLA Modules:
  0.0 76.9 jit_solution(8799073047861096708)
XLA Ops:
  0.0 2.1 %shard_map.91 = (f32[264,256]{1,0:T(8,128)}, f32[264,256]{1,0:T(8,128)}) custom-call(f32[1,2,256,256]{3,2,1,0:T(8,128)} %state_hbm.1, s32[1,3]{1,0:T(1,128)} %occ_hbm.1, s32[1,3]{1,0:T(1,128)} %up_hbm.1, s32[1,3]{1,0:T(1,128)} %low_hbm.1), custom_call_target="tpu_custom_call" | custom-call | bytes 1064996 | tf_op jit(solution)/shard_map/pallas_call | solution.py:384
  2.1 3.1 %collective-permute-start.2 = (f32[264,256]{1,0:T(8,128)}, f32[264,256]{1,0:T(8,128)S(1)}, u32[]{:S(2)}, u32[]{:S(2)}) collective-permute-start(f32[264,256]{1,0:T(8,128)} %get-tuple-element.51), channel_id=1, source_target_pairs={{0,4},{1,0},{2,5},{3,1},{4,7},{5,3},{6,11},{7,2},{8,14},{9,10},{10... | collective-permute-start | bytes 811016 | tf_op jit(solution)/shard_map/ppermute | solution.py:405
  5.8 12.0 %collective-permute-done.2 = f32[264,256]{1,0:T(8,128)S(1)} collective-permute-done((f32[264,256]{1,0:T(8,128)}, f32[264,256]{1,0:T(8,128)S(1)}, u32[]{:S(2)}, u32[]{:S(2)}) %collective-permute-start.2) | collective-permute-done | bytes 270368 | tf_op jit(solution)/shard_map/ppermute | solution.py:405
  17.9 1.0 %broadcast_select_fusion.1.array = f32[264,256]{1,0:T(8,128)S(1)} fusion(f32[264,256]{1,0:T(8,128)} %get-tuple-element.50, f32[264,256]{1,0:T(8,128)S(1)} %collective-permute-done, pred[]{:T(512)S(6)} %eq.6), kind=kLoop, calls=%fused_computation.1 | loop fusion | flops 67584 | bytes 811009 | tf_op jit(solution)/shard_map/jit(_where)/select_n | solution.py:420
  19.0 1.9 %collective-permute-start.3 = (f32[264,256]{1,0:T(8,128)S(1)}, f32[264,256]{1,0:T(8,128)S(1)}, u32[]{:S(2)}, u32[]{:S(2)}) collective-permute-start(f32[264,256]{1,0:T(8,128)S(1)} %broadcast_select_fusion.array), channel_id=1, source_target_pairs={{0,4},{1,3},{2,10},{3,1},{4,0},{5,7},{6,14},{7,5},{8,16},{9,11},{1... | collective-permute-start | bytes 811016 | tf_op jit(solution)/shard_map/ppermute | solution.py:405
  21.1 1.1 %copy-done = f32[3,256,256]{2,1,0:T(8,128)S(1)} copy-done((f32[3,256,256]{2,1,0:T(8,128)S(1)}, f32[3,256,256]{2,1,0:T(8,128)}, u32[]{:S(2)}) %copy-start) | copy-done | bytes 786456
  22.2 1.0 %copy-done.1 = f32[2,256,256]{2,1,0:T(8,128)S(1)} copy-done((f32[2,256,256]{2,1,0:T(8,128)S(1)}, f32[2,256,256]{2,1,0:T(8,128)}, u32[]{:S(2)}) %copy-start.1) | copy-done | bytes 524312
  23.3 1.0 %copy-done.2 = f32[2,256,256]{2,1,0:T(8,128)S(1)} copy-done((f32[2,256,256]{2,1,0:T(8,128)S(1)}, f32[2,256,256]{2,1,0:T(8,128)}, u32[]{:S(2)}) %copy-start.2) | copy-done | bytes 524312
  25.7 1.4 %shard_map.92 = (bf16[1,1536,256]{2,1,0:T(8,128)(2,1)S(1)}, bf16[1,1536,256]{2,1,0:T(8,128)(2,1)S(1)}, bf16[1,1536,256]{2,1,0:T(8,128)(2,1)S(1)}, f32[3,256,256]{2,1,0:T(8,128)S(1)}, f32[9,8,128]{2,1,0:T(8,128)S(1)}) custom-call(f32[2,256,256]{2,1,0:T(8,128)S(1)} %copy-done.1, f32[2,256,256]{2,1,0:T(8,128)S(1)} %copy-done.2, f32[3,256,256]{2,1,0:T(8,128)S(1)} %copy-done, ...), custom_call_target="tpu_custom_call" | custom-call | bytes 5017636 | tf_op jit(solution)/shard_map/pallas_call | solution.py:384
  27.1 1.2 %shard_map.93 = (bf16[8,1536,256]{2,1,0:T(8,128)(2,1)S(1)}, f32[2,256,256]{2,1,0:T(8,128)S(1)}, f32[2,8,128]{2,1,0:T(8,128)S(1)}, f32[2,256,256]{2,1,0:T(8,128)S(1)}) custom-call(f32[264,256]{1,0:T(8,128)S(1)} %broadcast_select_fusion.1.array, f32[3,256,256]{2,1,0:T(8,128)S(1)} %get-tuple-element.52.q_ref, f32[9,8,128]{2,1,0:T(8,128)S(1)} %get-tuple-element.53.damp, ...), custom_call_target="tpu_custom_call" | custom-call | flops 301989888 | bytes 9228288 | tf_op jit(solution)/shard_map/pallas_call | solution.py:384
  28.3 1.2 %shard_map.94 = (bf16[8,1536,256]{2,1,0:T(8,128)(2,1)S(1)}, f32[2,256,256]{2,1,0:T(8,128)S(1)}, f32[2,8,128]{2,1,0:T(8,128)S(1)}, f32[2,256,256]{2,1,0:T(8,128)S(1)}) custom-call(f32[264,256]{1,0:T(8,128)S(1)} %broadcast_select_fusion.array, ...), custom_call_target="tpu_custom_call", output_to_operand_aliasing={{0}: (4, {}), {1}: (5, {}), {2}: (6, {}), {3}: (7, {})} | custom-call | flops 301989888 | bytes 16576512 | tf_op jit(solution)/shard_map/pallas_call | solution.py:384
  30.3 0.9 %shard_map.96 = (f32[256,256]{1,0:T(8,128)S(1)}, f32[256,256]{1,0:T(8,128)S(1)}) custom-call(f32[264,256]{1,0:T(8,128)S(1)} %collective-permute-done.4.one, f32[264,256]{1,0:T(8,128)S(1)} %collective-permute-done.5.two, bf16[8,1536,256]{2,1,0:T(8,128)(2,1)S(1)} %get-tuple-element.59.weights, f32[256,256]{1,0:T(8,128)S(1)} %get-tuple-element.62.near, ...), custom_call_target="tpu_custom_call" | custom-call | flops 905969664 | bytes 7880704 | tf_op jit(solution)/shard_map/pallas_call | solution.py:384
  31.3 1.0 %shard_map.98 = (f32[256,256]{1,0:T(8,128)S(1)}, f32[256,256]{1,0:T(8,128)S(1)}) custom-call(f32[264,256]{1,0:T(8,128)S(1)} %collective-permute-done.1.one, f32[264,256]{1,0:T(8,128)S(1)} %collective-permute-done.3.two, bf16[8,1536,256]{2,1,0:T(8,128)(2,1)S(1)} %get-tuple-element.59.weights, f32[256,256]{1,0:T(8,128)S(1)} %get-tuple-element.66.early, ...), custom_call_target="tpu_custom_call" | custom-call | flops 603979776 | bytes 8142848 | tf_op jit(solution)/shard_map/pallas_call | solution.py:384
  33.4 1.8 %collective-permute-start.7 = (f32[256,256]{1,0:T(8,128)S(1)}, f32[256,256]{1,0:T(8,128)S(1)}, u32[]{:S(2)}, u32[]{:S(2)}) collective-permute-start(f32[256,256]{1,0:T(8,128)S(1)} %get-tuple-element.67.near), channel_id=1, source_target_pairs={{0,4},{1,3},{2,10},{3,1},{4,0},{5,7},{6,14},{7,5},{8,16},{9,11},{1... | collective-permute-start | bytes 786440 | tf_op jit(solution)/shard_map/ppermute | solution.py:405
  35.4 1.7 %shard_map.99 = (f32[256,256]{1,0:T(8,128)S(1)}, f32[256,256]{1,0:T(8,128)S(1)}) custom-call(f32[256,256]{1,0:T(8,128)S(1)} %get-tuple-element.67.near, f32[256,256]{1,0:T(8,128)S(1)} %get-tuple-element.65.far, bf16[1,1536,256]{2,1,0:T(8,128)(2,1)S(1)} %get-tuple-element.68.h_ref, bf16[8,1536,256]{2,1,0:T(8,128)(2,1)S(1)} %get-tuple-element.59.weights, ...), custom_call_target="tpu_custom_call" | custom-call | flops 1107296256 | bytes 8134656 | tf_op jit(solution)/shard_map/pallas_call | solution.py:384
  37.2 1.1 %shard_map.100 = (f32[256,256]{1,0:T(8,128)S(1)}, f32[256,256]{1,0:T(8,128)S(1)}) custom-call(f32[256,256]{1,0:T(8,128)S(1)} %collective-permute-done.8.one, f32[256,256]{1,0:T(8,128)S(1)} %collective-permute-done.9.two, bf16[8,1536,256]{2,1,0:T(8,128)(2,1)S(1)} %get-tuple-element.59.weights, f32[256,256]{1,0:T(8,128)S(1)} %get-tuple-element.70.near, ...), custom_call_target="tpu_custom_call" | custom-call | flops 905969664 | bytes 7864320 | tf_op jit(solution)/shard_map/pallas_call | solution.py:384
  38.3 1.5 %collective-permute-done.7.source = f32[256,256]{1,0:T(8,128)S(1)} collective-permute-done((f32[256,256]{1,0:T(8,128)S(1)}, f32[256,256]{1,0:T(8,128)S(1)}, u32[]{:S(2)}, u32[]{:S(2)}) %collective-permute-start.7) | collective-permute-done | bytes 262176 | tf_op jit(solution)/shard_map/ppermute | solution.py:405
  41.1 1.5 %collective-permute-done.6.source = f32[256,256]{1,0:T(8,128)S(1)} collective-permute-done((f32[256,256]{1,0:T(8,128)S(1)}, f32[256,256]{1,0:T(8,128)S(1)}, u32[]{:S(2)}, u32[]{:S(2)}) %collective-permute-start.6) | collective-permute-done | bytes 262176 | tf_op jit(solution)/shard_map/ppermute | solution.py:405
  43.3 1.9 %collective-permute-start.14 = (f32[256,256]{1,0:T(8,128)S(1)}, f32[256,256]{1,0:T(8,128)S(1)}, u32[]{:S(2)}, u32[]{:S(2)}) collective-permute-start(f32[256,256]{1,0:T(8,128)S(1)} %get-tuple-element.77.far), channel_id=1, source_target_pairs={{0,4},{1,3},{2,10},{3,1},{4,0},{5,7},{6,14},{7,5},{8,16},{9,11},{1... | collective-permute-start | bytes 786440 | tf_op jit(solution)/shard_map/ppermute | solution.py:405
  45.4 1.7 %shard_map.104 = (f32[256,256]{1,0:T(8,128)S(1)}, f32[256,256]{1,0:T(8,128)S(1)}) custom-call(f32[256,256]{1,0:T(8,128)S(1)} %get-tuple-element.74.near, f32[256,256]{1,0:T(8,128)S(1)} %get-tuple-element.77.far, bf16[1,1536,256]{2,1,0:T(8,128)(2,1)S(1)} %get-tuple-element.68.h_ref, bf16[8,1536,256]{2,1,0:T(8,128)(2,1)S(1)} %get-tuple-element.59.weights, ...), custom_call_target="tpu_custom_call" | custom-call | flops 1107296256 | bytes 8134656 | tf_op jit(solution)/shard_map/pallas_call | solution.py:384
  47.1 0.9 %shard_map.105 = (f32[256,256]{1,0:T(8,128)S(1)}, f32[256,256]{1,0:T(8,128)S(1)}) custom-call(f32[256,256]{1,0:T(8,128)S(1)} %collective-permute-done.11.one, f32[256,256]{1,0:T(8,128)S(1)} %collective-permute-done.12.two, bf16[8,1536,256]{2,1,0:T(8,128)(2,1)S(1)} %get-tuple-element.59.weights, f32[256,256]{1,0:T(8,128)S(1)} %get-tuple-element.78.near, ...), custom_call_target="tpu_custom_call" | custom-call | flops 905969664 | bytes 7864320 | tf_op jit(solution)/shard_map/pallas_call | solution.py:384
  48.0 1.7 %collective-permute-done.14.source = f32[256,256]{1,0:T(8,128)S(1)} collective-permute-done((f32[256,256]{1,0:T(8,128)S(1)}, f32[256,256]{1,0:T(8,128)S(1)}, u32[]{:S(2)}, u32[]{:S(2)}) %collective-permute-start.14) | collective-permute-done | bytes 262176 | tf_op jit(solution)/shard_map/ppermute | solution.py:405
  50.3 2.2 %collective-permute-done.10.source = f32[256,256]{1,0:T(8,128)S(1)} collective-permute-done((f32[256,256]{1,0:T(8,128)S(1)}, f32[256,256]{1,0:T(8,128)S(1)}, u32[]{:S(2)}, u32[]{:S(2)}) %collective-permute-start.10) | collective-permute-done | bytes 262176 | tf_op jit(solution)/shard_map/ppermute | solution.py:405
  54.2 1.8 %collective-permute-start.15 = (f32[256,256]{1,0:T(8,128)S(1)}, f32[256,256]{1,0:T(8,128)S(1)}, u32[]{:S(2)}, u32[]{:S(2)}) collective-permute-start(f32[256,256]{1,0:T(8,128)S(1)} %get-tuple-element.85.near), channel_id=1, source_target_pairs={{0,4},{1,3},{2,10},{3,1},{4,0},{5,7},{6,14},{7,5},{8,16},{9,11},{1... | collective-permute-start | bytes 786440 | tf_op jit(solution)/shard_map/ppermute | solution.py:405
  56.2 1.9 %shard_map.109 = (f32[256,256]{1,0:T(8,128)S(1)}, f32[256,256]{1,0:T(8,128)S(1)}) custom-call(f32[256,256]{1,0:T(8,128)S(1)} %get-tuple-element.85.near, f32[256,256]{1,0:T(8,128)S(1)} %get-tuple-element.82.far, bf16[1,1536,256]{2,1,0:T(8,128)(2,1)S(1)} %get-tuple-element.86.h_ref, bf16[8,1536,256]{2,1,0:T(8,128)(2,1)S(1)} %get-tuple-element.59.weights, ...), custom_call_target="tpu_custom_call" | custom-call | flops 1107296256 | bytes 8134656 | tf_op jit(solution)/shard_map/pallas_call | solution.py:384
  58.2 0.9 %shard_map.110 = (f32[256,256]{1,0:T(8,128)S(1)}, f32[256,256]{1,0:T(8,128)S(1)}) custom-call(f32[256,256]{1,0:T(8,128)S(1)} %collective-permute-done.16.one, f32[256,256]{1,0:T(8,128)S(1)} %collective-permute-done.17.two, bf16[8,1536,256]{2,1,0:T(8,128)(2,1)S(1)} %get-tuple-element.59.weights, f32[256,256]{1,0:T(8,128)S(1)} %get-tuple-element.87.near, ...), custom_call_target="tpu_custom_call" | custom-call | flops 905969664 | bytes 7864320 | tf_op jit(solution)/shard_map/pallas_call | solution.py:384
  59.1 1.5 %collective-permute-done.15.source = f32[256,256]{1,0:T(8,128)S(1)} collective-permute-done((f32[256,256]{1,0:T(8,128)S(1)}, f32[256,256]{1,0:T(8,128)S(1)}, u32[]{:S(2)}, u32[]{:S(2)}) %collective-permute-start.15) | collective-permute-done | bytes 262176 | tf_op jit(solution)/shard_map/ppermute | solution.py:405
  61.7 1.6 %collective-permute-done.13.source = f32[256,256]{1,0:T(8,128)S(1)} collective-permute-done((f32[256,256]{1,0:T(8,128)S(1)}, f32[256,256]{1,0:T(8,128)S(1)}, u32[]{:S(2)}, u32[]{:S(2)}) %collective-permute-start.13) | collective-permute-done | bytes 262176 | tf_op jit(solution)/shard_map/ppermute | solution.py:405
  64.0 1.4 %collective-permute-start.18 = (f32[256,256]{1,0:T(8,128)S(1)}, f32[256,256]{1,0:T(8,128)S(1)}, u32[]{:S(2)}, u32[]{:S(2)}) collective-permute-start(f32[256,256]{1,0:T(8,128)S(1)} %get-tuple-element.93.first_sent), channel_id=1, source_target_pairs={{0,13},{1,2},{2,6},{3,4},{4,1},{5,3},{6,7},{7,5},{8,14},{9,12},{10... | collective-permute-start | bytes 786440 | tf_op jit(solution)/shard_map/ppermute | solution.py:405
  65.3 5.5 %collective-permute-done.18.first = f32[256,256]{1,0:T(8,128)S(1)} collective-permute-done((f32[256,256]{1,0:T(8,128)S(1)}, f32[256,256]{1,0:T(8,128)S(1)}, u32[]{:S(2)}, u32[]{:S(2)}) %collective-permute-start.18) | collective-permute-done | bytes 262176 | tf_op jit(solution)/shard_map/ppermute | solution.py:405
  70.8 5.0 %collective-permute-done.19.second = f32[256,256]{1,0:T(8,128)S(1)} collective-permute-done((f32[256,256]{1,0:T(8,128)S(1)}, f32[256,256]{1,0:T(8,128)S(1)}, u32[]{:S(2)}, u32[]{:S(2)}) %collective-permute-start.19) | collective-permute-done | bytes 262176 | tf_op jit(solution)/shard_map/ppermute | solution.py:405
  75.8 1.0 %shard_map.114 = f32[1,2,256,256]{3,2,1,0:T(8,128)} custom-call(f32[256,256]{1,0:T(8,128)S(1)} %collective-permute-done.18.first, f32[256,256]{1,0:T(8,128)S(1)} %collective-permute-done.19.second, f32[256,256]{1,0:T(8,128)S(1)} %get-tuple-element.93.first_sent, f32[256,256]{1,0:T(8,128)S(1)} %get-tuple-element.94.second_sent), custom_call_target="tpu_custom_call" | custom-call | bytes 1572864 | tf_op jit(solution)/shard_map/pallas_call | solution.py:384
  (44 shorter events, 10.8 us)
Async XLA Ops:
  2.1 15.7 %collective-permute-start.2 = (f32[264,256]{1,0:T(8,128)}, f32[264,256]{1,0:T(8,128)S(1)}, u32[]{:S(2)}, u32[]{:S(2)}) collective-permute-start(f32[264,256]{1,0:T(8,128)} %get-tuple-element.51), channel_id=1, source_target_pairs={{0,4},{1,0},{2,5},{3,1},{4,7},{5,3},{6,11},{7,2},{8,14},{9,10},{10... | collective-permute-start | bytes 811016 | tf_op jit(solution)/shard_map/ppermute | solution.py:405
  5.2 12.8 %collective-permute-start = (f32[264,256]{1,0:T(8,128)}, f32[264,256]{1,0:T(8,128)S(1)}, u32[]{:S(2)}, u32[]{:S(2)}) collective-permute-start(f32[264,256]{1,0:T(8,128)} %get-tuple-element.50), channel_id=1, source_target_pairs={{0,13},{1,4},{2,1},{3,5},{4,3},{5,7},{6,2},{7,6},{8,10},{9,14},{10... | collective-permute-start | bytes 811016 | tf_op jit(solution)/shard_map/ppermute | solution.py:405
  17.8 12.4 %collective-permute-start.5 = (f32[264,256]{1,0:T(8,128)S(1)}, f32[264,256]{1,0:T(8,128)S(1)}, u32[]{:S(2)}, u32[]{:S(2)}) collective-permute-start(f32[264,256]{1,0:T(8,128)S(1)} %broadcast_select_fusion.array), channel_id=1, source_target_pairs={{0,1},{1,0},{2,3},{3,2},{4,5},{5,4},{6,7},{7,6},{8,9},{9,8},{10,11... | collective-permute-start | bytes 811016 | tf_op jit(solution)/shard_map/ppermute | solution.py:405
  18.9 11.4 %collective-permute-start.4 = (f32[264,256]{1,0:T(8,128)S(1)}, f32[264,256]{1,0:T(8,128)S(1)}, u32[]{:S(2)}, u32[]{:S(2)}) collective-permute-start(f32[264,256]{1,0:T(8,128)S(1)} %broadcast_select_fusion.1.array), channel_id=1, source_target_pairs={{0,1},{1,0},{2,3},{3,2},{4,5},{5,4},{6,7},{7,6},{8,9},{9,8},{10,11... | collective-permute-start | bytes 811016 | tf_op jit(solution)/shard_map/ppermute | solution.py:405
  19.0 12.2 %collective-permute-start.3 = (f32[264,256]{1,0:T(8,128)S(1)}, f32[264,256]{1,0:T(8,128)S(1)}, u32[]{:S(2)}, u32[]{:S(2)}) collective-permute-start(f32[264,256]{1,0:T(8,128)S(1)} %broadcast_select_fusion.array), channel_id=1, source_target_pairs={{0,4},{1,3},{2,10},{3,1},{4,0},{5,7},{6,14},{7,5},{8,16},{9,11},{1... | collective-permute-start | bytes 811016 | tf_op jit(solution)/shard_map/ppermute | solution.py:405
  20.9 10.3 %collective-permute-start.1 = (f32[264,256]{1,0:T(8,128)S(1)}, f32[264,256]{1,0:T(8,128)S(1)}, u32[]{:S(2)}, u32[]{:S(2)}) collective-permute-start(f32[264,256]{1,0:T(8,128)S(1)} %broadcast_select_fusion.1.array), channel_id=1, source_target_pairs={{0,4},{1,3},{2,10},{3,1},{4,0},{5,7},{6,14},{7,5},{8,16},{9,11},{1... | collective-permute-start | bytes 811016 | tf_op jit(solution)/shard_map/ppermute | solution.py:405
  21.1 1.1 %copy-start = (f32[3,256,256]{2,1,0:T(8,128)S(1)}, f32[3,256,256]{2,1,0:T(8,128)}, u32[]{:S(2)}) copy-start(f32[3,256,256]{2,1,0:T(8,128)} %couple.1) | copy-start | bytes 2359300
  22.2 1.0 %copy-start.1 = (f32[2,256,256]{2,1,0:T(8,128)S(1)}, f32[2,256,256]{2,1,0:T(8,128)}, u32[]{:S(2)}) copy-start(f32[2,256,256]{2,1,0:T(8,128)} %h_static.1) | copy-start | bytes 1572868
  23.3 1.0 %copy-start.2 = (f32[2,256,256]{2,1,0:T(8,128)S(1)}, f32[2,256,256]{2,1,0:T(8,128)}, u32[]{:S(2)}) copy-start(f32[2,256,256]{2,1,0:T(8,128)} %drive_op.1) | copy-start | bytes 1572868
  24.3 0.7 copy-start.3
  25.0 0.7 copy-start.4
  32.3 4.9 %collective-permute-start.8 = (f32[256,256]{1,0:T(8,128)S(1)}, f32[256,256]{1,0:T(8,128)S(1)}, u32[]{:S(2)}, u32[]{:S(2)}) collective-permute-start(f32[256,256]{1,0:T(8,128)S(1)} %get-tuple-element.67.near), channel_id=1, source_target_pairs={{0,1},{1,0},{2,3},{3,2},{4,5},{5,4},{6,7},{7,6},{8,9},{9,8},{10,11... | collective-permute-start | bytes 786440 | tf_op jit(solution)/shard_map/ppermute | solution.py:405
  33.0 4.2 %collective-permute-start.9 = (f32[256,256]{1,0:T(8,128)S(1)}, f32[256,256]{1,0:T(8,128)S(1)}, u32[]{:S(2)}, u32[]{:S(2)}) collective-permute-start(f32[256,256]{1,0:T(8,128)S(1)} %get-tuple-element.65.far), channel_id=1, source_target_pairs={{0,1},{1,0},{2,3},{3,2},{4,5},{5,4},{6,7},{7,6},{8,9},{9,8},{10,11... | collective-permute-start | bytes 786440 | tf_op jit(solution)/shard_map/ppermute | solution.py:405
  33.4 6.4 %collective-permute-start.7 = (f32[256,256]{1,0:T(8,128)S(1)}, f32[256,256]{1,0:T(8,128)S(1)}, u32[]{:S(2)}, u32[]{:S(2)}) collective-permute-start(f32[256,256]{1,0:T(8,128)S(1)} %get-tuple-element.67.near), channel_id=1, source_target_pairs={{0,4},{1,3},{2,10},{3,1},{4,0},{5,7},{6,14},{7,5},{8,16},{9,11},{1... | collective-permute-start | bytes 786440 | tf_op jit(solution)/shard_map/ppermute | solution.py:405
  35.2 7.4 %collective-permute-start.6 = (f32[256,256]{1,0:T(8,128)S(1)}, f32[256,256]{1,0:T(8,128)S(1)}, u32[]{:S(2)}, u32[]{:S(2)}) collective-permute-start(f32[256,256]{1,0:T(8,128)S(1)} %get-tuple-element.65.far), channel_id=1, source_target_pairs={{0,4},{1,3},{2,10},{3,1},{4,0},{5,7},{6,14},{7,5},{8,16},{9,11},{1... | collective-permute-start | bytes 786440 | tf_op jit(solution)/shard_map/ppermute | solution.py:405
  40.4 6.7 %collective-permute-start.12 = (f32[256,256]{1,0:T(8,128)S(1)}, f32[256,256]{1,0:T(8,128)S(1)}, u32[]{:S(2)}, u32[]{:S(2)}) collective-permute-start(f32[256,256]{1,0:T(8,128)S(1)} %get-tuple-element.77.far), channel_id=1, source_target_pairs={{0,1},{1,0},{2,3},{3,2},{4,5},{5,4},{6,7},{7,6},{8,9},{9,8},{10,11... | collective-permute-start | bytes 786440 | tf_op jit(solution)/shard_map/ppermute | solution.py:405
  43.2 3.9 %collective-permute-start.11 = (f32[256,256]{1,0:T(8,128)S(1)}, f32[256,256]{1,0:T(8,128)S(1)}, u32[]{:S(2)}, u32[]{:S(2)}) collective-permute-start(f32[256,256]{1,0:T(8,128)S(1)} %get-tuple-element.74.near), channel_id=1, source_target_pairs={{0,1},{1,0},{2,3},{3,2},{4,5},{5,4},{6,7},{7,6},{8,9},{9,8},{10,11... | collective-permute-start | bytes 786440 | tf_op jit(solution)/shard_map/ppermute | solution.py:405
  43.3 6.4 %collective-permute-start.14 = (f32[256,256]{1,0:T(8,128)S(1)}, f32[256,256]{1,0:T(8,128)S(1)}, u32[]{:S(2)}, u32[]{:S(2)}) collective-permute-start(f32[256,256]{1,0:T(8,128)S(1)} %get-tuple-element.77.far), channel_id=1, source_target_pairs={{0,4},{1,3},{2,10},{3,1},{4,0},{5,7},{6,14},{7,5},{8,16},{9,11},{1... | collective-permute-start | bytes 786440 | tf_op jit(solution)/shard_map/ppermute | solution.py:405
  45.2 7.4 %collective-permute-start.10 = (f32[256,256]{1,0:T(8,128)S(1)}, f32[256,256]{1,0:T(8,128)S(1)}, u32[]{:S(2)}, u32[]{:S(2)}) collective-permute-start(f32[256,256]{1,0:T(8,128)S(1)} %get-tuple-element.74.near), channel_id=1, source_target_pairs={{0,4},{1,3},{2,10},{3,1},{4,0},{5,7},{6,14},{7,5},{8,16},{9,11},{1... | collective-permute-start | bytes 786440 | tf_op jit(solution)/shard_map/ppermute | solution.py:405
  53.1 5.0 %collective-permute-start.16 = (f32[256,256]{1,0:T(8,128)S(1)}, f32[256,256]{1,0:T(8,128)S(1)}, u32[]{:S(2)}, u32[]{:S(2)}) collective-permute-start(f32[256,256]{1,0:T(8,128)S(1)} %get-tuple-element.85.near), channel_id=1, source_target_pairs={{0,1},{1,0},{2,3},{3,2},{4,5},{5,4},{6,7},{7,6},{8,9},{9,8},{10,11... | collective-permute-start | bytes 786440 | tf_op jit(solution)/shard_map/ppermute | solution.py:405
  53.8 4.4 %collective-permute-start.17 = (f32[256,256]{1,0:T(8,128)S(1)}, f32[256,256]{1,0:T(8,128)S(1)}, u32[]{:S(2)}, u32[]{:S(2)}) collective-permute-start(f32[256,256]{1,0:T(8,128)S(1)} %get-tuple-element.82.far), channel_id=1, source_target_pairs={{0,1},{1,0},{2,3},{3,2},{4,5},{5,4},{6,7},{7,6},{8,9},{9,8},{10,11... | collective-permute-start | bytes 786440 | tf_op jit(solution)/shard_map/ppermute | solution.py:405
  54.2 6.4 %collective-permute-start.15 = (f32[256,256]{1,0:T(8,128)S(1)}, f32[256,256]{1,0:T(8,128)S(1)}, u32[]{:S(2)}, u32[]{:S(2)}) collective-permute-start(f32[256,256]{1,0:T(8,128)S(1)} %get-tuple-element.85.near), channel_id=1, source_target_pairs={{0,4},{1,3},{2,10},{3,1},{4,0},{5,7},{6,14},{7,5},{8,16},{9,11},{1... | collective-permute-start | bytes 786440 | tf_op jit(solution)/shard_map/ppermute | solution.py:405
  56.0 7.4 %collective-permute-start.13 = (f32[256,256]{1,0:T(8,128)S(1)}, f32[256,256]{1,0:T(8,128)S(1)}, u32[]{:S(2)}, u32[]{:S(2)}) collective-permute-start(f32[256,256]{1,0:T(8,128)S(1)} %get-tuple-element.82.far), channel_id=1, source_target_pairs={{0,4},{1,3},{2,10},{3,1},{4,0},{5,7},{6,14},{7,5},{8,16},{9,11},{1... | collective-permute-start | bytes 786440 | tf_op jit(solution)/shard_map/ppermute | solution.py:405
  64.0 6.9 %collective-permute-start.18 = (f32[256,256]{1,0:T(8,128)S(1)}, f32[256,256]{1,0:T(8,128)S(1)}, u32[]{:S(2)}, u32[]{:S(2)}) collective-permute-start(f32[256,256]{1,0:T(8,128)S(1)} %get-tuple-element.93.first_sent), channel_id=1, source_target_pairs={{0,13},{1,2},{2,6},{3,4},{4,1},{5,3},{6,7},{7,5},{8,14},{9,12},{10... | collective-permute-start | bytes 786440 | tf_op jit(solution)/shard_map/ppermute | solution.py:405
  65.3 10.5 %collective-permute-start.19 = (f32[256,256]{1,0:T(8,128)S(1)}, f32[256,256]{1,0:T(8,128)S(1)}, u32[]{:S(2)}, u32[]{:S(2)}) collective-permute-start(f32[256,256]{1,0:T(8,128)S(1)} %get-tuple-element.94.second_sent), channel_id=1, source_target_pairs={{0,1},{1,3},{2,7},{3,5},{4,0},{5,2},{6,11},{7,4},{8,15},{9,13},{10... | collective-permute-start | bytes 786440 | tf_op jit(solution)/shard_map/ppermute | solution.py:405

commit v2 on v1

--- a/solution.py
+++ b/solution.py
@@ -55,8 +55,10 @@
 
 def full(pairs):
     fixed = [a for a, b in pairs if a == b]
-    swaps = dict(zip(fixed[::2], fixed[1::2]))
-    swaps.update({b: a for a, b in swaps.items()})
+    swaps = {}
+    for place in range(0, len(fixed) - 3, 4):
+        for a, b in ((fixed[place], fixed[place + 2]), (fixed[place + 1], fixed[place + 3])):
+            swaps.update({a: b, b: a})
     return [(a, swaps.get(a, b)) for a, b in pairs]
 
 

time: 77.2 us -> 74.4 us (0.964)
  the two profiles are of different devices: /device:TPU:0 before, /device:TPU:8 now
where the time goes in v2:
time: 74.4 us; the launch traced here: 73 us
  waiting for transfers between devices  30.5 us (41%)
  Pallas kernels  23.5 us (32%)
  starting transfers between devices  14 us (19%)
  local copies, waits for them, and re-layouts  4.55 us (6%)
    ppermute x20, waiting for transfers between devices, send(): return lax.ppermute(value, 'aux', pairs)  30.5 us
    pallas_call x24, Pallas kernels, call(): pl.pallas_call(kernel, out_shape=shapes[0] if single else shapes, in_spec...  23.5 us
    ppermute x20, starting transfers between devices, send(): return lax.ppermute(value, 'aux', pairs)  14 us
    unnamed x10, local copies, waits for them, and re-layouts  4.55 us
  transfers between devices with their start and end apart: 20, of which 10 were waited for; matrix products, arithmetic and copies ran while one was open for 0% of the time, Pallas kernels for 26%

profile of v2, /device:TPU:8, one launch (start us, length us, event | category | flops | bytes accessed | tf_op | source)
XLA Modules:
  0.0 73.0 jit_solution(2079516053721579094)
XLA Ops:
  0.0 2.1 %shard_map.91 = (f32[264,256]{1,0:T(8,128)}, f32[264,256]{1,0:T(8,128)}) custom-call(f32[1,2,256,256]{3,2,1,0:T(8,128)} %state_hbm.1, s32[1,3]{1,0:T(1,128)} %occ_hbm.1, s32[1,3]{1,0:T(1,128)} %up_hbm.1, s32[1,3]{1,0:T(1,128)} %low_hbm.1), custom_call_target="tpu_custom_call" | custom-call | bytes 1064996 | tf_op jit(solution)/shard_map/pallas_call | solution.py:386
  2.1 2.5 %collective-permute-start.2 = (f32[264,256]{1,0:T(8,128)}, f32[264,256]{1,0:T(8,128)S(1)}, u32[]{:S(2)}, u32[]{:S(2)}) collective-permute-start(f32[264,256]{1,0:T(8,128)} %get-tuple-element.51), channel_id=1, source_target_pairs={{0,4},{1,0},{2,5},{3,1},{4,7},{5,3},{6,22},{7,2},{8,14},{9,10},{10... | collective-permute-start | bytes 811016 | tf_op jit(solution)/shard_map/ppermute | solution.py:407
  4.6 7.2 %collective-permute-done.2 = f32[264,256]{1,0:T(8,128)S(1)} collective-permute-done((f32[264,256]{1,0:T(8,128)}, f32[264,256]{1,0:T(8,128)S(1)}, u32[]{:S(2)}, u32[]{:S(2)}) %collective-permute-start.2) | collective-permute-done | bytes 270368 | tf_op jit(solution)/shard_map/ppermute | solution.py:407
  12.0 5.9 %collective-permute-done = f32[264,256]{1,0:T(8,128)S(1)} collective-permute-done((f32[264,256]{1,0:T(8,128)}, f32[264,256]{1,0:T(8,128)S(1)}, u32[]{:S(2)}, u32[]{:S(2)}) %collective-permute-start) | collective-permute-done | bytes 270368 | tf_op jit(solution)/shard_map/ppermute | solution.py:407
  18.0 1.2 %collective-permute-start.3 = (f32[264,256]{1,0:T(8,128)S(1)}, f32[264,256]{1,0:T(8,128)S(1)}, u32[]{:S(2)}, u32[]{:S(2)}) collective-permute-start(f32[264,256]{1,0:T(8,128)S(1)} %broadcast_select_fusion.array), channel_id=1, source_target_pairs={{0,4},{1,3},{2,10},{3,1},{4,0},{5,7},{6,14},{7,5},{8,16},{9,11},{1... | collective-permute-start | bytes 811016 | tf_op jit(solution)/shard_map/ppermute | solution.py:407
  20.1 1.1 %copy-done = f32[3,256,256]{2,1,0:T(8,128)S(1)} copy-done((f32[3,256,256]{2,1,0:T(8,128)S(1)}, f32[3,256,256]{2,1,0:T(8,128)}, u32[]{:S(2)}) %copy-start) | copy-done | bytes 786456
  21.2 1.0 %copy-done.1 = f32[2,256,256]{2,1,0:T(8,128)S(1)} copy-done((f32[2,256,256]{2,1,0:T(8,128)S(1)}, f32[2,256,256]{2,1,0:T(8,128)}, u32[]{:S(2)}) %copy-start.1) | copy-done | bytes 524312
  22.2 1.0 %copy-done.2 = f32[2,256,256]{2,1,0:T(8,128)S(1)} copy-done((f32[2,256,256]{2,1,0:T(8,128)S(1)}, f32[2,256,256]{2,1,0:T(8,128)}, u32[]{:S(2)}) %copy-start.2) | copy-done | bytes 524312
  24.6 1.4 %shard_map.92 = (bf16[1,1536,256]{2,1,0:T(8,128)(2,1)S(1)}, bf16[1,1536,256]{2,1,0:T(8,128)(2,1)S(1)}, bf16[1,1536,256]{2,1,0:T(8,128)(2,1)S(1)}, f32[3,256,256]{2,1,0:T(8,128)S(1)}, f32[9,8,128]{2,1,0:T(8,128)S(1)}) custom-call(f32[2,256,256]{2,1,0:T(8,128)S(1)} %copy-done.1, f32[2,256,256]{2,1,0:T(8,128)S(1)} %copy-done.2, f32[3,256,256]{2,1,0:T(8,128)S(1)} %copy-done, ...), custom_call_target="tpu_custom_call" | custom-call | bytes 5017636 | tf_op jit(solution)/shard_map/pallas_call | solution.py:386
  26.0 1.2 %shard_map.93 = (bf16[8,1536,256]{2,1,0:T(8,128)(2,1)S(1)}, f32[2,256,256]{2,1,0:T(8,128)S(1)}, f32[2,8,128]{2,1,0:T(8,128)S(1)}, f32[2,256,256]{2,1,0:T(8,128)S(1)}) custom-call(f32[264,256]{1,0:T(8,128)S(1)} %broadcast_select_fusion.1.array, f32[3,256,256]{2,1,0:T(8,128)S(1)} %get-tuple-element.52.q_ref, f32[9,8,128]{2,1,0:T(8,128)S(1)} %get-tuple-element.53.damp, ...), custom_call_target="tpu_custom_call" | custom-call | flops 301989888 | bytes 9228288 | tf_op jit(solution)/shard_map/pallas_call | solution.py:386
  27.2 1.2 %shard_map.94 = (bf16[8,1536,256]{2,1,0:T(8,128)(2,1)S(1)}, f32[2,256,256]{2,1,0:T(8,128)S(1)}, f32[2,8,128]{2,1,0:T(8,128)S(1)}, f32[2,256,256]{2,1,0:T(8,128)S(1)}) custom-call(f32[264,256]{1,0:T(8,128)S(1)} %broadcast_select_fusion.array, ...), custom_call_target="tpu_custom_call", output_to_operand_aliasing={{0}: (4, {}), {1}: (5, {}), {2}: (6, {}), {3}: (7, {})} | custom-call | flops 301989888 | bytes 16576512 | tf_op jit(solution)/shard_map/pallas_call | solution.py:386
  29.3 1.3 %shard_map.96 = (f32[256,256]{1,0:T(8,128)S(1)}, f32[256,256]{1,0:T(8,128)S(1)}) custom-call(f32[264,256]{1,0:T(8,128)S(1)} %collective-permute-done.4.one, f32[264,256]{1,0:T(8,128)S(1)} %collective-permute-done.5.two, bf16[8,1536,256]{2,1,0:T(8,128)(2,1)S(1)} %get-tuple-element.59.weights, f32[256,256]{1,0:T(8,128)S(1)} %get-tuple-element.62.near, ...), custom_call_target="tpu_custom_call" | custom-call | flops 905969664 | bytes 7880704 | tf_op jit(solution)/shard_map/pallas_call | solution.py:386
  33.5 1.1 %collective-permute-start.6 = (f32[256,256]{1,0:T(8,128)S(1)}, f32[256,256]{1,0:T(8,128)S(1)}, u32[]{:S(2)}, u32[]{:S(2)}) collective-permute-start(f32[256,256]{1,0:T(8,128)S(1)} %get-tuple-element.65.far), channel_id=1, source_target_pairs={{0,4},{1,3},{2,10},{3,1},{4,0},{5,7},{6,14},{7,5},{8,16},{9,11},{1... | collective-permute-start | bytes 786440 | tf_op jit(solution)/shard_map/ppermute | solution.py:407
  34.6 1.7 %shard_map.99 = (f32[256,256]{1,0:T(8,128)S(1)}, f32[256,256]{1,0:T(8,128)S(1)}) custom-call(f32[256,256]{1,0:T(8,128)S(1)} %get-tuple-element.67.near, f32[256,256]{1,0:T(8,128)S(1)} %get-tuple-element.65.far, bf16[1,1536,256]{2,1,0:T(8,128)(2,1)S(1)} %get-tuple-element.68.h_ref, bf16[8,1536,256]{2,1,0:T(8,128)(2,1)S(1)} %get-tuple-element.59.weights, ...), custom_call_target="tpu_custom_call" | custom-call | flops 1107296256 | bytes 8134656 | tf_op jit(solution)/shard_map/pallas_call | solution.py:386
  36.3 1.4 %shard_map.100 = (f32[256,256]{1,0:T(8,128)S(1)}, f32[256,256]{1,0:T(8,128)S(1)}) custom-call(f32[256,256]{1,0:T(8,128)S(1)} %collective-permute-done.8.one, f32[256,256]{1,0:T(8,128)S(1)} %collective-permute-done.9.two, bf16[8,1536,256]{2,1,0:T(8,128)(2,1)S(1)} %get-tuple-element.59.weights, f32[256,256]{1,0:T(8,128)S(1)} %get-tuple-element.70.near, ...), custom_call_target="tpu_custom_call" | custom-call | flops 905969664 | bytes 7864320 | tf_op jit(solution)/shard_map/pallas_call | solution.py:386
  37.8 1.2 %collective-permute-done.7.source = f32[256,256]{1,0:T(8,128)S(1)} collective-permute-done((f32[256,256]{1,0:T(8,128)S(1)}, f32[256,256]{1,0:T(8,128)S(1)}, u32[]{:S(2)}, u32[]{:S(2)}) %collective-permute-start.7) | collective-permute-done | bytes 262176 | tf_op jit(solution)/shard_map/ppermute | solution.py:407
  39.9 1.8 %collective-permute-done.6.source = f32[256,256]{1,0:T(8,128)S(1)} collective-permute-done((f32[256,256]{1,0:T(8,128)S(1)}, f32[256,256]{1,0:T(8,128)S(1)}, u32[]{:S(2)}, u32[]{:S(2)}) %collective-permute-start.6) | collective-permute-done | bytes 262176 | tf_op jit(solution)/shard_map/ppermute | solution.py:407
  42.3 1.2 %collective-permute-start.14 = (f32[256,256]{1,0:T(8,128)S(1)}, f32[256,256]{1,0:T(8,128)S(1)}, u32[]{:S(2)}, u32[]{:S(2)}) collective-permute-start(f32[256,256]{1,0:T(8,128)S(1)} %get-tuple-element.77.far), channel_id=1, source_target_pairs={{0,4},{1,3},{2,10},{3,1},{4,0},{5,7},{6,14},{7,5},{8,16},{9,11},{1... | collective-permute-start | bytes 786440 | tf_op jit(solution)/shard_map/ppermute | solution.py:407
  44.4 1.7 %shard_map.104 = (f32[256,256]{1,0:T(8,128)S(1)}, f32[256,256]{1,0:T(8,128)S(1)}) custom-call(f32[256,256]{1,0:T(8,128)S(1)} %get-tuple-element.74.near, f32[256,256]{1,0:T(8,128)S(1)} %get-tuple-element.77.far, bf16[1,1536,256]{2,1,0:T(8,128)(2,1)S(1)} %get-tuple-element.68.h_ref, bf16[8,1536,256]{2,1,0:T(8,128)(2,1)S(1)} %get-tuple-element.59.weights, ...), custom_call_target="tpu_custom_call" | custom-call | flops 1107296256 | bytes 8134656 | tf_op jit(solution)/shard_map/pallas_call | solution.py:386
  46.1 1.3 %shard_map.105 = (f32[256,256]{1,0:T(8,128)S(1)}, f32[256,256]{1,0:T(8,128)S(1)}) custom-call(f32[256,256]{1,0:T(8,128)S(1)} %collective-permute-done.11.one, f32[256,256]{1,0:T(8,128)S(1)} %collective-permute-done.12.two, bf16[8,1536,256]{2,1,0:T(8,128)(2,1)S(1)} %get-tuple-element.59.weights, f32[256,256]{1,0:T(8,128)S(1)} %get-tuple-element.78.near, ...), custom_call_target="tpu_custom_call" | custom-call | flops 905969664 | bytes 7864320 | tf_op jit(solution)/shard_map/pallas_call | solution.py:386
  47.4 1.3 %collective-permute-done.14.source = f32[256,256]{1,0:T(8,128)S(1)} collective-permute-done((f32[256,256]{1,0:T(8,128)S(1)}, f32[256,256]{1,0:T(8,128)S(1)}, u32[]{:S(2)}, u32[]{:S(2)}) %collective-permute-start.14) | collective-permute-done | bytes 262176 | tf_op jit(solution)/shard_map/ppermute | solution.py:407
  49.1 2.4 %collective-permute-done.10.source = f32[256,256]{1,0:T(8,128)S(1)} collective-permute-done((f32[256,256]{1,0:T(8,128)S(1)}, f32[256,256]{1,0:T(8,128)S(1)}, u32[]{:S(2)}, u32[]{:S(2)}) %collective-permute-start.10) | collective-permute-done | bytes 262176 | tf_op jit(solution)/shard_map/ppermute | solution.py:407
  53.2 1.1 %collective-permute-start.15 = (f32[256,256]{1,0:T(8,128)S(1)}, f32[256,256]{1,0:T(8,128)S(1)}, u32[]{:S(2)}, u32[]{:S(2)}) collective-permute-start(f32[256,256]{1,0:T(8,128)S(1)} %get-tuple-element.85.near), channel_id=1, source_target_pairs={{0,4},{1,3},{2,10},{3,1},{4,0},{5,7},{6,14},{7,5},{8,16},{9,11},{1... | collective-permute-start | bytes 786440 | tf_op jit(solution)/shard_map/ppermute | solution.py:407
  54.3 0.9 %collective-permute-start.13 = (f32[256,256]{1,0:T(8,128)S(1)}, f32[256,256]{1,0:T(8,128)S(1)}, u32[]{:S(2)}, u32[]{:S(2)}) collective-permute-start(f32[256,256]{1,0:T(8,128)S(1)} %get-tuple-element.82.far), channel_id=1, source_target_pairs={{0,4},{1,3},{2,10},{3,1},{4,0},{5,7},{6,14},{7,5},{8,16},{9,11},{1... | collective-permute-start | bytes 786440 | tf_op jit(solution)/shard_map/ppermute | solution.py:407
  55.2 1.9 %shard_map.109 = (f32[256,256]{1,0:T(8,128)S(1)}, f32[256,256]{1,0:T(8,128)S(1)}) custom-call(f32[256,256]{1,0:T(8,128)S(1)} %get-tuple-element.85.near, f32[256,256]{1,0:T(8,128)S(1)} %get-tuple-element.82.far, bf16[1,1536,256]{2,1,0:T(8,128)(2,1)S(1)} %get-tuple-element.86.h_ref, bf16[8,1536,256]{2,1,0:T(8,128)(2,1)S(1)} %get-tuple-element.59.weights, ...), custom_call_target="tpu_custom_call" | custom-call | flops 1107296256 | bytes 8134656 | tf_op jit(solution)/shard_map/pallas_call | solution.py:386
  57.2 1.3 %shard_map.110 = (f32[256,256]{1,0:T(8,128)S(1)}, f32[256,256]{1,0:T(8,128)S(1)}) custom-call(f32[256,256]{1,0:T(8,128)S(1)} %collective-permute-done.16.one, f32[256,256]{1,0:T(8,128)S(1)} %collective-permute-done.17.two, bf16[8,1536,256]{2,1,0:T(8,128)(2,1)S(1)} %get-tuple-element.59.weights, f32[256,256]{1,0:T(8,128)S(1)} %get-tuple-element.87.near, ...), custom_call_target="tpu_custom_call" | custom-call | flops 905969664 | bytes 7864320 | tf_op jit(solution)/shard_map/pallas_call | solution.py:386
  58.5 1.1 %collective-permute-done.15.source = f32[256,256]{1,0:T(8,128)S(1)} collective-permute-done((f32[256,256]{1,0:T(8,128)S(1)}, f32[256,256]{1,0:T(8,128)S(1)}, u32[]{:S(2)}, u32[]{:S(2)}) %collective-permute-start.15) | collective-permute-done | bytes 262176 | tf_op jit(solution)/shard_map/ppermute | solution.py:407
  60.5 1.9 %collective-permute-done.13.source = f32[256,256]{1,0:T(8,128)S(1)} collective-permute-done((f32[256,256]{1,0:T(8,128)S(1)}, f32[256,256]{1,0:T(8,128)S(1)}, u32[]{:S(2)}, u32[]{:S(2)}) %collective-permute-start.13) | collective-permute-done | bytes 262176 | tf_op jit(solution)/shard_map/ppermute | solution.py:407
  62.8 1.5 %collective-permute-start.18 = (f32[256,256]{1,0:T(8,128)S(1)}, f32[256,256]{1,0:T(8,128)S(1)}, u32[]{:S(2)}, u32[]{:S(2)}) collective-permute-start(f32[256,256]{1,0:T(8,128)S(1)} %get-tuple-element.93.first_sent), channel_id=1, source_target_pairs={{0,16},{1,2},{2,6},{3,4},{4,1},{5,3},{6,7},{7,5},{8,14},{9,12},{10... | collective-permute-start | bytes 786440 | tf_op jit(solution)/shard_map/ppermute | solution.py:407
  64.3 5.0 %collective-permute-done.18.first = f32[256,256]{1,0:T(8,128)S(1)} collective-permute-done((f32[256,256]{1,0:T(8,128)S(1)}, f32[256,256]{1,0:T(8,128)S(1)}, u32[]{:S(2)}, u32[]{:S(2)}) %collective-permute-start.18) | collective-permute-done | bytes 262176 | tf_op jit(solution)/shard_map/ppermute | solution.py:407
  69.3 2.7 %collective-permute-done.19.second = f32[256,256]{1,0:T(8,128)S(1)} collective-permute-done((f32[256,256]{1,0:T(8,128)S(1)}, f32[256,256]{1,0:T(8,128)S(1)}, u32[]{:S(2)}, u32[]{:S(2)}) %collective-permute-start.19) | collective-permute-done | bytes 262176 | tf_op jit(solution)/shard_map/ppermute | solution.py:407
  72.0 1.0 %shard_map.114 = f32[1,2,256,256]{3,2,1,0:T(8,128)} custom-call(f32[256,256]{1,0:T(8,128)S(1)} %collective-permute-done.18.first, f32[256,256]{1,0:T(8,128)S(1)} %collective-permute-done.19.second, f32[256,256]{1,0:T(8,128)S(1)} %get-tuple-element.93.first_sent, f32[256,256]{1,0:T(8,128)S(1)} %get-tuple-element.94.second_sent), custom_call_target="tpu_custom_call" | custom-call | bytes 1572864 | tf_op jit(solution)/shard_map/pallas_call | solution.py:386
  (44 shorter events, 12.0 us)
Async XLA Ops:
  2.1 9.7 %collective-permute-start.2 = (f32[264,256]{1,0:T(8,128)}, f32[264,256]{1,0:T(8,128)S(1)}, u32[]{:S(2)}, u32[]{:S(2)}) collective-permute-start(f32[264,256]{1,0:T(8,128)} %get-tuple-element.51), channel_id=1, source_target_pairs={{0,4},{1,0},{2,5},{3,1},{4,7},{5,3},{6,22},{7,2},{8,14},{9,10},{10... | collective-permute-start | bytes 811016 | tf_op jit(solution)/shard_map/ppermute | solution.py:407
  4.6 13.2 %collective-permute-start = (f32[264,256]{1,0:T(8,128)}, f32[264,256]{1,0:T(8,128)S(1)}, u32[]{:S(2)}, u32[]{:S(2)}) collective-permute-start(f32[264,256]{1,0:T(8,128)} %get-tuple-element.50), channel_id=1, source_target_pairs={{0,16},{1,4},{2,1},{3,5},{4,3},{5,7},{6,2},{7,6},{8,10},{9,14},{10... | collective-permute-start | bytes 811016 | tf_op jit(solution)/shard_map/ppermute | solution.py:407
  11.9 17.4 %collective-permute-start.5 = (f32[264,256]{1,0:T(8,128)S(1)}, f32[264,256]{1,0:T(8,128)S(1)}, u32[]{:S(2)}, u32[]{:S(2)}) collective-permute-start(f32[264,256]{1,0:T(8,128)S(1)} %broadcast_select_fusion.array), channel_id=1, source_target_pairs={{0,1},{1,0},{2,3},{3,2},{4,5},{5,4},{6,7},{7,6},{8,9},{9,8},{10,11... | collective-permute-start | bytes 811016 | tf_op jit(solution)/shard_map/ppermute | solution.py:407
  17.9 11.4 %collective-permute-start.4 = (f32[264,256]{1,0:T(8,128)S(1)}, f32[264,256]{1,0:T(8,128)S(1)}, u32[]{:S(2)}, u32[]{:S(2)}) collective-permute-start(f32[264,256]{1,0:T(8,128)S(1)} %broadcast_select_fusion.1.array), channel_id=1, source_target_pairs={{0,1},{1,0},{2,3},{3,2},{4,5},{5,4},{6,7},{7,6},{8,9},{9,8},{10,11... | collective-permute-start | bytes 811016 | tf_op jit(solution)/shard_map/ppermute | solution.py:407
  18.0 12.6 %collective-permute-start.3 = (f32[264,256]{1,0:T(8,128)S(1)}, f32[264,256]{1,0:T(8,128)S(1)}, u32[]{:S(2)}, u32[]{:S(2)}) collective-permute-start(f32[264,256]{1,0:T(8,128)S(1)} %broadcast_select_fusion.array), channel_id=1, source_target_pairs={{0,4},{1,3},{2,10},{3,1},{4,0},{5,7},{6,14},{7,5},{8,16},{9,11},{1... | collective-permute-start | bytes 811016 | tf_op jit(solution)/shard_map/ppermute | solution.py:407
  19.2 11.4 %collective-permute-start.1 = (f32[264,256]{1,0:T(8,128)S(1)}, f32[264,256]{1,0:T(8,128)S(1)}, u32[]{:S(2)}, u32[]{:S(2)}) collective-permute-start(f32[264,256]{1,0:T(8,128)S(1)} %broadcast_select_fusion.1.array), channel_id=1, source_target_pairs={{0,4},{1,3},{2,10},{3,1},{4,0},{5,7},{6,14},{7,5},{8,16},{9,11},{1... | collective-permute-start | bytes 811016 | tf_op jit(solution)/shard_map/ppermute | solution.py:407
  20.1 1.1 %copy-start = (f32[3,256,256]{2,1,0:T(8,128)S(1)}, f32[3,256,256]{2,1,0:T(8,128)}, u32[]{:S(2)}) copy-start(f32[3,256,256]{2,1,0:T(8,128)} %couple.1) | copy-start | bytes 2359300
  21.2 1.0 %copy-start.1 = (f32[2,256,256]{2,1,0:T(8,128)S(1)}, f32[2,256,256]{2,1,0:T(8,128)}, u32[]{:S(2)}) copy-start(f32[2,256,256]{2,1,0:T(8,128)} %h_static.1) | copy-start | bytes 1572868
  22.2 1.0 %copy-start.2 = (f32[2,256,256]{2,1,0:T(8,128)S(1)}, f32[2,256,256]{2,1,0:T(8,128)}, u32[]{:S(2)}) copy-start(f32[2,256,256]{2,1,0:T(8,128)} %drive_op.1) | copy-start | bytes 1572868
  23.3 0.7 copy-start.3
  24.0 0.7 copy-start.4
  31.3 5.0 %collective-permute-start.8 = (f32[256,256]{1,0:T(8,128)S(1)}, f32[256,256]{1,0:T(8,128)S(1)}, u32[]{:S(2)}, u32[]{:S(2)}) collective-permute-start(f32[256,256]{1,0:T(8,128)S(1)} %get-tuple-element.67.near), channel_id=1, source_target_pairs={{0,1},{1,0},{2,3},{3,2},{4,5},{5,4},{6,7},{7,6},{8,9},{9,8},{10,11... | collective-permute-start | bytes 786440 | tf_op jit(solution)/shard_map/ppermute | solution.py:407
  31.9 4.4 %collective-permute-start.9 = (f32[256,256]{1,0:T(8,128)S(1)}, f32[256,256]{1,0:T(8,128)S(1)}, u32[]{:S(2)}, u32[]{:S(2)}) collective-permute-start(f32[256,256]{1,0:T(8,128)S(1)} %get-tuple-element.65.far), channel_id=1, source_target_pairs={{0,1},{1,0},{2,3},{3,2},{4,5},{5,4},{6,7},{7,6},{8,9},{9,8},{10,11... | collective-permute-start | bytes 786440 | tf_op jit(solution)/shard_map/ppermute | solution.py:407
  32.6 6.4 %collective-permute-start.7 = (f32[256,256]{1,0:T(8,128)S(1)}, f32[256,256]{1,0:T(8,128)S(1)}, u32[]{:S(2)}, u32[]{:S(2)}) collective-permute-start(f32[256,256]{1,0:T(8,128)S(1)} %get-tuple-element.67.near), channel_id=1, source_target_pairs={{0,4},{1,3},{2,10},{3,1},{4,0},{5,7},{6,14},{7,5},{8,16},{9,11},{1... | collective-permute-start | bytes 786440 | tf_op jit(solution)/shard_map/ppermute | solution.py:407
  33.5 8.2 %collective-permute-start.6 = (f32[256,256]{1,0:T(8,128)S(1)}, f32[256,256]{1,0:T(8,128)S(1)}, u32[]{:S(2)}, u32[]{:S(2)}) collective-permute-start(f32[256,256]{1,0:T(8,128)S(1)} %get-tuple-element.65.far), channel_id=1, source_target_pairs={{0,4},{1,3},{2,10},{3,1},{4,0},{5,7},{6,14},{7,5},{8,16},{9,11},{1... | collective-permute-start | bytes 786440 | tf_op jit(solution)/shard_map/ppermute | solution.py:407
  39.4 6.7 %collective-permute-start.12 = (f32[256,256]{1,0:T(8,128)S(1)}, f32[256,256]{1,0:T(8,128)S(1)}, u32[]{:S(2)}, u32[]{:S(2)}) collective-permute-start(f32[256,256]{1,0:T(8,128)S(1)} %get-tuple-element.77.far), channel_id=1, source_target_pairs={{0,1},{1,0},{2,3},{3,2},{4,5},{5,4},{6,7},{7,6},{8,9},{9,8},{10,11... | collective-permute-start | bytes 786440 | tf_op jit(solution)/shard_map/ppermute | solution.py:407
  42.2 3.9 %collective-permute-start.11 = (f32[256,256]{1,0:T(8,128)S(1)}, f32[256,256]{1,0:T(8,128)S(1)}, u32[]{:S(2)}, u32[]{:S(2)}) collective-permute-start(f32[256,256]{1,0:T(8,128)S(1)} %get-tuple-element.74.near), channel_id=1, source_target_pairs={{0,1},{1,0},{2,3},{3,2},{4,5},{5,4},{6,7},{7,6},{8,9},{9,8},{10,11... | collective-permute-start | bytes 786440 | tf_op jit(solution)/shard_map/ppermute | solution.py:407
  42.3 6.4 %collective-permute-start.14 = (f32[256,256]{1,0:T(8,128)S(1)}, f32[256,256]{1,0:T(8,128)S(1)}, u32[]{:S(2)}, u32[]{:S(2)}) collective-permute-start(f32[256,256]{1,0:T(8,128)S(1)} %get-tuple-element.77.far), channel_id=1, source_target_pairs={{0,4},{1,3},{2,10},{3,1},{4,0},{5,7},{6,14},{7,5},{8,16},{9,11},{1... | collective-permute-start | bytes 786440 | tf_op jit(solution)/shard_map/ppermute | solution.py:407
  43.4 8.1 %collective-permute-start.10 = (f32[256,256]{1,0:T(8,128)S(1)}, f32[256,256]{1,0:T(8,128)S(1)}, u32[]{:S(2)}, u32[]{:S(2)}) collective-permute-start(f32[256,256]{1,0:T(8,128)S(1)} %get-tuple-element.74.near), channel_id=1, source_target_pairs={{0,4},{1,3},{2,10},{3,1},{4,0},{5,7},{6,14},{7,5},{8,16},{9,11},{1... | collective-permute-start | bytes 786440 | tf_op jit(solution)/shard_map/ppermute | solution.py:407
  52.0 5.2 %collective-permute-start.16 = (f32[256,256]{1,0:T(8,128)S(1)}, f32[256,256]{1,0:T(8,128)S(1)}, u32[]{:S(2)}, u32[]{:S(2)}) collective-permute-start(f32[256,256]{1,0:T(8,128)S(1)} %get-tuple-element.85.near), channel_id=1, source_target_pairs={{0,1},{1,0},{2,3},{3,2},{4,5},{5,4},{6,7},{7,6},{8,9},{9,8},{10,11... | collective-permute-start | bytes 786440 | tf_op jit(solution)/shard_map/ppermute | solution.py:407
  52.5 4.7 %collective-permute-start.17 = (f32[256,256]{1,0:T(8,128)S(1)}, f32[256,256]{1,0:T(8,128)S(1)}, u32[]{:S(2)}, u32[]{:S(2)}) collective-permute-start(f32[256,256]{1,0:T(8,128)S(1)} %get-tuple-element.82.far), channel_id=1, source_target_pairs={{0,1},{1,0},{2,3},{3,2},{4,5},{5,4},{6,7},{7,6},{8,9},{9,8},{10,11... | collective-permute-start | bytes 786440 | tf_op jit(solution)/shard_map/ppermute | solution.py:407
  53.2 6.4 %collective-permute-start.15 = (f32[256,256]{1,0:T(8,128)S(1)}, f32[256,256]{1,0:T(8,128)S(1)}, u32[]{:S(2)}, u32[]{:S(2)}) collective-permute-start(f32[256,256]{1,0:T(8,128)S(1)} %get-tuple-element.85.near), channel_id=1, source_target_pairs={{0,4},{1,3},{2,10},{3,1},{4,0},{5,7},{6,14},{7,5},{8,16},{9,11},{1... | collective-permute-start | bytes 786440 | tf_op jit(solution)/shard_map/ppermute | solution.py:407
  54.3 8.1 %collective-permute-start.13 = (f32[256,256]{1,0:T(8,128)S(1)}, f32[256,256]{1,0:T(8,128)S(1)}, u32[]{:S(2)}, u32[]{:S(2)}) collective-permute-start(f32[256,256]{1,0:T(8,128)S(1)} %get-tuple-element.82.far), channel_id=1, source_target_pairs={{0,4},{1,3},{2,10},{3,1},{4,0},{5,7},{6,14},{7,5},{8,16},{9,11},{1... | collective-permute-start | bytes 786440 | tf_op jit(solution)/shard_map/ppermute | solution.py:407
  62.8 6.4 %collective-permute-start.18 = (f32[256,256]{1,0:T(8,128)S(1)}, f32[256,256]{1,0:T(8,128)S(1)}, u32[]{:S(2)}, u32[]{:S(2)}) collective-permute-start(f32[256,256]{1,0:T(8,128)S(1)} %get-tuple-element.93.first_sent), channel_id=1, source_target_pairs={{0,16},{1,2},{2,6},{3,4},{4,1},{5,3},{6,7},{7,5},{8,14},{9,12},{10... | collective-permute-start | bytes 786440 | tf_op jit(solution)/shard_map/ppermute | solution.py:407
  64.3 7.7 %collective-permute-start.19 = (f32[256,256]{1,0:T(8,128)S(1)}, f32[256,256]{1,0:T(8,128)S(1)}, u32[]{:S(2)}, u32[]{:S(2)}) collective-permute-start(f32[256,256]{1,0:T(8,128)S(1)} %get-tuple-element.94.second_sent), channel_id=1, source_target_pairs={{0,1},{1,3},{2,7},{3,5},{4,0},{5,2},{6,22},{7,4},{8,15},{9,13},{10... | collective-permute-start | bytes 786440 | tf_op jit(solution)/shard_map/ppermute | solution.py:407

commit v3 on v2

--- a/solution.py
+++ b/solution.py
@@ -35,13 +35,33 @@
     return problem, 2 * group + odd, core ^ odd
 
 
+def start_of(device):
+    return device >> 2, (device >> 1) & 1, device & 1, (device >> 3) & 1
+
+
+def targets_of(device):
+    block, half, slot, _ = start_of(device)
+    problem = slot ^ half
+    return device_of(problem ^ 1, block, half), device_of(problem, block, half)
+
+
+def straight(device):
+    block, half, _, parity = start_of(device)
+    return half == ((block & 1) ^ parity)
+
+
 def permutations(count):
     blocks = count // 4
-    first, second, link = [], [], []
+    first, second, rows, columns, link = [], [], [], [], []
     for device in range(count):
-        block, half, slot = device >> 2, (device >> 1) & 1, device & 1
-        first.append((device, device_of(slot, block, half)))
-        second.append((device, device_of(1 - slot, block, half)))
+        block, half, slot, parity = start_of(device)
+        to_first, to_second = targets_of(device)
+        first.append((device, to_first))
+        second.append((device, to_second))
+        idle = device ^ 8 if device ^ 8 < count else device
+        rows.append((device, device ^ 5 if (slot ^ half) != (block & 1) else idle))
+        idle = device ^ 9 if device ^ 9 < count else device
+        columns.append((device, device ^ 2 if slot != parity else idle))
     for problem in range(2):
         for block in range(blocks - 1):
             here, there = device_of(problem, block, 1), device_of(problem, block + 1, 0)
@@ -50,7 +70,7 @@
         here, there = device_of(0, block, pair), device_of(1, block, pair)
         link += [(here, there), (there, here)]
     core = [(device, device ^ 1) for device in range(count)]
-    return full(first), full(second), sorted(link), core
+    return full(first), full(second), rows, columns, sorted(link), core
 
 
 def full(pairs):
@@ -63,8 +83,8 @@
 
 
 def kept(device):
-    block, half, slot = device >> 2, (device >> 1) & 1, device & 1
-    return device_of(slot, block, half) == device, device_of(1 - slot, block, half) == device
+    first, second = targets_of(device)
+    return first == device, second == device
 
 
 def flipped(pairs):
@@ -136,34 +156,41 @@
         body(False)
 
 
-def convert_kernel(state_hbm, occ_hbm, up_hbm, low_hbm, first, second, state, occ, up, low, sems):
+def convert_kernel(which, *refs):
+    inputs, out, held, sems = refs[:6], refs[6], refs[7:13], refs[13]
+    state, occ, up, low, bath, damp = held
     copies = [
-        pltpu.make_async_copy(src, dst, sems.at[index])
-        for index, (src, dst) in enumerate(((state_hbm, state), (occ_hbm, occ), (up_hbm, up), (low_hbm, low)))
+        pltpu.make_async_copy(src, dst, sems.at[index]) for index, (src, dst) in enumerate(zip(inputs, held))
     ]
     for copy in copies:
         copy.start()
     for copy in copies:
         copy.wait()
-    slot = lax.axis_index("aux") & 1
+    _, half, slot, _ = start_of(lax.axis_index("aux"))
+    problem = slot ^ half ^ 1 ^ which
     re, im = state[0, 0], state[0, 1]
     size = re.shape[0]
-    total, diff = re + im, re - im
-    herm = 0.5 * (total + diff.T)
-    anti = 0.5 * (total.T - diff)
-    first[0:size] = jnp.where(slot == 0, herm, anti)
-    second[0:size] = jnp.where(slot == 0, anti, herm)
+
+    @pl.when(problem == 0)
+    def _():
+        out[0:size] = 0.5 * ((re + im) + (re - im).T)
+
+    @pl.when(problem == 1)
+    def _():
+        out[0:size] = 0.5 * ((re + im).T - (re - im))
+
     lane = lax.broadcasted_iota(jnp.int32, (META, size), 1)
     modes = occ.shape[1]
     row = jnp.zeros((META, size), F32)
     for mode in range(modes):
         for place, table in enumerate((occ, up, low)):
             row = jnp.where(lane == place * modes + mode, table[0, mode].astype(F32), row)
-    first[size : size + META] = row
-    second[size : size + META] = row
-
-
-def prepare_kernel(h_static, drive_op, couple, bath_coef, damping, h_a, h_b, h_c, q_out, damp_out):
+        for place, value in enumerate((damp[mode], bath[0, mode], bath[1, mode])):
+            row = jnp.where(lane == (3 + place) * modes + mode, value, row)
+    out[size : size + META] = row
+
+
+def prepare_kernel(h_static, drive_op, couple, h_a, h_b, h_c, q_out):
     h_re = (h_static[0] + h_static[0].T) * 0.5
     h_im = (h_static[1] - h_static[1].T) * 0.5
     v_re = (drive_op[0] + drive_op[0].T) * 0.5
@@ -173,14 +200,12 @@
         store_stack(h_out, 0, h_re + drive * v_re, h_im + drive * v_im)
     for mode in range(couple.shape[0]):
         q_out[mode] = (couple[mode] + couple[mode].T) * 0.5
-        for place, value in enumerate((damping[mode], bath_coef[0, mode], bath_coef[1, mode])):
-            damp_out[3 * mode + place] = jnp.full(damp_out.shape[1:], value, F32)
-
-
-def arrive_kernel(which, array, q_ref, damp, h_ref, *refs):
+
+
+def arrive_kernel(which, array, q_ref, h_ref, *refs):
     weights, base, rate, early = refs[-4:]
     problem, block, pair = role("aux")
-    part = pair ^ problem ^ which
+    part = problem ^ 1 ^ which
     size = q_ref.shape[1]
     modes = q_ref.shape[0]
     meta = array[size : size + 1]
@@ -190,7 +215,7 @@
         return meta[:, column : column + 1]
 
     def constant(place, mode):
-        return damp[3 * mode + place][0:1, 0:1]
+        return entry(3 + place, mode)
 
     total = jnp.zeros((1, 1), F32)
     for mode in range(modes):
@@ -274,19 +299,19 @@
     by_type(pair == 1, body)
 
 
-def pick(one, two, pair, sorted_already):
+def pick(one, two, sorted_already):
     if sorted_already:
         return one[...], two[...]
     problem, _, _ = role("aux")
     size = one.shape[1]
-    near_first = pair == problem
+    near_first = problem == 1
     one, two = one[0:size], two[0:size]
     return jnp.where(near_first, one, two), jnp.where(near_first, two, one)
 
 
 def partner_kernel(sorted_already, one, two, weights, near, far, near_out, far_out):
     _, _, pair = role("aux")
-    x_n, x_f = pick(one, two, 1 - pair, sorted_already)
+    x_n, x_f = pick(one, two, sorted_already)
 
     def body(lower):
         f_n, f_f = forms(x_n, lower), forms(x_f, lower)
@@ -318,30 +343,60 @@
     by_type(pair == 0, body)
 
 
-def first_near_kernel(step, weight, one, two, weights, early, base, out, acc_out):
-    _, _, pair = role("aux")
-    x_n, x_f = pick(one, two, 1 - pair, False)
-
-    def body(lower):
-        m_a, p_a = products(weights.at[N_LINK_N], forms(x_n, lower))
-        m_b, p_b = products(weights.at[N_LINK_F], forms(x_f, lower))
-        slope = early[...] + m_a + m_b + (p_a + p_b).T
+def sent_far(which):
+    problem, _, _ = role("aux")
+    return problem ^ 1 ^ which
+
+
+def first_part_kernel(array, weights, near, far, near_out, far_out):
+    _, _, pair = role("aux")
+    is_far = sent_far(0)
+
+    def body(lower):
+        source = forms(array[0 : array.shape[1]], lower)
+        near_out[...] = near[...] + term(weights, N_LINK_N + is_far, source)
+
+        @pl.when(is_far == 0)
+        def _():
+            far_out[...] = far[...] + term(weights, F_LINK_N, source)
+
+        @pl.when(is_far == 1)
+        def _():
+            far_out[...] = far[...]
+
+    by_type(pair == 0, body)
+
+
+def first_near_kernel(step, weight, array, weights, early, base, out, acc_out):
+    _, _, pair = role("aux")
+
+    def body(lower):
+        source = forms(array[0 : array.shape[1]], lower)
+        slope = early[...] + term(weights, N_LINK_N + sent_far(1), source)
         out[...] = base[0] + step * slope
         acc_out[...] = base[0] + weight * slope
 
     by_type(pair == 0, body)
 
 
-def first_far_kernel(step, weight, one, two, weights, early, base, out, acc_out):
-    _, _, pair = role("aux")
-    x_n, _ = pick(one, two, 1 - pair, False)
-
-    def body(lower):
-        slope = early[...] + term(weights, F_LINK_N, forms(x_n, lower))
+def first_far_kernel(step, weight, array, weights, early, base, out, acc_out):
+    _, _, pair = role("aux")
+    is_far = sent_far(1)
+
+    def store(slope):
         out[...] = base[1] + step * slope
         acc_out[...] = base[1] + weight * slope
 
-    by_type(pair == 0, body)
+    def body(lower):
+        @pl.when(is_far == 0)
+        def _():
+            store(early[...] + term(weights, F_LINK_N, forms(array[0 : array.shape[1]], lower)))
+
+    by_type(pair == 0, body)
+
+    @pl.when(is_far == 1)
+    def _():
+        store(early[...])
 
 
 def last_far_kernel(weight, source, weights, early, acc, out):
@@ -355,7 +410,7 @@
 
 def last_near_kernel(weight, source, weights, early, acc, far, first, second):
     problem, _, pair = role("aux")
-    near_first = pair == problem
+    near_first = problem == 1
 
     def body(lower):
         near = acc[...] + weight * (early[...] + term(weights, N_LINK_F, forms(source[...], lower)))
@@ -365,21 +420,26 @@
     by_type(pair == 0, body)
 
 
-def restore_kernel(first, second, first_sent, second_sent, out):
+def restore_kernel(first, second, first_sent, second_sent, out_hbm, out, sems):
     device = lax.axis_index("aux")
-    slot = device & 1
+    _, half, slot, _ = start_of(device)
     keep_first, keep_second = kept(device)
     one = jnp.where(keep_first, first_sent[...], first[...])
     two = jnp.where(keep_second, second_sent[...], second[...])
-    herm = jnp.where(slot == 0, one, two)
-    anti = jnp.where(slot == 0, two, one)
+    herm = jnp.where(slot == half, two, one)
+    anti = jnp.where(slot == half, one, two)
     total = herm + anti.T
     diff = herm.T - anti
-    out[0, 0] = 0.5 * (total + diff)
-    out[0, 1] = 0.5 * (total - diff)
-
-
-def call(kernel, out_shapes, args, smem=(), flops=0, space=None, scratch=(), grant=32, aliases=None):
+    copies = []
+    for half, value in enumerate((total + diff, total - diff)):
+        out[0, half] = 0.5 * value
+        copies.append(pltpu.make_async_copy(out.at[0, half], out_hbm.at[0, half], sems.at[half]))
+        copies[-1].start()
+    for copy in copies:
+        copy.wait()
+
+
+def call(kernel, out_shapes, args, smem=(), flops=0, space=None, scratch=(), grant=32, aliases=None, out_space=None):
     shapes = [jax.ShapeDtypeStruct(shape, dtype) for shape, dtype in out_shapes]
     moved = sum(math.prod(a.shape) * a.dtype.itemsize for a in list(args) + shapes)
     single = len(shapes) == 1
@@ -387,7 +447,7 @@
         kernel,
         out_shape=shapes[0] if single else shapes,
         in_specs=[space or (SMEM if index in smem else VMEM) for index in range(len(args))],
-        out_specs=VMEM if single else [VMEM] * len(shapes),
+        out_specs=(out_space or VMEM) if single else [VMEM] * len(shapes),
         scratch_shapes=scratch,
         input_output_aliases=aliases or {},
         cost_estimate=pl.CostEstimate(flops=flops, bytes_accessed=moved, transcendentals=0),
@@ -399,7 +459,7 @@
     count = lax.axis_size("aux")
     size = state.shape[-1]
     modes = couple.shape[0]
-    first_to, second_to, link_to, core_to = permutations(count)
+    first_to, second_to, rows_to, columns_to, link_to, core_to = permutations(count)
     pair_shape = (2, size, size)
     unit = 2 * size**3
 
@@ -407,38 +467,43 @@
         return lax.ppermute(value, "aux", pairs)
 
     tall = ((size + META, size), F32)
-    tables = [occupation, raise_nbr, lower_nbr]
-    first, second = call(
-        convert_kernel,
-        [tall, tall],
-        [state] + tables,
-        space=pl.BlockSpec(memory_space=pltpu.HBM),
-        grant=60,
-        scratch=[pltpu.VMEM(state.shape, F32)]
-        + [pltpu.SMEM(table.shape, jnp.int32) for table in tables]
-        + [pltpu.SemaphoreType.DMA((4,))],
-    )
-    keep_first, keep_second = kept(lax.axis_index("aux"))
+    tables = [occupation, raise_nbr, lower_nbr, bath_coef, damping]
+    first, second = (
+        call(
+            partial(convert_kernel, which),
+            [tall],
+            [state] + tables,
+            space=pl.BlockSpec(memory_space=pltpu.HBM),
+            grant=60,
+            scratch=[pltpu.VMEM(state.shape, F32)]
+            + [pltpu.SMEM(table.shape, table.dtype) for table in tables]
+            + [pltpu.SemaphoreType.DMA((1 + len(tables),))],
+        )
+        for which in range(2)
+    )
+    device = lax.axis_index("aux")
+    _, _, slot, parity = start_of(device)
+    keep_first, _ = kept(device)
+    crossed = send(second, rows_to)
     first = jnp.where(keep_first, first, send(first, first_to))
-    second = jnp.where(keep_second, second, send(second, second_to))
-    *h_now, q_all, damp = call(
-        prepare_kernel,
-        [((1, 6 * size, size), BF16)] * 3 + [((modes, size, size), F32), ((3 * modes, 8, 128), F32)],
-        [h_static, drive_op, couple, bath_coef, damping],
-        smem=(3, 4),
+    is_straight = straight(device)
+    turned = send(jnp.where(is_straight, crossed, second), columns_to)
+    second = jnp.where(slot == parity, jnp.where(is_straight, second, crossed), turned)
+    *h_now, q_all = call(
+        prepare_kernel, [((1, 6 * size, size), BF16)] * 3 + [((modes, size, size), F32)], [h_static, drive_op, couple]
     )
     flat = ((size, size), F32)
 
     held = [((8, 6 * size, size), BF16), (pair_shape, F32), ((2, 8, 128), F32), (pair_shape, F32)]
-    state_now = call(partial(arrive_kernel, 0), held, [first, q_all, damp, h_now[0]], flops=9 * unit)
+    state_now = call(partial(arrive_kernel, 0), held, [first, q_all, h_now[0]], flops=9 * unit)
     link = [send(first, link_to)]
     partner = [send(first, core_to)]
     weights, base, rate, early = call(
         partial(arrive_kernel, 1),
         held,
-        [second, q_all, damp, h_now[0], *state_now],
+        [second, q_all, h_now[0], *state_now],
         flops=9 * unit,
-        aliases={4 + index: index for index in range(4)},
+        aliases={3 + index: index for index in range(4)},
     )
     link.append(send(second, link_to))
     partner.append(send(second, core_to))
@@ -467,11 +532,12 @@
         )
 
     near_e, far_e = with_partner(0, near_e, far_e)
+    near_e, far_e = call(first_part_kernel, [flat, flat], [link[0], weights, near_e, far_e], flops=18 * unit)
     near, near_acc = call(
-        partial(first_near_kernel, steps[0], shares[0]), [flat, flat], [*link, weights, near_e, base], flops=18 * unit
+        partial(first_near_kernel, steps[0], shares[0]), [flat, flat], [link[1], weights, near_e, base], flops=9 * unit
     )
     far, far_acc = call(
-        partial(first_far_kernel, steps[0], shares[0]), [flat, flat], [*link, weights, far_e, base], flops=9 * unit
+        partial(first_far_kernel, steps[0], shares[0]), [flat, flat], [link[1], weights, far_e, base], flops=9 * unit
     )
     link_n, link_f = send(near, link_to), send(far, link_to)
     partner = [send(near, core_to), send(far, core_to)]
@@ -495,7 +561,13 @@
         partial(last_near_kernel, shares[3]), [flat, flat], [link_f, weights, near_e, near_acc, far], flops=9 * unit
     )
     back = [send(first, flipped(first_to)), send(second, flipped(second_to)), first, second]
-    return call(restore_kernel, [((1, 2, size, size), F32)], back)
+    return call(
+        restore_kernel,
+        [(state.shape, F32)],
+        back,
+        out_space=pl.BlockSpec(memory_space=pltpu.HBM),
+        scratch=[pltpu.VMEM(state.shape, F32), pltpu.SemaphoreType.DMA((2,))],
+    )
 
 
 def solution(mesh):

time: 74.4 us -> 75.5 us (1.015)
  the two profiles are of different devices: /device:TPU:8 before, /device:TPU:9 now
where the time goes in v3:
time: 75.5 us; the launch traced here: 75.2 us
  waiting for transfers between devices  27.8 us (37%)
  Pallas kernels  24.9 us (33%)
  starting transfers between devices  17.7 us (23%)
  local copies, waits for them, and re-layouts  3.21 us (4%)
  other arithmetic  1.09 us (1%)
    ppermute x21, waiting for transfers between devices, send(): return lax.ppermute(value, 'aux', pairs)  27.8 us
    pallas_call x26, Pallas kernels, call(): pl.pallas_call(kernel, out_shape=shapes[0] if single else shapes, in_spec...  24.9 us
    ppermute x21, starting transfers between devices, send(): return lax.ppermute(value, 'aux', pairs)  17.7 us
    unnamed x6, local copies, waits for them, and re-layouts  3.21 us
  transfers between devices with their start and end apart: 21, of which 11 were waited for; matrix products, arithmetic and copies ran while one was open for 1% of the time, Pallas kernels for 27%

profile of v3, /device:TPU:9, one launch (start us, length us, event | category | flops | bytes accessed | tf_op | source)
XLA Modules:
  0.0 75.2 jit_solution(14603454147024241276)
XLA Ops:
  0.0 2.0 %shard_map.91 = f32[264,256]{1,0:T(8,128)} custom-call(f32[1,2,256,256]{3,2,1,0:T(8,128)} %refs_0_.3, s32[1,3]{1,0:T(1,128)} %refs_1_.3, s32[1,3]{1,0:T(1,128)} %refs_2_.3, s32[1,3]{1,0:T(1,128)} %refs_3_.3, f32[2,3]{1,0:T(2,128)} %refs_4_.3, f32[3]{0:T(128)} %refs_5_.3), custom_call_target="tpu_custom_call" | custom-call | bytes 794696 | tf_op jit(solution)/shard_map/pallas_call | solution.py:446
  2.0 1.9 %collective-permute-start = (f32[264,256]{1,0:T(8,128)}, f32[264,256]{1,0:T(8,128)S(1)}, u32[]{:S(2)}, u32[]{:S(2)}) collective-permute-start(f32[264,256]{1,0:T(8,128)} %shard_map.91), channel_id=1, source_target_pairs={{0,8},{1,4},{2,7},{3,11},{4,1},{5,13},{6,14},{7,2},{8,0},{9,12},{1... | collective-permute-start | bytes 811016 | tf_op jit(solution)/shard_map/ppermute | solution.py:467
  3.9 2.0 %shard_map.93 = f32[264,256]{1,0:T(8,128)} custom-call(f32[1,2,256,256]{3,2,1,0:T(8,128)} %refs_0_.3, s32[1,3]{1,0:T(1,128)} %refs_1_.3, s32[1,3]{1,0:T(1,128)} %refs_2_.3, s32[1,3]{1,0:T(1,128)} %refs_3_.3, f32[2,3]{1,0:T(2,128)} %refs_4_.3, f32[3]{0:T(128)} %refs_5_.3), custom_call_target="tpu_custom_call" | custom-call | bytes 794696 | tf_op jit(solution)/shard_map/pallas_call | solution.py:446
  5.9 1.0 %collective-permute-start.3 = (f32[264,256]{1,0:T(8,128)}, f32[264,256]{1,0:T(8,128)S(1)}, u32[]{:S(2)}, u32[]{:S(2)}) collective-permute-start(f32[264,256]{1,0:T(8,128)} %shard_map.93), channel_id=1, source_target_pairs={{0,4},{1,0},{2,1},{3,5},{4,7},{5,3},{6,2},{7,6},{8,14},{9,10},{10,... | collective-permute-start | bytes 811016 | tf_op jit(solution)/shard_map/ppermute | solution.py:467
  6.9 1.6 %collective-permute-done = f32[264,256]{1,0:T(8,128)S(1)} collective-permute-done((f32[264,256]{1,0:T(8,128)}, f32[264,256]{1,0:T(8,128)S(1)}, u32[]{:S(2)}, u32[]{:S(2)}) %collective-permute-start) | collective-permute-done | bytes 270368 | tf_op jit(solution)/shard_map/ppermute | solution.py:467
  8.5 1.0 %broadcast_select_fusion.1 = f32[264,256]{1,0:T(8,128)S(1)} fusion(f32[264,256]{1,0:T(8,128)S(1)} %collective-permute-done, f32[264,256]{1,0:T(8,128)} %shard_map.91, pred[]{:T(512)S(6)} %eq.10), kind=kLoop, calls=%fused_computation.2 | loop fusion | flops 67584 | bytes 811009 | tf_op jit(solution)/shard_map/jit(_where)/select_n | solution.py:490
  9.6 5.0 %collective-permute-done.3 = f32[264,256]{1,0:T(8,128)S(1)} collective-permute-done((f32[264,256]{1,0:T(8,128)}, f32[264,256]{1,0:T(8,128)S(1)}, u32[]{:S(2)}, u32[]{:S(2)}) %collective-permute-start.3) | collective-permute-done | bytes 270368 | tf_op jit(solution)/shard_map/ppermute | solution.py:467
  15.8 1.2 %collective-permute-start.6 = (f32[264,256]{1,0:T(8,128)S(1)}, f32[264,256]{1,0:T(8,128)S(1)}, u32[]{:S(2)}, u32[]{:S(2)}) collective-permute-start(f32[264,256]{1,0:T(8,128)S(1)} %select_select_fusion.array), channel_id=1, source_target_pairs={{0,1},{1,0},{2,3},{3,2},{4,5},{5,4},{6,7},{7,6},{8,9},{9,8},{10,11... | collective-permute-start | bytes 811016 | tf_op jit(solution)/shard_map/ppermute | solution.py:467
  17.1 2.9 %collective-permute-start.4 = (f32[264,256]{1,0:T(8,128)S(1)}, f32[264,256]{1,0:T(8,128)S(1)}, u32[]{:S(2)}, u32[]{:S(2)}) collective-permute-start(f32[264,256]{1,0:T(8,128)S(1)} %broadcast_select_fusion.array), channel_id=1, source_target_pairs={{0,4},{1,3},{2,10},{3,1},{4,0},{5,7},{6,14},{7,5},{8,16},{9,11},{1... | collective-permute-start | bytes 811016 | tf_op jit(solution)/shard_map/ppermute | solution.py:467
  20.0 1.1 %copy-done = f32[3,256,256]{2,1,0:T(8,128)S(1)} copy-done((f32[3,256,256]{2,1,0:T(8,128)S(1)}, f32[3,256,256]{2,1,0:T(8,128)}, u32[]{:S(2)}) %copy-start) | copy-done | bytes 786456
  21.1 1.0 %copy-done.1 = f32[2,256,256]{2,1,0:T(8,128)S(1)} copy-done((f32[2,256,256]{2,1,0:T(8,128)S(1)}, f32[2,256,256]{2,1,0:T(8,128)}, u32[]{:S(2)}) %copy-start.1) | copy-done | bytes 524312
  22.2 1.0 %copy-done.2 = f32[2,256,256]{2,1,0:T(8,128)S(1)} copy-done((f32[2,256,256]{2,1,0:T(8,128)S(1)}, f32[2,256,256]{2,1,0:T(8,128)}, u32[]{:S(2)}) %copy-start.2) | copy-done | bytes 524312
  24.1 1.1 %shard_map.94 = (bf16[8,1536,256]{2,1,0:T(8,128)(2,1)S(1)}, f32[2,256,256]{2,1,0:T(8,128)S(1)}, f32[2,8,128]{2,1,0:T(8,128)S(1)}, f32[2,256,256]{2,1,0:T(8,128)S(1)}) custom-call(f32[264,256]{1,0:T(8,128)S(1)} %broadcast_select_fusion.array, f32[3,256,256]{2,1,0:T(8,128)S(1)} %get-tuple-element.49.q_ref, bf16[1,1536,256]{2,1,0:T(8,128)(2,1)S(1)} %get-tuple-element.50.h_ref), custom_call_target="tpu_custom_call" | custom-call | flops 301989888 | bytes 9191424 | tf_op jit(solution)/shard_map/pallas_call | solution.py:446
  25.2 1.0 %shard_map.95 = (bf16[8,1536,256]{2,1,0:T(8,128)(2,1)S(1)}, f32[2,256,256]{2,1,0:T(8,128)S(1)}, f32[2,8,128]{2,1,0:T(8,128)S(1)}, f32[2,256,256]{2,1,0:T(8,128)S(1)}) custom-call(f32[264,256]{1,0:T(8,128)S(1)} %select_select_fusion.array, ...), custom_call_target="tpu_custom_call", output_to_operand_aliasing={{0}: (3, {}), {1}: (4, {}), {2}: (5, {}), {3}: (6, {})} | custom-call | flops 301989888 | bytes 16539648 | tf_op jit(solution)/shard_map/pallas_call | solution.py:446
  29.2 1.1 %collective-permute-start.9 = (f32[256,256]{1,0:T(8,128)S(1)}, f32[256,256]{1,0:T(8,128)S(1)}, u32[]{:S(2)}, u32[]{:S(2)}) collective-permute-start(f32[256,256]{1,0:T(8,128)S(1)} %get-tuple-element.65.near), channel_id=1, source_target_pairs={{0,1},{1,0},{2,3},{3,2},{4,5},{5,4},{6,7},{7,6},{8,9},{9,8},{10,11... | collective-permute-start | bytes 786440 | tf_op jit(solution)/shard_map/ppermute | solution.py:467
  30.9 1.1 %collective-permute-start.8 = (f32[256,256]{1,0:T(8,128)S(1)}, f32[256,256]{1,0:T(8,128)S(1)}, u32[]{:S(2)}, u32[]{:S(2)}) collective-permute-start(f32[256,256]{1,0:T(8,128)S(1)} %get-tuple-element.65.near), channel_id=1, source_target_pairs={{0,4},{1,3},{2,10},{3,1},{4,0},{5,7},{6,14},{7,5},{8,16},{9,11},{1... | collective-permute-start | bytes 786440 | tf_op jit(solution)/shard_map/ppermute | solution.py:467
  32.4 1.8 %shard_map.101 = (f32[256,256]{1,0:T(8,128)S(1)}, f32[256,256]{1,0:T(8,128)S(1)}) custom-call(f32[256,256]{1,0:T(8,128)S(1)} %get-tuple-element.65.near, f32[256,256]{1,0:T(8,128)S(1)} %get-tuple-element.63.far, bf16[1,1536,256]{2,1,0:T(8,128)(2,1)S(1)} %get-tuple-element.66.h_ref, bf16[8,1536,256]{2,1,0:T(8,128)(2,1)S(1)} %get-tuple-element.55.weights, ...), custom_call_target="tpu_custom_call" | custom-call | flops 1107296256 | bytes 8134656 | tf_op jit(solution)/shard_map/pallas_call | solution.py:446
  35.2 1.3 %collective-permute-done.8.source = f32[256,256]{1,0:T(8,128)S(1)} collective-permute-done((f32[256,256]{1,0:T(8,128)S(1)}, f32[256,256]{1,0:T(8,128)S(1)}, u32[]{:S(2)}, u32[]{:S(2)}) %collective-permute-start.8) | collective-permute-done | bytes 262176 | tf_op jit(solution)/shard_map/ppermute | solution.py:467
  37.1 1.2 %collective-permute-start.13 = (f32[256,256]{1,0:T(8,128)S(1)}, f32[256,256]{1,0:T(8,128)S(1)}, u32[]{:S(2)}, u32[]{:S(2)}) collective-permute-start(f32[256,256]{1,0:T(8,128)S(1)} %get-tuple-element.75.far), channel_id=1, source_target_pairs={{0,1},{1,0},{2,3},{3,2},{4,5},{5,4},{6,7},{7,6},{8,9},{9,8},{10,11... | collective-permute-start | bytes 786440 | tf_op jit(solution)/shard_map/ppermute | solution.py:467
  39.9 1.2 %collective-permute-start.12 = (f32[256,256]{1,0:T(8,128)S(1)}, f32[256,256]{1,0:T(8,128)S(1)}, u32[]{:S(2)}, u32[]{:S(2)}) collective-permute-start(f32[256,256]{1,0:T(8,128)S(1)} %get-tuple-element.72.near), channel_id=1, source_target_pairs={{0,1},{1,0},{2,3},{3,2},{4,5},{5,4},{6,7},{7,6},{8,9},{9,8},{10,11... | collective-permute-start | bytes 786440 | tf_op jit(solution)/shard_map/ppermute | solution.py:467
  41.1 1.1 %collective-permute-start.15 = (f32[256,256]{1,0:T(8,128)S(1)}, f32[256,256]{1,0:T(8,128)S(1)}, u32[]{:S(2)}, u32[]{:S(2)}) collective-permute-start(f32[256,256]{1,0:T(8,128)S(1)} %get-tuple-element.75.far), channel_id=1, source_target_pairs={{0,4},{1,3},{2,10},{3,1},{4,0},{5,7},{6,14},{7,5},{8,16},{9,11},{1... | collective-permute-start | bytes 786440 | tf_op jit(solution)/shard_map/ppermute | solution.py:467
  42.6 1.7 %shard_map.106 = (f32[256,256]{1,0:T(8,128)S(1)}, f32[256,256]{1,0:T(8,128)S(1)}) custom-call(f32[256,256]{1,0:T(8,128)S(1)} %get-tuple-element.72.near, f32[256,256]{1,0:T(8,128)S(1)} %get-tuple-element.75.far, bf16[1,1536,256]{2,1,0:T(8,128)(2,1)S(1)} %get-tuple-element.66.h_ref, bf16[8,1536,256]{2,1,0:T(8,128)(2,1)S(1)} %get-tuple-element.55.weights, ...), custom_call_target="tpu_custom_call" | custom-call | flops 1107296256 | bytes 8134656 | tf_op jit(solution)/shard_map/pallas_call | solution.py:446
  45.2 1.4 %collective-permute-done.15.source = f32[256,256]{1,0:T(8,128)S(1)} collective-permute-done((f32[256,256]{1,0:T(8,128)S(1)}, f32[256,256]{1,0:T(8,128)S(1)}, u32[]{:S(2)}, u32[]{:S(2)}) %collective-permute-start.15) | collective-permute-done | bytes 262176 | tf_op jit(solution)/shard_map/ppermute | solution.py:467
  47.2 2.2 %collective-permute-done.11.source = f32[256,256]{1,0:T(8,128)S(1)} collective-permute-done((f32[256,256]{1,0:T(8,128)S(1)}, f32[256,256]{1,0:T(8,128)S(1)}, u32[]{:S(2)}, u32[]{:S(2)}) %collective-permute-start.11) | collective-permute-done | bytes 262176 | tf_op jit(solution)/shard_map/ppermute | solution.py:467
  51.6 1.2 %collective-permute-start.16 = (f32[256,256]{1,0:T(8,128)S(1)}, f32[256,256]{1,0:T(8,128)S(1)}, u32[]{:S(2)}, u32[]{:S(2)}) collective-permute-start(f32[256,256]{1,0:T(8,128)S(1)} %get-tuple-element.83.near), channel_id=1, source_target_pairs={{0,4},{1,3},{2,10},{3,1},{4,0},{5,7},{6,14},{7,5},{8,16},{9,11},{1... | collective-permute-start | bytes 786440 | tf_op jit(solution)/shard_map/ppermute | solution.py:467
  53.1 1.9 %shard_map.111 = (f32[256,256]{1,0:T(8,128)S(1)}, f32[256,256]{1,0:T(8,128)S(1)}) custom-call(f32[256,256]{1,0:T(8,128)S(1)} %get-tuple-element.83.near, f32[256,256]{1,0:T(8,128)S(1)} %get-tuple-element.80.far, bf16[1,1536,256]{2,1,0:T(8,128)(2,1)S(1)} %get-tuple-element.84.h_ref, bf16[8,1536,256]{2,1,0:T(8,128)(2,1)S(1)} %get-tuple-element.55.weights, ...), custom_call_target="tpu_custom_call" | custom-call | flops 1107296256 | bytes 8134656 | tf_op jit(solution)/shard_map/pallas_call | solution.py:446
  55.9 1.2 %collective-permute-done.16.source = f32[256,256]{1,0:T(8,128)S(1)} collective-permute-done((f32[256,256]{1,0:T(8,128)S(1)}, f32[256,256]{1,0:T(8,128)S(1)}, u32[]{:S(2)}, u32[]{:S(2)}) %collective-permute-start.16) | collective-permute-done | bytes 262176 | tf_op jit(solution)/shard_map/ppermute | solution.py:467
  58.3 1.6 %collective-permute-done.14.source = f32[256,256]{1,0:T(8,128)S(1)} collective-permute-done((f32[256,256]{1,0:T(8,128)S(1)}, f32[256,256]{1,0:T(8,128)S(1)}, u32[]{:S(2)}, u32[]{:S(2)}) %collective-permute-start.14) | collective-permute-done | bytes 262176 | tf_op jit(solution)/shard_map/ppermute | solution.py:467
  60.8 1.1 %collective-permute-start.20 = (f32[256,256]{1,0:T(8,128)S(1)}, f32[256,256]{1,0:T(8,128)S(1)}, u32[]{:S(2)}, u32[]{:S(2)}) collective-permute-start(f32[256,256]{1,0:T(8,128)S(1)} %get-tuple-element.92.second_sent), channel_id=1, source_target_pairs={{0,11},{1,3},{2,7},{3,4},{4,1},{5,2},{6,13},{7,5},{8,15},{9,12},{1... | collective-permute-start | bytes 786440 | tf_op jit(solution)/shard_map/ppermute | solution.py:467
  61.9 5.4 %collective-permute-done.19.first = f32[256,256]{1,0:T(8,128)S(1)} collective-permute-done((f32[256,256]{1,0:T(8,128)S(1)}, f32[256,256]{1,0:T(8,128)S(1)}, u32[]{:S(2)}, u32[]{:S(2)}) %collective-permute-start.19) | collective-permute-done | bytes 262176 | tf_op jit(solution)/shard_map/ppermute | solution.py:467
  67.2 6.7 %collective-permute-done.20.second = f32[256,256]{1,0:T(8,128)S(1)} collective-permute-done((f32[256,256]{1,0:T(8,128)S(1)}, f32[256,256]{1,0:T(8,128)S(1)}, u32[]{:S(2)}, u32[]{:S(2)}) %collective-permute-start.20) | collective-permute-done | bytes 262176 | tf_op jit(solution)/shard_map/ppermute | solution.py:467
  73.9 1.0 %shard_map.116 = f32[1,2,256,256]{3,2,1,0:T(8,128)} custom-call(f32[256,256]{1,0:T(8,128)S(1)} %collective-permute-done.19.first, f32[256,256]{1,0:T(8,128)S(1)} %collective-permute-done.20.second, f32[256,256]{1,0:T(8,128)S(1)} %get-tuple-element.91.first_sent, f32[256,256]{1,0:T(8,128)S(1)} %get-tuple-element.92.second_sent), custom_call_target="tpu_custom_call" | custom-call | bytes 1572864 | tf_op jit(solution)/shard_map/pallas_call | solution.py:446
  (45 shorter events, 16.3 us)
Async XLA Ops:
  2.0 6.5 %collective-permute-start = (f32[264,256]{1,0:T(8,128)}, f32[264,256]{1,0:T(8,128)S(1)}, u32[]{:S(2)}, u32[]{:S(2)}) collective-permute-start(f32[264,256]{1,0:T(8,128)} %shard_map.91), channel_id=1, source_target_pairs={{0,8},{1,4},{2,7},{3,11},{4,1},{5,13},{6,14},{7,2},{8,0},{9,12},{1... | collective-permute-start | bytes 811016 | tf_op jit(solution)/shard_map/ppermute | solution.py:467
  5.9 8.8 %collective-permute-start.3 = (f32[264,256]{1,0:T(8,128)}, f32[264,256]{1,0:T(8,128)S(1)}, u32[]{:S(2)}, u32[]{:S(2)}) collective-permute-start(f32[264,256]{1,0:T(8,128)} %shard_map.93), channel_id=1, source_target_pairs={{0,4},{1,0},{2,1},{3,5},{4,7},{5,3},{6,2},{7,6},{8,14},{9,10},{10,... | collective-permute-start | bytes 811016 | tf_op jit(solution)/shard_map/ppermute | solution.py:467
  9.5 6.2 %collective-permute-start.1 = (f32[264,256]{1,0:T(8,128)S(1)}, f32[264,256]{1,0:T(8,128)S(1)}, u32[]{:S(2)}, u32[]{:S(2)}) collective-permute-start(f32[264,256]{1,0:T(8,128)S(1)} %broadcast_select_fusion.1), channel_id=1, source_target_pairs={{0,9},{1,3},{2,11},{3,1},{4,13},{5,7},{6,15},{7,5},{8,10},{9,0},{1... | collective-permute-start | bytes 811016 | tf_op jit(solution)/shard_map/ppermute | solution.py:467
  14.7 12.3 %collective-permute-start.5 = (f32[264,256]{1,0:T(8,128)S(1)}, f32[264,256]{1,0:T(8,128)S(1)}, u32[]{:S(2)}, u32[]{:S(2)}) collective-permute-start(f32[264,256]{1,0:T(8,128)S(1)} %broadcast_select_fusion.array), channel_id=1, source_target_pairs={{0,1},{1,0},{2,3},{3,2},{4,5},{5,4},{6,7},{7,6},{8,9},{9,8},{10,11... | collective-permute-start | bytes 811016 | tf_op jit(solution)/shard_map/ppermute | solution.py:467
  15.8 11.2 %collective-permute-start.6 = (f32[264,256]{1,0:T(8,128)S(1)}, f32[264,256]{1,0:T(8,128)S(1)}, u32[]{:S(2)}, u32[]{:S(2)}) collective-permute-start(f32[264,256]{1,0:T(8,128)S(1)} %select_select_fusion.array), channel_id=1, source_target_pairs={{0,1},{1,0},{2,3},{3,2},{4,5},{5,4},{6,7},{7,6},{8,9},{9,8},{10,11... | collective-permute-start | bytes 811016 | tf_op jit(solution)/shard_map/ppermute | solution.py:467
  17.1 10.9 %collective-permute-start.4 = (f32[264,256]{1,0:T(8,128)S(1)}, f32[264,256]{1,0:T(8,128)S(1)}, u32[]{:S(2)}, u32[]{:S(2)}) collective-permute-start(f32[264,256]{1,0:T(8,128)S(1)} %broadcast_select_fusion.array), channel_id=1, source_target_pairs={{0,4},{1,3},{2,10},{3,1},{4,0},{5,7},{6,14},{7,5},{8,16},{9,11},{1... | collective-permute-start | bytes 811016 | tf_op jit(solution)/shard_map/ppermute | solution.py:467
  20.0 8.6 %collective-permute-start.2 = (f32[264,256]{1,0:T(8,128)S(1)}, f32[264,256]{1,0:T(8,128)S(1)}, u32[]{:S(2)}, u32[]{:S(2)}) collective-permute-start(f32[264,256]{1,0:T(8,128)S(1)} %select_select_fusion.array), channel_id=1, source_target_pairs={{0,4},{1,3},{2,10},{3,1},{4,0},{5,7},{6,14},{7,5},{8,16},{9,11},{1... | collective-permute-start | bytes 811016 | tf_op jit(solution)/shard_map/ppermute | solution.py:467
  20.0 1.1 %copy-start = (f32[3,256,256]{2,1,0:T(8,128)S(1)}, f32[3,256,256]{2,1,0:T(8,128)}, u32[]{:S(2)}) copy-start(f32[3,256,256]{2,1,0:T(8,128)} %couple.1) | copy-start | bytes 2359300
  21.1 1.0 %copy-start.1 = (f32[2,256,256]{2,1,0:T(8,128)S(1)}, f32[2,256,256]{2,1,0:T(8,128)}, u32[]{:S(2)}) copy-start(f32[2,256,256]{2,1,0:T(8,128)} %h_static.1) | copy-start | bytes 1572868
  22.2 1.0 %copy-start.2 = (f32[2,256,256]{2,1,0:T(8,128)S(1)}, f32[2,256,256]{2,1,0:T(8,128)}, u32[]{:S(2)}) copy-start(f32[2,256,256]{2,1,0:T(8,128)} %drive_op.1) | copy-start | bytes 1572868
  29.2 5.1 %collective-permute-start.9 = (f32[256,256]{1,0:T(8,128)S(1)}, f32[256,256]{1,0:T(8,128)S(1)}, u32[]{:S(2)}, u32[]{:S(2)}) collective-permute-start(f32[256,256]{1,0:T(8,128)S(1)} %get-tuple-element.65.near), channel_id=1, source_target_pairs={{0,1},{1,0},{2,3},{3,2},{4,5},{5,4},{6,7},{7,6},{8,9},{9,8},{10,11... | collective-permute-start | bytes 786440 | tf_op jit(solution)/shard_map/ppermute | solution.py:467
  30.8 3.5 %collective-permute-start.10 = (f32[256,256]{1,0:T(8,128)S(1)}, f32[256,256]{1,0:T(8,128)S(1)}, u32[]{:S(2)}, u32[]{:S(2)}) collective-permute-start(f32[256,256]{1,0:T(8,128)S(1)} %get-tuple-element.63.far), channel_id=1, source_target_pairs={{0,1},{1,0},{2,3},{3,2},{4,5},{5,4},{6,7},{7,6},{8,9},{9,8},{10,11... | collective-permute-start | bytes 786440 | tf_op jit(solution)/shard_map/ppermute | solution.py:467
  30.9 5.6 %collective-permute-start.8 = (f32[256,256]{1,0:T(8,128)S(1)}, f32[256,256]{1,0:T(8,128)S(1)}, u32[]{:S(2)}, u32[]{:S(2)}) collective-permute-start(f32[256,256]{1,0:T(8,128)S(1)} %get-tuple-element.65.near), channel_id=1, source_target_pairs={{0,4},{1,3},{2,10},{3,1},{4,0},{5,7},{6,14},{7,5},{8,16},{9,11},{1... | collective-permute-start | bytes 786440 | tf_op jit(solution)/shard_map/ppermute | solution.py:467
  32.0 7.3 %collective-permute-start.7 = (f32[256,256]{1,0:T(8,128)S(1)}, f32[256,256]{1,0:T(8,128)S(1)}, u32[]{:S(2)}, u32[]{:S(2)}) collective-permute-start(f32[256,256]{1,0:T(8,128)S(1)} %get-tuple-element.63.far), channel_id=1, source_target_pairs={{0,4},{1,3},{2,10},{3,1},{4,0},{5,7},{6,14},{7,5},{8,16},{9,11},{1... | collective-permute-start | bytes 786440 | tf_op jit(solution)/shard_map/ppermute | solution.py:467
  37.1 7.2 %collective-permute-start.13 = (f32[256,256]{1,0:T(8,128)S(1)}, f32[256,256]{1,0:T(8,128)S(1)}, u32[]{:S(2)}, u32[]{:S(2)}) collective-permute-start(f32[256,256]{1,0:T(8,128)S(1)} %get-tuple-element.75.far), channel_id=1, source_target_pairs={{0,1},{1,0},{2,3},{3,2},{4,5},{5,4},{6,7},{7,6},{8,9},{9,8},{10,11... | collective-permute-start | bytes 786440 | tf_op jit(solution)/shard_map/ppermute | solution.py:467
  39.9 4.4 %collective-permute-start.12 = (f32[256,256]{1,0:T(8,128)S(1)}, f32[256,256]{1,0:T(8,128)S(1)}, u32[]{:S(2)}, u32[]{:S(2)}) collective-permute-start(f32[256,256]{1,0:T(8,128)S(1)} %get-tuple-element.72.near), channel_id=1, source_target_pairs={{0,1},{1,0},{2,3},{3,2},{4,5},{5,4},{6,7},{7,6},{8,9},{9,8},{10,11... | collective-permute-start | bytes 786440 | tf_op jit(solution)/shard_map/ppermute | solution.py:467
  41.1 5.5 %collective-permute-start.15 = (f32[256,256]{1,0:T(8,128)S(1)}, f32[256,256]{1,0:T(8,128)S(1)}, u32[]{:S(2)}, u32[]{:S(2)}) collective-permute-start(f32[256,256]{1,0:T(8,128)S(1)} %get-tuple-element.75.far), channel_id=1, source_target_pairs={{0,4},{1,3},{2,10},{3,1},{4,0},{5,7},{6,14},{7,5},{8,16},{9,11},{1... | collective-permute-start | bytes 786440 | tf_op jit(solution)/shard_map/ppermute | solution.py:467
  42.2 7.2 %collective-permute-start.11 = (f32[256,256]{1,0:T(8,128)S(1)}, f32[256,256]{1,0:T(8,128)S(1)}, u32[]{:S(2)}, u32[]{:S(2)}) collective-permute-start(f32[256,256]{1,0:T(8,128)S(1)} %get-tuple-element.72.near), channel_id=1, source_target_pairs={{0,4},{1,3},{2,10},{3,1},{4,0},{5,7},{6,14},{7,5},{8,16},{9,11},{1... | collective-permute-start | bytes 786440 | tf_op jit(solution)/shard_map/ppermute | solution.py:467
  50.0 5.0 %collective-permute-start.17 = (f32[256,256]{1,0:T(8,128)S(1)}, f32[256,256]{1,0:T(8,128)S(1)}, u32[]{:S(2)}, u32[]{:S(2)}) collective-permute-start(f32[256,256]{1,0:T(8,128)S(1)} %get-tuple-element.83.near), channel_id=1, source_target_pairs={{0,1},{1,0},{2,3},{3,2},{4,5},{5,4},{6,7},{7,6},{8,9},{9,8},{10,11... | collective-permute-start | bytes 786440 | tf_op jit(solution)/shard_map/ppermute | solution.py:467
  51.5 3.5 %collective-permute-start.18 = (f32[256,256]{1,0:T(8,128)S(1)}, f32[256,256]{1,0:T(8,128)S(1)}, u32[]{:S(2)}, u32[]{:S(2)}) collective-permute-start(f32[256,256]{1,0:T(8,128)S(1)} %get-tuple-element.80.far), channel_id=1, source_target_pairs={{0,1},{1,0},{2,3},{3,2},{4,5},{5,4},{6,7},{7,6},{8,9},{9,8},{10,11... | collective-permute-start | bytes 786440 | tf_op jit(solution)/shard_map/ppermute | solution.py:467
  51.6 5.6 %collective-permute-start.16 = (f32[256,256]{1,0:T(8,128)S(1)}, f32[256,256]{1,0:T(8,128)S(1)}, u32[]{:S(2)}, u32[]{:S(2)}) collective-permute-start(f32[256,256]{1,0:T(8,128)S(1)} %get-tuple-element.83.near), channel_id=1, source_target_pairs={{0,4},{1,3},{2,10},{3,1},{4,0},{5,7},{6,14},{7,5},{8,16},{9,11},{1... | collective-permute-start | bytes 786440 | tf_op jit(solution)/shard_map/ppermute | solution.py:467
  52.8 7.1 %collective-permute-start.14 = (f32[256,256]{1,0:T(8,128)S(1)}, f32[256,256]{1,0:T(8,128)S(1)}, u32[]{:S(2)}, u32[]{:S(2)}) collective-permute-start(f32[256,256]{1,0:T(8,128)S(1)} %get-tuple-element.80.far), channel_id=1, source_target_pairs={{0,4},{1,3},{2,10},{3,1},{4,0},{5,7},{6,14},{7,5},{8,16},{9,11},{1... | collective-permute-start | bytes 786440 | tf_op jit(solution)/shard_map/ppermute | solution.py:467
  60.6 6.7 %collective-permute-start.19 = (f32[256,256]{1,0:T(8,128)S(1)}, f32[256,256]{1,0:T(8,128)S(1)}, u32[]{:S(2)}, u32[]{:S(2)}) collective-permute-start(f32[256,256]{1,0:T(8,128)S(1)} %get-tuple-element.91.first_sent), channel_id=1, source_target_pairs={{0,1},{1,2},{2,6},{3,5},{4,0},{5,3},{6,7},{7,4},{8,14},{9,13},{10,... | collective-permute-start | bytes 786440 | tf_op jit(solution)/shard_map/ppermute | solution.py:467
  60.8 13.2 %collective-permute-start.20 = (f32[256,256]{1,0:T(8,128)S(1)}, f32[256,256]{1,0:T(8,128)S(1)}, u32[]{:S(2)}, u32[]{:S(2)}) collective-permute-start(f32[256,256]{1,0:T(8,128)S(1)} %get-tuple-element.92.second_sent), channel_id=1, source_target_pairs={{0,11},{1,3},{2,7},{3,4},{4,1},{5,2},{6,13},{7,5},{8,15},{9,12},{1... | collective-permute-start | bytes 786440 | tf_op jit(solution)/shard_map/ppermute | solution.py:467

commit v4 on v3

--- a/solution.py
+++ b/solution.py
@@ -45,6 +45,11 @@
     return device_of(problem ^ 1, block, half), device_of(problem, block, half)
 
 
+def homes_of(device):
+    block, half, slot, _ = start_of(device)
+    return device_of(slot, block, half), device_of(1 - slot, block, half)
+
+
 def straight(device):
     block, half, _, parity = start_of(device)
     return half == ((block & 1) ^ parity)
@@ -52,12 +57,11 @@
 
 def permutations(count):
     blocks = count // 4
-    first, second, rows, columns, link = [], [], [], [], []
+    first, rows, columns, link = [], [], [], []
+    back = [[(device, homes_of(device)[place]) for device in range(count)] for place in range(2)]
     for device in range(count):
         block, half, slot, parity = start_of(device)
-        to_first, to_second = targets_of(device)
-        first.append((device, to_first))
-        second.append((device, to_second))
+        first.append((device, targets_of(device)[0]))
         idle = device ^ 8 if device ^ 8 < count else device
         rows.append((device, device ^ 5 if (slot ^ half) != (block & 1) else idle))
         idle = device ^ 9 if device ^ 9 < count else device
@@ -70,7 +74,8 @@
         here, there = device_of(0, block, pair), device_of(1, block, pair)
         link += [(here, there), (there, here)]
     core = [(device, device ^ 1) for device in range(count)]
-    return full(first), full(second), rows, columns, sorted(link), core
+    back = [flipped(full(pairs)) for pairs in back]
+    return full(first), rows, columns, sorted(link), core, back
 
 
 def full(pairs):
@@ -83,7 +88,7 @@
 
 
 def kept(device):
-    first, second = targets_of(device)
+    first, second = homes_of(device)
     return first == device, second == device
 
 
@@ -410,7 +415,7 @@
 
 def last_near_kernel(weight, source, weights, early, acc, far, first, second):
     problem, _, pair = role("aux")
-    near_first = problem == 1
+    near_first = pair == problem
 
     def body(lower):
         near = acc[...] + weight * (early[...] + term(weights, N_LINK_F, forms(source[...], lower)))
@@ -422,12 +427,12 @@
 
 def restore_kernel(first, second, first_sent, second_sent, out_hbm, out, sems):
     device = lax.axis_index("aux")
-    _, half, slot, _ = start_of(device)
+    slot = device & 1
     keep_first, keep_second = kept(device)
     one = jnp.where(keep_first, first_sent[...], first[...])
     two = jnp.where(keep_second, second_sent[...], second[...])
-    herm = jnp.where(slot == half, two, one)
-    anti = jnp.where(slot == half, one, two)
+    herm = jnp.where(slot == 0, one, two)
+    anti = jnp.where(slot == 0, two, one)
     total = herm + anti.T
     diff = herm.T - anti
     copies = []
@@ -459,7 +464,7 @@
     count = lax.axis_size("aux")
     size = state.shape[-1]
     modes = couple.shape[0]
-    first_to, second_to, rows_to, columns_to, link_to, core_to = permutations(count)
+    first_to, rows_to, columns_to, link_to, core_to, back_to = permutations(count)
     pair_shape = (2, size, size)
     unit = 2 * size**3
 
@@ -483,7 +488,7 @@
     )
     device = lax.axis_index("aux")
     _, _, slot, parity = start_of(device)
-    keep_first, _ = kept(device)
+    keep_first = targets_of(device)[0] == device
     crossed = send(second, rows_to)
     first = jnp.where(keep_first, first, send(first, first_to))
     is_straight = straight(device)
@@ -560,7 +565,7 @@
     first, second = call(
         partial(last_near_kernel, shares[3]), [flat, flat], [link_f, weights, near_e, near_acc, far], flops=9 * unit
     )
-    back = [send(first, flipped(first_to)), send(second, flipped(second_to)), first, second]
+    back = [send(first, back_to[0]), send(second, back_to[1]), first, second]
     return call(
         restore_kernel,
         [(state.shape, F32)],

time: 75.5 us -> 73.6 us (0.975)
  the two profiles are of different devices: /device:TPU:9 before, /device:TPU:0 now
where the time goes in v4:
time: 73.6 us; the launch traced here: 73.2 us
  Pallas kernels  24.9 us (34%)
  starting transfers between devices  22.7 us (31%)
  waiting for transfers between devices  20.8 us (28%)
  local copies, waits for them, and re-layouts  3.21 us (4%)
  other arithmetic  1.09 us (1%)
    pallas_call x26, Pallas kernels, call(): pl.pallas_call(kernel, out_shape=shapes[0] if single else shapes, in_spec...  24.9 us
    ppermute x21, starting transfers between devices, send(): return lax.ppermute(value, 'aux', pairs)  22.7 us
    ppermute x21, waiting for transfers between devices, send(): return lax.ppermute(value, 'aux', pairs)  20.8 us
    unnamed x6, local copies, waits for them, and re-layouts  3.21 us
  transfers between devices with their start and end apart: 21, of which 10 were waited for; matrix products, arithmetic and copies ran while one was open for 1% of the time, Pallas kernels for 27%

profile of v4, /device:TPU:0, one launch (start us, length us, event | category | flops | bytes accessed | tf_op | source)
XLA Modules:
  0.0 73.2 jit_solution(2720502031053380762)
XLA Ops:
  0.0 2.0 %shard_map.91 = f32[264,256]{1,0:T(8,128)} custom-call(f32[1,2,256,256]{3,2,1,0:T(8,128)} %refs_0_.3, s32[1,3]{1,0:T(1,128)} %refs_1_.3, s32[1,3]{1,0:T(1,128)} %refs_2_.3, s32[1,3]{1,0:T(1,128)} %refs_3_.3, f32[2,3]{1,0:T(2,128)} %refs_4_.3, f32[3]{0:T(128)} %refs_5_.3), custom_call_target="tpu_custom_call" | custom-call | bytes 794696 | tf_op jit(solution)/shard_map/pallas_call | solution.py:451
  2.0 3.1 %collective-permute-start = (f32[264,256]{1,0:T(8,128)}, f32[264,256]{1,0:T(8,128)S(1)}, u32[]{:S(2)}, u32[]{:S(2)}) collective-permute-start(f32[264,256]{1,0:T(8,128)} %shard_map.91), channel_id=1, source_target_pairs={{0,8},{1,4},{2,7},{3,11},{4,1},{5,13},{6,14},{7,2},{8,0},{9,12},{1... | collective-permute-start | bytes 811016 | tf_op jit(solution)/shard_map/ppermute | solution.py:472
  5.1 2.0 %shard_map.93 = f32[264,256]{1,0:T(8,128)} custom-call(f32[1,2,256,256]{3,2,1,0:T(8,128)} %refs_0_.3, s32[1,3]{1,0:T(1,128)} %refs_1_.3, s32[1,3]{1,0:T(1,128)} %refs_2_.3, s32[1,3]{1,0:T(1,128)} %refs_3_.3, f32[2,3]{1,0:T(2,128)} %refs_4_.3, f32[3]{0:T(128)} %refs_5_.3), custom_call_target="tpu_custom_call" | custom-call | bytes 794696 | tf_op jit(solution)/shard_map/pallas_call | solution.py:451
  7.2 2.5 %collective-permute-done = f32[264,256]{1,0:T(8,128)S(1)} collective-permute-done((f32[264,256]{1,0:T(8,128)}, f32[264,256]{1,0:T(8,128)S(1)}, u32[]{:S(2)}, u32[]{:S(2)}) %collective-permute-start) | collective-permute-done | bytes 270368 | tf_op jit(solution)/shard_map/ppermute | solution.py:472
  9.8 2.3 %collective-permute-start.1 = (f32[264,256]{1,0:T(8,128)S(1)}, f32[264,256]{1,0:T(8,128)S(1)}, u32[]{:S(2)}, u32[]{:S(2)}) collective-permute-start(f32[264,256]{1,0:T(8,128)S(1)} %broadcast_select_fusion.1), channel_id=1, source_target_pairs={{0,9},{1,3},{2,11},{3,1},{4,13},{5,7},{6,15},{7,5},{8,10},{9,0},{1... | collective-permute-start | bytes 811016 | tf_op jit(solution)/shard_map/ppermute | solution.py:472
  12.1 1.7 %collective-permute-done.3 = f32[264,256]{1,0:T(8,128)S(1)} collective-permute-done((f32[264,256]{1,0:T(8,128)}, f32[264,256]{1,0:T(8,128)S(1)}, u32[]{:S(2)}, u32[]{:S(2)}) %collective-permute-start.3) | collective-permute-done | bytes 270368 | tf_op jit(solution)/shard_map/ppermute | solution.py:472
  13.8 2.7 %collective-permute-start.5 = (f32[264,256]{1,0:T(8,128)S(1)}, f32[264,256]{1,0:T(8,128)S(1)}, u32[]{:S(2)}, u32[]{:S(2)}) collective-permute-start(f32[264,256]{1,0:T(8,128)S(1)} %broadcast_select_fusion.array), channel_id=1, source_target_pairs={{0,1},{1,0},{2,3},{3,2},{4,5},{5,4},{6,7},{7,6},{8,9},{9,8},{10,11... | collective-permute-start | bytes 811016 | tf_op jit(solution)/shard_map/ppermute | solution.py:472
  16.4 1.0 %select_select_fusion.array = f32[264,256]{1,0:T(8,128)S(1)} fusion(f32[264,256]{1,0:T(8,128)S(1)} %collective-permute-done.1, f32[264,256]{1,0:T(8,128)} %shard_map.91, f32[264,256]{1,0:T(8,128)S(1)} %collective-permute-done, pred[]{:T(512)S(6)} %eq.10, pred[]{:T(512)S(6)} %eq.9), kind=kLoop, calls=%fused_computation | loop fusion | flops 135168 | bytes 1081346 | tf_op jit(solution)/shard_map/jit(_where)/select_n | solution.py:496
  17.5 2.6 %collective-permute-start.6 = (f32[264,256]{1,0:T(8,128)S(1)}, f32[264,256]{1,0:T(8,128)S(1)}, u32[]{:S(2)}, u32[]{:S(2)}) collective-permute-start(f32[264,256]{1,0:T(8,128)S(1)} %select_select_fusion.array), channel_id=1, source_target_pairs={{0,1},{1,0},{2,3},{3,2},{4,5},{5,4},{6,7},{7,6},{8,9},{9,8},{10,11... | collective-permute-start | bytes 811016 | tf_op jit(solution)/shard_map/ppermute | solution.py:472
  20.1 2.0 %collective-permute-start.2 = (f32[264,256]{1,0:T(8,128)S(1)}, f32[264,256]{1,0:T(8,128)S(1)}, u32[]{:S(2)}, u32[]{:S(2)}) collective-permute-start(f32[264,256]{1,0:T(8,128)S(1)} %select_select_fusion.array), channel_id=1, source_target_pairs={{0,4},{1,3},{2,10},{3,1},{4,0},{5,7},{6,14},{7,5},{8,16},{9,11},{1... | collective-permute-start | bytes 811016 | tf_op jit(solution)/shard_map/ppermute | solution.py:472
  22.1 1.1 %copy-done = f32[3,256,256]{2,1,0:T(8,128)S(1)} copy-done((f32[3,256,256]{2,1,0:T(8,128)S(1)}, f32[3,256,256]{2,1,0:T(8,128)}, u32[]{:S(2)}) %copy-start) | copy-done | bytes 786456
  23.3 1.0 %copy-done.1 = f32[2,256,256]{2,1,0:T(8,128)S(1)} copy-done((f32[2,256,256]{2,1,0:T(8,128)S(1)}, f32[2,256,256]{2,1,0:T(8,128)}, u32[]{:S(2)}) %copy-start.1) | copy-done | bytes 524312
  24.3 1.0 %copy-done.2 = f32[2,256,256]{2,1,0:T(8,128)S(1)} copy-done((f32[2,256,256]{2,1,0:T(8,128)S(1)}, f32[2,256,256]{2,1,0:T(8,128)}, u32[]{:S(2)}) %copy-start.2) | copy-done | bytes 524312
  26.2 1.1 %shard_map.94 = (bf16[8,1536,256]{2,1,0:T(8,128)(2,1)S(1)}, f32[2,256,256]{2,1,0:T(8,128)S(1)}, f32[2,8,128]{2,1,0:T(8,128)S(1)}, f32[2,256,256]{2,1,0:T(8,128)S(1)}) custom-call(f32[264,256]{1,0:T(8,128)S(1)} %broadcast_select_fusion.array, f32[3,256,256]{2,1,0:T(8,128)S(1)} %get-tuple-element.49.q_ref, bf16[1,1536,256]{2,1,0:T(8,128)(2,1)S(1)} %get-tuple-element.50.h_ref), custom_call_target="tpu_custom_call" | custom-call | flops 301989888 | bytes 9191424 | tf_op jit(solution)/shard_map/pallas_call | solution.py:451
  27.3 1.0 %shard_map.95 = (bf16[8,1536,256]{2,1,0:T(8,128)(2,1)S(1)}, f32[2,256,256]{2,1,0:T(8,128)S(1)}, f32[2,8,128]{2,1,0:T(8,128)S(1)}, f32[2,256,256]{2,1,0:T(8,128)S(1)}) custom-call(f32[264,256]{1,0:T(8,128)S(1)} %select_select_fusion.array, ...), custom_call_target="tpu_custom_call", output_to_operand_aliasing={{0}: (3, {}), {1}: (4, {}), {2}: (5, {}), {3}: (6, {})} | custom-call | flops 301989888 | bytes 16539648 | tf_op jit(solution)/shard_map/pallas_call | solution.py:451
  29.2 0.9 %shard_map.97 = (f32[256,256]{1,0:T(8,128)S(1)}, f32[256,256]{1,0:T(8,128)S(1)}) custom-call(f32[264,256]{1,0:T(8,128)S(1)} %collective-permute-done.5.one, f32[264,256]{1,0:T(8,128)S(1)} %collective-permute-done.6.two, bf16[8,1536,256]{2,1,0:T(8,128)(2,1)S(1)} %get-tuple-element.55.weights, f32[256,256]{1,0:T(8,128)S(1)} %get-tuple-element.58.near, ...), custom_call_target="tpu_custom_call" | custom-call | flops 905969664 | bytes 7880704 | tf_op jit(solution)/shard_map/pallas_call | solution.py:451
  32.6 1.8 %collective-permute-start.7 = (f32[256,256]{1,0:T(8,128)S(1)}, f32[256,256]{1,0:T(8,128)S(1)}, u32[]{:S(2)}, u32[]{:S(2)}) collective-permute-start(f32[256,256]{1,0:T(8,128)S(1)} %get-tuple-element.63.far), channel_id=1, source_target_pairs={{0,4},{1,3},{2,10},{3,1},{4,0},{5,7},{6,14},{7,5},{8,16},{9,11},{1... | collective-permute-start | bytes 786440 | tf_op jit(solution)/shard_map/ppermute | solution.py:472
  34.4 1.8 %shard_map.101 = (f32[256,256]{1,0:T(8,128)S(1)}, f32[256,256]{1,0:T(8,128)S(1)}) custom-call(f32[256,256]{1,0:T(8,128)S(1)} %get-tuple-element.65.near, f32[256,256]{1,0:T(8,128)S(1)} %get-tuple-element.63.far, bf16[1,1536,256]{2,1,0:T(8,128)(2,1)S(1)} %get-tuple-element.66.h_ref, bf16[8,1536,256]{2,1,0:T(8,128)(2,1)S(1)} %get-tuple-element.55.weights, ...), custom_call_target="tpu_custom_call" | custom-call | flops 1107296256 | bytes 8134656 | tf_op jit(solution)/shard_map/pallas_call | solution.py:451
  37.2 1.6 %collective-permute-done.8.source = f32[256,256]{1,0:T(8,128)S(1)} collective-permute-done((f32[256,256]{1,0:T(8,128)S(1)}, f32[256,256]{1,0:T(8,128)S(1)}, u32[]{:S(2)}, u32[]{:S(2)}) %collective-permute-start.8) | collective-permute-done | bytes 262176 | tf_op jit(solution)/shard_map/ppermute | solution.py:472
  40.0 1.5 %collective-permute-done.7.source = f32[256,256]{1,0:T(8,128)S(1)} collective-permute-done((f32[256,256]{1,0:T(8,128)S(1)}, f32[256,256]{1,0:T(8,128)S(1)}, u32[]{:S(2)}, u32[]{:S(2)}) %collective-permute-start.7) | collective-permute-done | bytes 262176 | tf_op jit(solution)/shard_map/ppermute | solution.py:472
  42.5 1.8 %collective-permute-start.11 = (f32[256,256]{1,0:T(8,128)S(1)}, f32[256,256]{1,0:T(8,128)S(1)}, u32[]{:S(2)}, u32[]{:S(2)}) collective-permute-start(f32[256,256]{1,0:T(8,128)S(1)} %get-tuple-element.72.near), channel_id=1, source_target_pairs={{0,4},{1,3},{2,10},{3,1},{4,0},{5,7},{6,14},{7,5},{8,16},{9,11},{1... | collective-permute-start | bytes 786440 | tf_op jit(solution)/shard_map/ppermute | solution.py:472
  44.3 1.7 %shard_map.106 = (f32[256,256]{1,0:T(8,128)S(1)}, f32[256,256]{1,0:T(8,128)S(1)}) custom-call(f32[256,256]{1,0:T(8,128)S(1)} %get-tuple-element.72.near, f32[256,256]{1,0:T(8,128)S(1)} %get-tuple-element.75.far, bf16[1,1536,256]{2,1,0:T(8,128)(2,1)S(1)} %get-tuple-element.66.h_ref, bf16[8,1536,256]{2,1,0:T(8,128)(2,1)S(1)} %get-tuple-element.55.weights, ...), custom_call_target="tpu_custom_call" | custom-call | flops 1107296256 | bytes 8134656 | tf_op jit(solution)/shard_map/pallas_call | solution.py:451
  47.0 1.7 %collective-permute-done.15.source = f32[256,256]{1,0:T(8,128)S(1)} collective-permute-done((f32[256,256]{1,0:T(8,128)S(1)}, f32[256,256]{1,0:T(8,128)S(1)}, u32[]{:S(2)}, u32[]{:S(2)}) %collective-permute-start.15) | collective-permute-done | bytes 262176 | tf_op jit(solution)/shard_map/ppermute | solution.py:472
  49.3 2.2 %collective-permute-done.11.source = f32[256,256]{1,0:T(8,128)S(1)} collective-permute-done((f32[256,256]{1,0:T(8,128)S(1)}, f32[256,256]{1,0:T(8,128)S(1)}, u32[]{:S(2)}, u32[]{:S(2)}) %collective-permute-start.11) | collective-permute-done | bytes 262176 | tf_op jit(solution)/shard_map/ppermute | solution.py:472
  53.4 1.8 %collective-permute-start.14 = (f32[256,256]{1,0:T(8,128)S(1)}, f32[256,256]{1,0:T(8,128)S(1)}, u32[]{:S(2)}, u32[]{:S(2)}) collective-permute-start(f32[256,256]{1,0:T(8,128)S(1)} %get-tuple-element.80.far), channel_id=1, source_target_pairs={{0,4},{1,3},{2,10},{3,1},{4,0},{5,7},{6,14},{7,5},{8,16},{9,11},{1... | collective-permute-start | bytes 786440 | tf_op jit(solution)/shard_map/ppermute | solution.py:472
  55.2 1.9 %shard_map.111 = (f32[256,256]{1,0:T(8,128)S(1)}, f32[256,256]{1,0:T(8,128)S(1)}) custom-call(f32[256,256]{1,0:T(8,128)S(1)} %get-tuple-element.83.near, f32[256,256]{1,0:T(8,128)S(1)} %get-tuple-element.80.far, bf16[1,1536,256]{2,1,0:T(8,128)(2,1)S(1)} %get-tuple-element.84.h_ref, bf16[8,1536,256]{2,1,0:T(8,128)(2,1)S(1)} %get-tuple-element.55.weights, ...), custom_call_target="tpu_custom_call" | custom-call | flops 1107296256 | bytes 8134656 | tf_op jit(solution)/shard_map/pallas_call | solution.py:451
  58.1 1.5 %collective-permute-done.16.source = f32[256,256]{1,0:T(8,128)S(1)} collective-permute-done((f32[256,256]{1,0:T(8,128)S(1)}, f32[256,256]{1,0:T(8,128)S(1)}, u32[]{:S(2)}, u32[]{:S(2)}) %collective-permute-start.16) | collective-permute-done | bytes 262176 | tf_op jit(solution)/shard_map/ppermute | solution.py:472
  60.7 1.6 %collective-permute-done.14.source = f32[256,256]{1,0:T(8,128)S(1)} collective-permute-done((f32[256,256]{1,0:T(8,128)S(1)}, f32[256,256]{1,0:T(8,128)S(1)}, u32[]{:S(2)}, u32[]{:S(2)}) %collective-permute-start.14) | collective-permute-done | bytes 262176 | tf_op jit(solution)/shard_map/ppermute | solution.py:472
  63.0 2.7 %collective-permute-start.19 = (f32[256,256]{1,0:T(8,128)S(1)}, f32[256,256]{1,0:T(8,128)S(1)}, u32[]{:S(2)}, u32[]{:S(2)}) collective-permute-start(f32[256,256]{1,0:T(8,128)S(1)} %get-tuple-element.91.first_sent), channel_id=1, source_target_pairs={{0,16},{1,2},{2,6},{3,4},{4,1},{5,3},{6,7},{7,5},{8,14},{9,12},{10... | collective-permute-start | bytes 786440 | tf_op jit(solution)/shard_map/ppermute | solution.py:472
  65.7 4.7 %collective-permute-done.19.first = f32[256,256]{1,0:T(8,128)S(1)} collective-permute-done((f32[256,256]{1,0:T(8,128)S(1)}, f32[256,256]{1,0:T(8,128)S(1)}, u32[]{:S(2)}, u32[]{:S(2)}) %collective-permute-start.19) | collective-permute-done | bytes 262176 | tf_op jit(solution)/shard_map/ppermute | solution.py:472
  70.3 1.7 %collective-permute-done.20.second = f32[256,256]{1,0:T(8,128)S(1)} collective-permute-done((f32[256,256]{1,0:T(8,128)S(1)}, f32[256,256]{1,0:T(8,128)S(1)}, u32[]{:S(2)}, u32[]{:S(2)}) %collective-permute-start.20) | collective-permute-done | bytes 262176 | tf_op jit(solution)/shard_map/ppermute | solution.py:472
  72.0 1.0 %shard_map.116 = f32[1,2,256,256]{3,2,1,0:T(8,128)} custom-call(f32[256,256]{1,0:T(8,128)S(1)} %collective-permute-done.19.first, f32[256,256]{1,0:T(8,128)S(1)} %collective-permute-done.20.second, f32[256,256]{1,0:T(8,128)S(1)} %get-tuple-element.91.first_sent, f32[256,256]{1,0:T(8,128)S(1)} %get-tuple-element.92.second_sent), custom_call_target="tpu_custom_call" | custom-call | bytes 1572864 | tf_op jit(solution)/shard_map/pallas_call | solution.py:451
  (45 shorter events, 13.4 us)
Async XLA Ops:
  2.0 7.8 %collective-permute-start = (f32[264,256]{1,0:T(8,128)}, f32[264,256]{1,0:T(8,128)S(1)}, u32[]{:S(2)}, u32[]{:S(2)}) collective-permute-start(f32[264,256]{1,0:T(8,128)} %shard_map.91), channel_id=1, source_target_pairs={{0,8},{1,4},{2,7},{3,11},{4,1},{5,13},{6,14},{7,2},{8,0},{9,12},{1... | collective-permute-start | bytes 811016 | tf_op jit(solution)/shard_map/ppermute | solution.py:472
  7.1 6.6 %collective-permute-start.3 = (f32[264,256]{1,0:T(8,128)}, f32[264,256]{1,0:T(8,128)S(1)}, u32[]{:S(2)}, u32[]{:S(2)}) collective-permute-start(f32[264,256]{1,0:T(8,128)} %shard_map.93), channel_id=1, source_target_pairs={{0,4},{1,0},{2,1},{3,5},{4,7},{5,3},{6,2},{7,6},{8,14},{9,10},{10,... | collective-permute-start | bytes 811016 | tf_op jit(solution)/shard_map/ppermute | solution.py:472
  9.8 6.6 %collective-permute-start.1 = (f32[264,256]{1,0:T(8,128)S(1)}, f32[264,256]{1,0:T(8,128)S(1)}, u32[]{:S(2)}, u32[]{:S(2)}) collective-permute-start(f32[264,256]{1,0:T(8,128)S(1)} %broadcast_select_fusion.1), channel_id=1, source_target_pairs={{0,9},{1,3},{2,11},{3,1},{4,13},{5,7},{6,15},{7,5},{8,10},{9,0},{1... | collective-permute-start | bytes 811016 | tf_op jit(solution)/shard_map/ppermute | solution.py:472
  13.8 15.4 %collective-permute-start.5 = (f32[264,256]{1,0:T(8,128)S(1)}, f32[264,256]{1,0:T(8,128)S(1)}, u32[]{:S(2)}, u32[]{:S(2)}) collective-permute-start(f32[264,256]{1,0:T(8,128)S(1)} %broadcast_select_fusion.array), channel_id=1, source_target_pairs={{0,1},{1,0},{2,3},{3,2},{4,5},{5,4},{6,7},{7,6},{8,9},{9,8},{10,11... | collective-permute-start | bytes 811016 | tf_op jit(solution)/shard_map/ppermute | solution.py:472
  17.5 11.7 %collective-permute-start.6 = (f32[264,256]{1,0:T(8,128)S(1)}, f32[264,256]{1,0:T(8,128)S(1)}, u32[]{:S(2)}, u32[]{:S(2)}) collective-permute-start(f32[264,256]{1,0:T(8,128)S(1)} %select_select_fusion.array), channel_id=1, source_target_pairs={{0,1},{1,0},{2,3},{3,2},{4,5},{5,4},{6,7},{7,6},{8,9},{9,8},{10,11... | collective-permute-start | bytes 811016 | tf_op jit(solution)/shard_map/ppermute | solution.py:472
  20.1 10.0 %collective-permute-start.4 = (f32[264,256]{1,0:T(8,128)S(1)}, f32[264,256]{1,0:T(8,128)S(1)}, u32[]{:S(2)}, u32[]{:S(2)}) collective-permute-start(f32[264,256]{1,0:T(8,128)S(1)} %broadcast_select_fusion.array), channel_id=1, source_target_pairs={{0,4},{1,3},{2,10},{3,1},{4,0},{5,7},{6,14},{7,5},{8,16},{9,11},{1... | collective-permute-start | bytes 811016 | tf_op jit(solution)/shard_map/ppermute | solution.py:472
  20.1 10.6 %collective-permute-start.2 = (f32[264,256]{1,0:T(8,128)S(1)}, f32[264,256]{1,0:T(8,128)S(1)}, u32[]{:S(2)}, u32[]{:S(2)}) collective-permute-start(f32[264,256]{1,0:T(8,128)S(1)} %select_select_fusion.array), channel_id=1, source_target_pairs={{0,4},{1,3},{2,10},{3,1},{4,0},{5,7},{6,14},{7,5},{8,16},{9,11},{1... | collective-permute-start | bytes 811016 | tf_op jit(solution)/shard_map/ppermute | solution.py:472
  22.1 1.1 %copy-start = (f32[3,256,256]{2,1,0:T(8,128)S(1)}, f32[3,256,256]{2,1,0:T(8,128)}, u32[]{:S(2)}) copy-start(f32[3,256,256]{2,1,0:T(8,128)} %couple.1) | copy-start | bytes 2359300
  23.3 1.0 %copy-start.1 = (f32[2,256,256]{2,1,0:T(8,128)S(1)}, f32[2,256,256]{2,1,0:T(8,128)}, u32[]{:S(2)}) copy-start(f32[2,256,256]{2,1,0:T(8,128)} %h_static.1) | copy-start | bytes 1572868
  24.3 1.0 %copy-start.2 = (f32[2,256,256]{2,1,0:T(8,128)S(1)}, f32[2,256,256]{2,1,0:T(8,128)}, u32[]{:S(2)}) copy-start(f32[2,256,256]{2,1,0:T(8,128)} %drive_op.1) | copy-start | bytes 1572868
  31.3 5.0 %collective-permute-start.9 = (f32[256,256]{1,0:T(8,128)S(1)}, f32[256,256]{1,0:T(8,128)S(1)}, u32[]{:S(2)}, u32[]{:S(2)}) collective-permute-start(f32[256,256]{1,0:T(8,128)S(1)} %get-tuple-element.65.near), channel_id=1, source_target_pairs={{0,1},{1,0},{2,3},{3,2},{4,5},{5,4},{6,7},{7,6},{8,9},{9,8},{10,11... | collective-permute-start | bytes 786440 | tf_op jit(solution)/shard_map/ppermute | solution.py:472
  32.0 4.3 %collective-permute-start.10 = (f32[256,256]{1,0:T(8,128)S(1)}, f32[256,256]{1,0:T(8,128)S(1)}, u32[]{:S(2)}, u32[]{:S(2)}) collective-permute-start(f32[256,256]{1,0:T(8,128)S(1)} %get-tuple-element.63.far), channel_id=1, source_target_pairs={{0,1},{1,0},{2,3},{3,2},{4,5},{5,4},{6,7},{7,6},{8,9},{9,8},{10,11... | collective-permute-start | bytes 786440 | tf_op jit(solution)/shard_map/ppermute | solution.py:472
  32.4 6.4 %collective-permute-start.8 = (f32[256,256]{1,0:T(8,128)S(1)}, f32[256,256]{1,0:T(8,128)S(1)}, u32[]{:S(2)}, u32[]{:S(2)}) collective-permute-start(f32[256,256]{1,0:T(8,128)S(1)} %get-tuple-element.65.near), channel_id=1, source_target_pairs={{0,4},{1,3},{2,10},{3,1},{4,0},{5,7},{6,14},{7,5},{8,16},{9,11},{1... | collective-permute-start | bytes 786440 | tf_op jit(solution)/shard_map/ppermute | solution.py:472
  32.6 9.0 %collective-permute-start.7 = (f32[256,256]{1,0:T(8,128)S(1)}, f32[256,256]{1,0:T(8,128)S(1)}, u32[]{:S(2)}, u32[]{:S(2)}) collective-permute-start(f32[256,256]{1,0:T(8,128)S(1)} %get-tuple-element.63.far), channel_id=1, source_target_pairs={{0,4},{1,3},{2,10},{3,1},{4,0},{5,7},{6,14},{7,5},{8,16},{9,11},{1... | collective-permute-start | bytes 786440 | tf_op jit(solution)/shard_map/ppermute | solution.py:472
  39.4 6.7 %collective-permute-start.13 = (f32[256,256]{1,0:T(8,128)S(1)}, f32[256,256]{1,0:T(8,128)S(1)}, u32[]{:S(2)}, u32[]{:S(2)}) collective-permute-start(f32[256,256]{1,0:T(8,128)S(1)} %get-tuple-element.75.far), channel_id=1, source_target_pairs={{0,1},{1,0},{2,3},{3,2},{4,5},{5,4},{6,7},{7,6},{8,9},{9,8},{10,11... | collective-permute-start | bytes 786440 | tf_op jit(solution)/shard_map/ppermute | solution.py:472
  42.2 3.9 %collective-permute-start.12 = (f32[256,256]{1,0:T(8,128)S(1)}, f32[256,256]{1,0:T(8,128)S(1)}, u32[]{:S(2)}, u32[]{:S(2)}) collective-permute-start(f32[256,256]{1,0:T(8,128)S(1)} %get-tuple-element.72.near), channel_id=1, source_target_pairs={{0,1},{1,0},{2,3},{3,2},{4,5},{5,4},{6,7},{7,6},{8,9},{9,8},{10,11... | collective-permute-start | bytes 786440 | tf_op jit(solution)/shard_map/ppermute | solution.py:472
  42.3 6.4 %collective-permute-start.15 = (f32[256,256]{1,0:T(8,128)S(1)}, f32[256,256]{1,0:T(8,128)S(1)}, u32[]{:S(2)}, u32[]{:S(2)}) collective-permute-start(f32[256,256]{1,0:T(8,128)S(1)} %get-tuple-element.75.far), channel_id=1, source_target_pairs={{0,4},{1,3},{2,10},{3,1},{4,0},{5,7},{6,14},{7,5},{8,16},{9,11},{1... | collective-permute-start | bytes 786440 | tf_op jit(solution)/shard_map/ppermute | solution.py:472
  42.5 9.0 %collective-permute-start.11 = (f32[256,256]{1,0:T(8,128)S(1)}, f32[256,256]{1,0:T(8,128)S(1)}, u32[]{:S(2)}, u32[]{:S(2)}) collective-permute-start(f32[256,256]{1,0:T(8,128)S(1)} %get-tuple-element.72.near), channel_id=1, source_target_pairs={{0,4},{1,3},{2,10},{3,1},{4,0},{5,7},{6,14},{7,5},{8,16},{9,11},{1... | collective-permute-start | bytes 786440 | tf_op jit(solution)/shard_map/ppermute | solution.py:472
  52.1 5.0 %collective-permute-start.17 = (f32[256,256]{1,0:T(8,128)S(1)}, f32[256,256]{1,0:T(8,128)S(1)}, u32[]{:S(2)}, u32[]{:S(2)}) collective-permute-start(f32[256,256]{1,0:T(8,128)S(1)} %get-tuple-element.83.near), channel_id=1, source_target_pairs={{0,1},{1,0},{2,3},{3,2},{4,5},{5,4},{6,7},{7,6},{8,9},{9,8},{10,11... | collective-permute-start | bytes 786440 | tf_op jit(solution)/shard_map/ppermute | solution.py:472
  52.8 4.3 %collective-permute-start.18 = (f32[256,256]{1,0:T(8,128)S(1)}, f32[256,256]{1,0:T(8,128)S(1)}, u32[]{:S(2)}, u32[]{:S(2)}) collective-permute-start(f32[256,256]{1,0:T(8,128)S(1)} %get-tuple-element.80.far), channel_id=1, source_target_pairs={{0,1},{1,0},{2,3},{3,2},{4,5},{5,4},{6,7},{7,6},{8,9},{9,8},{10,11... | collective-permute-start | bytes 786440 | tf_op jit(solution)/shard_map/ppermute | solution.py:472
  53.2 6.4 %collective-permute-start.16 = (f32[256,256]{1,0:T(8,128)S(1)}, f32[256,256]{1,0:T(8,128)S(1)}, u32[]{:S(2)}, u32[]{:S(2)}) collective-permute-start(f32[256,256]{1,0:T(8,128)S(1)} %get-tuple-element.83.near), channel_id=1, source_target_pairs={{0,4},{1,3},{2,10},{3,1},{4,0},{5,7},{6,14},{7,5},{8,16},{9,11},{1... | collective-permute-start | bytes 786440 | tf_op jit(solution)/shard_map/ppermute | solution.py:472
  53.4 9.0 %collective-permute-start.14 = (f32[256,256]{1,0:T(8,128)S(1)}, f32[256,256]{1,0:T(8,128)S(1)}, u32[]{:S(2)}, u32[]{:S(2)}) collective-permute-start(f32[256,256]{1,0:T(8,128)S(1)} %get-tuple-element.80.far), channel_id=1, source_target_pairs={{0,4},{1,3},{2,10},{3,1},{4,0},{5,7},{6,14},{7,5},{8,16},{9,11},{1... | collective-permute-start | bytes 786440 | tf_op jit(solution)/shard_map/ppermute | solution.py:472
  63.0 7.3 %collective-permute-start.19 = (f32[256,256]{1,0:T(8,128)S(1)}, f32[256,256]{1,0:T(8,128)S(1)}, u32[]{:S(2)}, u32[]{:S(2)}) collective-permute-start(f32[256,256]{1,0:T(8,128)S(1)} %get-tuple-element.91.first_sent), channel_id=1, source_target_pairs={{0,16},{1,2},{2,6},{3,4},{4,1},{5,3},{6,7},{7,5},{8,14},{9,12},{10... | collective-permute-start | bytes 786440 | tf_op jit(solution)/shard_map/ppermute | solution.py:472
  65.6 6.4 %collective-permute-start.20 = (f32[256,256]{1,0:T(8,128)S(1)}, f32[256,256]{1,0:T(8,128)S(1)}, u32[]{:S(2)}, u32[]{:S(2)}) collective-permute-start(f32[256,256]{1,0:T(8,128)S(1)} %get-tuple-element.92.second_sent), channel_id=1, source_target_pairs={{0,1},{1,3},{2,7},{3,5},{4,0},{5,2},{6,22},{7,4},{8,15},{9,13},{10... | collective-permute-start | bytes 786440 | tf_op jit(solution)/shard_map/ppermute | solution.py:472

commit v5 on v4

--- a/solution.py
+++ b/solution.py
@@ -35,37 +35,13 @@
     return problem, 2 * group + odd, core ^ odd
 
 
-def start_of(device):
-    return device >> 2, (device >> 1) & 1, device & 1, (device >> 3) & 1
-
-
-def targets_of(device):
-    block, half, slot, _ = start_of(device)
-    problem = slot ^ half
-    return device_of(problem ^ 1, block, half), device_of(problem, block, half)
-
-
-def homes_of(device):
-    block, half, slot, _ = start_of(device)
-    return device_of(slot, block, half), device_of(1 - slot, block, half)
-
-
-def straight(device):
-    block, half, _, parity = start_of(device)
-    return half == ((block & 1) ^ parity)
-
-
 def permutations(count):
     blocks = count // 4
-    first, rows, columns, link = [], [], [], []
-    back = [[(device, homes_of(device)[place]) for device in range(count)] for place in range(2)]
+    first, second, link = [], [], []
     for device in range(count):
-        block, half, slot, parity = start_of(device)
-        first.append((device, targets_of(device)[0]))
-        idle = device ^ 8 if device ^ 8 < count else device
-        rows.append((device, device ^ 5 if (slot ^ half) != (block & 1) else idle))
-        idle = device ^ 9 if device ^ 9 < count else device
-        columns.append((device, device ^ 2 if slot != parity else idle))
+        block, half, slot = device >> 2, (device >> 1) & 1, device & 1
+        first.append((device, device_of(slot, block, half)))
+        second.append((device, device_of(1 - slot, block, half)))
     for problem in range(2):
         for block in range(blocks - 1):
             here, there = device_of(problem, block, 1), device_of(problem, block + 1, 0)
@@ -74,8 +50,7 @@
         here, there = device_of(0, block, pair), device_of(1, block, pair)
         link += [(here, there), (there, here)]
     core = [(device, device ^ 1) for device in range(count)]
-    back = [flipped(full(pairs)) for pairs in back]
-    return full(first), rows, columns, sorted(link), core, back
+    return full(first), full(second), sorted(link), core
 
 
 def full(pairs):
@@ -88,8 +63,8 @@
 
 
 def kept(device):
-    first, second = homes_of(device)
-    return first == device, second == device
+    block, half, slot = device >> 2, (device >> 1) & 1, device & 1
+    return device_of(slot, block, half) == device, device_of(1 - slot, block, half) == device
 
 
 def flipped(pairs):
@@ -161,41 +136,38 @@
         body(False)
 
 
-def convert_kernel(which, *refs):
-    inputs, out, held, sems = refs[:6], refs[6], refs[7:13], refs[13]
-    state, occ, up, low, bath, damp = held
+def convert_kernel(which, state_hbm, occ_hbm, up_hbm, low_hbm, out, state, occ, up, low, sems):
     copies = [
-        pltpu.make_async_copy(src, dst, sems.at[index]) for index, (src, dst) in enumerate(zip(inputs, held))
+        pltpu.make_async_copy(src, dst, sems.at[index])
+        for index, (src, dst) in enumerate(((state_hbm, state), (occ_hbm, occ), (up_hbm, up), (low_hbm, low)))
     ]
     for copy in copies:
         copy.start()
-    for copy in copies:
-        copy.wait()
-    _, half, slot, _ = start_of(lax.axis_index("aux"))
-    problem = slot ^ half ^ 1 ^ which
+    copies[0].wait()
+    slot = lax.axis_index("aux") & 1
     re, im = state[0, 0], state[0, 1]
     size = re.shape[0]
 
-    @pl.when(problem == 0)
+    @pl.when(slot == which)
     def _():
         out[0:size] = 0.5 * ((re + im) + (re - im).T)
 
-    @pl.when(problem == 1)
+    @pl.when(slot != which)
     def _():
         out[0:size] = 0.5 * ((re + im).T - (re - im))
 
+    for copy in copies[1:]:
+        copy.wait()
     lane = lax.broadcasted_iota(jnp.int32, (META, size), 1)
     modes = occ.shape[1]
     row = jnp.zeros((META, size), F32)
     for mode in range(modes):
         for place, table in enumerate((occ, up, low)):
             row = jnp.where(lane == place * modes + mode, table[0, mode].astype(F32), row)
-        for place, value in enumerate((damp[mode], bath[0, mode], bath[1, mode])):
-            row = jnp.where(lane == (3 + place) * modes + mode, value, row)
     out[size : size + META] = row
 
 
-def prepare_kernel(h_static, drive_op, couple, h_a, h_b, h_c, q_out):
+def prepare_kernel(h_static, drive_op, couple, bath_coef, damping, h_a, h_b, h_c, q_out, damp_out):
     h_re = (h_static[0] + h_static[0].T) * 0.5
     h_im = (h_static[1] - h_static[1].T) * 0.5
     v_re = (drive_op[0] + drive_op[0].T) * 0.5
@@ -205,12 +177,14 @@
         store_stack(h_out, 0, h_re + drive * v_re, h_im + drive * v_im)
     for mode in range(couple.shape[0]):
         q_out[mode] = (couple[mode] + couple[mode].T) * 0.5
-
-
-def arrive_kernel(which, array, q_ref, h_ref, *refs):
+        for place, value in enumerate((damping[mode], bath_coef[0, mode], bath_coef[1, mode])):
+            damp_out[3 * mode + place] = jnp.full(damp_out.shape[1:], value, F32)
+
+
+def arrive_kernel(which, array, q_ref, damp, h_ref, *refs):
     weights, base, rate, early = refs[-4:]
     problem, block, pair = role("aux")
-    part = problem ^ 1 ^ which
+    part = pair ^ problem ^ which
     size = q_ref.shape[1]
     modes = q_ref.shape[0]
     meta = array[size : size + 1]
@@ -220,7 +194,7 @@
         return meta[:, column : column + 1]
 
     def constant(place, mode):
-        return entry(3 + place, mode)
+        return damp[3 * mode + place][0:1, 0:1]
 
     total = jnp.zeros((1, 1), F32)
     for mode in range(modes):
@@ -304,19 +278,19 @@
     by_type(pair == 1, body)
 
 
-def pick(one, two, sorted_already):
+def pick(one, two, pair, sorted_already):
     if sorted_already:
         return one[...], two[...]
     problem, _, _ = role("aux")
     size = one.shape[1]
-    near_first = problem == 1
+    near_first = pair == problem
     one, two = one[0:size], two[0:size]
     return jnp.where(near_first, one, two), jnp.where(near_first, two, one)
 
 
 def partner_kernel(sorted_already, one, two, weights, near, far, near_out, far_out):
     _, _, pair = role("aux")
-    x_n, x_f = pick(one, two, sorted_already)
+    x_n, x_f = pick(one, two, 1 - pair, sorted_already)
 
     def body(lower):
         f_n, f_f = forms(x_n, lower), forms(x_f, lower)
@@ -349,8 +323,8 @@
 
 
 def sent_far(which):
-    problem, _, _ = role("aux")
-    return problem ^ 1 ^ which
+    problem, _, pair = role("aux")
+    return pair ^ 1 ^ problem ^ which
 
 
 def first_part_kernel(array, weights, near, far, near_out, far_out):
@@ -464,7 +438,7 @@
     count = lax.axis_size("aux")
     size = state.shape[-1]
     modes = couple.shape[0]
-    first_to, rows_to, columns_to, link_to, core_to, back_to = permutations(count)
+    first_to, second_to, link_to, core_to = permutations(count)
     pair_shape = (2, size, size)
     unit = 2 * size**3
 
@@ -472,7 +446,7 @@
         return lax.ppermute(value, "aux", pairs)
 
     tall = ((size + META, size), F32)
-    tables = [occupation, raise_nbr, lower_nbr, bath_coef, damping]
+    tables = [occupation, raise_nbr, lower_nbr]
     first, second = (
         call(
             partial(convert_kernel, which),
@@ -481,34 +455,32 @@
             space=pl.BlockSpec(memory_space=pltpu.HBM),
             grant=60,
             scratch=[pltpu.VMEM(state.shape, F32)]
-            + [pltpu.SMEM(table.shape, table.dtype) for table in tables]
-            + [pltpu.SemaphoreType.DMA((1 + len(tables),))],
+            + [pltpu.SMEM(table.shape, jnp.int32) for table in tables]
+            + [pltpu.SemaphoreType.DMA((4,))],
         )
         for which in range(2)
     )
-    device = lax.axis_index("aux")
-    _, _, slot, parity = start_of(device)
-    keep_first = targets_of(device)[0] == device
-    crossed = send(second, rows_to)
+    keep_first, keep_second = kept(lax.axis_index("aux"))
     first = jnp.where(keep_first, first, send(first, first_to))
-    is_straight = straight(device)
-    turned = send(jnp.where(is_straight, crossed, second), columns_to)
-    second = jnp.where(slot == parity, jnp.where(is_straight, second, crossed), turned)
-    *h_now, q_all = call(
-        prepare_kernel, [((1, 6 * size, size), BF16)] * 3 + [((modes, size, size), F32)], [h_static, drive_op, couple]
+    second = jnp.where(keep_second, second, send(second, second_to))
+    *h_now, q_all, damp = call(
+        prepare_kernel,
+        [((1, 6 * size, size), BF16)] * 3 + [((modes, size, size), F32), ((3 * modes, 8, 128), F32)],
+        [h_static, drive_op, couple, bath_coef, damping],
+        smem=(3, 4),
     )
     flat = ((size, size), F32)
 
     held = [((8, 6 * size, size), BF16), (pair_shape, F32), ((2, 8, 128), F32), (pair_shape, F32)]
-    state_now = call(partial(arrive_kernel, 0), held, [first, q_all, h_now[0]], flops=9 * unit)
+    state_now = call(partial(arrive_kernel, 0), held, [first, q_all, damp, h_now[0]], flops=9 * unit)
     link = [send(first, link_to)]
     partner = [send(first, core_to)]
     weights, base, rate, early = call(
         partial(arrive_kernel, 1),
         held,
-        [second, q_all, h_now[0], *state_now],
+        [second, q_all, damp, h_now[0], *state_now],
         flops=9 * unit,
-        aliases={3 + index: index for index in range(4)},
+        aliases={4 + index: index for index in range(4)},
     )
     link.append(send(second, link_to))
     partner.append(send(second, core_to))
@@ -565,7 +537,7 @@
     first, second = call(
         partial(last_near_kernel, shares[3]), [flat, flat], [link_f, weights, near_e, near_acc, far], flops=9 * unit
     )
-    back = [send(first, back_to[0]), send(second, back_to[1]), first, second]
+    back = [send(first, flipped(first_to)), send(second, flipped(second_to)), first, second]
     return call(
         restore_kernel,
         [(state.shape, F32)],

time: 73.6 us -> 74.5 us (1.012)
  the two profiles are of different devices: /device:TPU:0 before, /device:TPU:8 now
where the time goes in v5:
time: 74.5 us; the launch traced here: 73.7 us
  waiting for transfers between devices  27.2 us (37%)
  Pallas kernels  25.5 us (34%)
  starting transfers between devices  15.8 us (21%)
  local copies, waits for them, and re-layouts  4.55 us (6%)
    ppermute x20, waiting for transfers between devices, send(): return lax.ppermute(value, 'aux', pairs)  27.2 us
    pallas_call x26, Pallas kernels, call(): pl.pallas_call(kernel, out_shape=shapes[0] if single else shapes, in_spec...  25.5 us
    ppermute x20, starting transfers between devices, send(): return lax.ppermute(value, 'aux', pairs)  15.8 us
    unnamed x10, local copies, waits for them, and re-layouts  4.55 us
  transfers between devices with their start and end apart: 20, of which 10 were waited for; matrix products, arithmetic and copies ran while one was open for 0% of the time, Pallas kernels for 29%

profile of v5, /device:TPU:8, one launch (start us, length us, event | category | flops | bytes accessed | tf_op | source)
XLA Modules:
  0.0 73.7 jit_solution(18114246596076473930)
XLA Ops:
  0.0 2.0 %shard_map.93 = f32[264,256]{1,0:T(8,128)} custom-call(f32[1,2,256,256]{3,2,1,0:T(8,128)} %state_hbm.3, s32[1,3]{1,0:T(1,128)} %occ_hbm.3, s32[1,3]{1,0:T(1,128)} %up_hbm.3, s32[1,3]{1,0:T(1,128)} %low_hbm.3), custom_call_target="tpu_custom_call" | custom-call | bytes 794660 | tf_op jit(solution)/shard_map/pallas_call | solution.py:425
  2.0 1.5 %collective-permute-start.2 = (f32[264,256]{1,0:T(8,128)}, f32[264,256]{1,0:T(8,128)S(1)}, u32[]{:S(2)}, u32[]{:S(2)}) collective-permute-start(f32[264,256]{1,0:T(8,128)} %shard_map.93), channel_id=1, source_target_pairs={{0,16},{1,4},{2,1},{3,5},{4,3},{5,7},{6,2},{7,6},{8,10},{9,14},{10... | collective-permute-start | bytes 811016 | tf_op jit(solution)/shard_map/ppermute | solution.py:446
  3.5 2.0 %shard_map.91 = f32[264,256]{1,0:T(8,128)} custom-call(f32[1,2,256,256]{3,2,1,0:T(8,128)} %state_hbm.3, s32[1,3]{1,0:T(1,128)} %occ_hbm.3, s32[1,3]{1,0:T(1,128)} %up_hbm.3, s32[1,3]{1,0:T(1,128)} %low_hbm.3), custom_call_target="tpu_custom_call" | custom-call | bytes 794660 | tf_op jit(solution)/shard_map/pallas_call | solution.py:425
  5.5 1.5 %collective-permute-start = (f32[264,256]{1,0:T(8,128)}, f32[264,256]{1,0:T(8,128)S(1)}, u32[]{:S(2)}, u32[]{:S(2)}) collective-permute-start(f32[264,256]{1,0:T(8,128)} %shard_map.91), channel_id=1, source_target_pairs={{0,4},{1,0},{2,5},{3,1},{4,7},{5,3},{6,22},{7,2},{8,14},{9,10},{10... | collective-permute-start | bytes 811016 | tf_op jit(solution)/shard_map/ppermute | solution.py:446
  7.0 5.6 %collective-permute-done.2 = f32[264,256]{1,0:T(8,128)S(1)} collective-permute-done((f32[264,256]{1,0:T(8,128)}, f32[264,256]{1,0:T(8,128)S(1)}, u32[]{:S(2)}, u32[]{:S(2)}) %collective-permute-start.2) | collective-permute-done | bytes 270368 | tf_op jit(solution)/shard_map/ppermute | solution.py:446
  12.7 4.6 %collective-permute-done = f32[264,256]{1,0:T(8,128)S(1)} collective-permute-done((f32[264,256]{1,0:T(8,128)}, f32[264,256]{1,0:T(8,128)S(1)}, u32[]{:S(2)}, u32[]{:S(2)}) %collective-permute-start) | collective-permute-done | bytes 270368 | tf_op jit(solution)/shard_map/ppermute | solution.py:446
  18.4 1.1 %collective-permute-start.1 = (f32[264,256]{1,0:T(8,128)S(1)}, f32[264,256]{1,0:T(8,128)S(1)}, u32[]{:S(2)}, u32[]{:S(2)}) collective-permute-start(f32[264,256]{1,0:T(8,128)S(1)} %broadcast_select_fusion.1.array), channel_id=1, source_target_pairs={{0,4},{1,3},{2,10},{3,1},{4,0},{5,7},{6,14},{7,5},{8,16},{9,11},{1... | collective-permute-start | bytes 811016 | tf_op jit(solution)/shard_map/ppermute | solution.py:446
  19.5 1.1 %copy-done = f32[3,256,256]{2,1,0:T(8,128)S(1)} copy-done((f32[3,256,256]{2,1,0:T(8,128)S(1)}, f32[3,256,256]{2,1,0:T(8,128)}, u32[]{:S(2)}) %copy-start) | copy-done | bytes 786456
  20.6 1.0 %copy-done.1 = f32[2,256,256]{2,1,0:T(8,128)S(1)} copy-done((f32[2,256,256]{2,1,0:T(8,128)S(1)}, f32[2,256,256]{2,1,0:T(8,128)}, u32[]{:S(2)}) %copy-start.1) | copy-done | bytes 524312
  24.1 1.4 %shard_map.92 = (bf16[1,1536,256]{2,1,0:T(8,128)(2,1)S(1)}, bf16[1,1536,256]{2,1,0:T(8,128)(2,1)S(1)}, bf16[1,1536,256]{2,1,0:T(8,128)(2,1)S(1)}, f32[3,256,256]{2,1,0:T(8,128)S(1)}, f32[9,8,128]{2,1,0:T(8,128)S(1)}) custom-call(f32[2,256,256]{2,1,0:T(8,128)S(1)} %copy-done.1, f32[2,256,256]{2,1,0:T(8,128)S(1)} %copy-done.2, f32[3,256,256]{2,1,0:T(8,128)S(1)} %copy-done, ...), custom_call_target="tpu_custom_call" | custom-call | bytes 5017636 | tf_op jit(solution)/shard_map/pallas_call | solution.py:425
  25.5 1.2 %shard_map.94 = (bf16[8,1536,256]{2,1,0:T(8,128)(2,1)S(1)}, f32[2,256,256]{2,1,0:T(8,128)S(1)}, f32[2,8,128]{2,1,0:T(8,128)S(1)}, f32[2,256,256]{2,1,0:T(8,128)S(1)}) custom-call(f32[264,256]{1,0:T(8,128)S(1)} %broadcast_select_fusion.array, f32[3,256,256]{2,1,0:T(8,128)S(1)} %get-tuple-element.50.q_ref, f32[9,8,128]{2,1,0:T(8,128)S(1)} %get-tuple-element.51.damp, ...), custom_call_target="tpu_custom_call" | custom-call | flops 301989888 | bytes 9228288 | tf_op jit(solution)/shard_map/pallas_call | solution.py:425
  26.7 1.2 %shard_map.95 = (bf16[8,1536,256]{2,1,0:T(8,128)(2,1)S(1)}, f32[2,256,256]{2,1,0:T(8,128)S(1)}, f32[2,8,128]{2,1,0:T(8,128)S(1)}, f32[2,256,256]{2,1,0:T(8,128)S(1)}) custom-call(f32[264,256]{1,0:T(8,128)S(1)} %broadcast_select_fusion.1.array, ...), custom_call_target="tpu_custom_call", output_to_operand_aliasing={{0}: (4, {}), {1}: (5, {}), {2}: (6, {}), {3}: (7, {})} | custom-call | flops 301989888 | bytes 16576512 | tf_op jit(solution)/shard_map/pallas_call | solution.py:425
  28.7 1.3 %shard_map.97 = (f32[256,256]{1,0:T(8,128)S(1)}, f32[256,256]{1,0:T(8,128)S(1)}) custom-call(f32[264,256]{1,0:T(8,128)S(1)} %collective-permute-done.4.one, f32[264,256]{1,0:T(8,128)S(1)} %collective-permute-done.5.two, bf16[8,1536,256]{2,1,0:T(8,128)(2,1)S(1)} %get-tuple-element.57.weights, f32[256,256]{1,0:T(8,128)S(1)} %get-tuple-element.60.near, ...), custom_call_target="tpu_custom_call" | custom-call | flops 905969664 | bytes 7880704 | tf_op jit(solution)/shard_map/pallas_call | solution.py:425
  31.6 1.1 %collective-permute-start.9 = (f32[256,256]{1,0:T(8,128)S(1)}, f32[256,256]{1,0:T(8,128)S(1)}, u32[]{:S(2)}, u32[]{:S(2)}) collective-permute-start(f32[256,256]{1,0:T(8,128)S(1)} %get-tuple-element.65.far), channel_id=1, source_target_pairs={{0,1},{1,0},{2,3},{3,2},{4,5},{5,4},{6,7},{7,6},{8,9},{9,8},{10,11... | collective-permute-start | bytes 786440 | tf_op jit(solution)/shard_map/ppermute | solution.py:446
  33.5 1.2 %collective-permute-start.6 = (f32[256,256]{1,0:T(8,128)S(1)}, f32[256,256]{1,0:T(8,128)S(1)}, u32[]{:S(2)}, u32[]{:S(2)}) collective-permute-start(f32[256,256]{1,0:T(8,128)S(1)} %get-tuple-element.65.far), channel_id=1, source_target_pairs={{0,4},{1,3},{2,10},{3,1},{4,0},{5,7},{6,14},{7,5},{8,16},{9,11},{1... | collective-permute-start | bytes 786440 | tf_op jit(solution)/shard_map/ppermute | solution.py:446
  34.6 1.9 %shard_map.101 = (f32[256,256]{1,0:T(8,128)S(1)}, f32[256,256]{1,0:T(8,128)S(1)}) custom-call(f32[256,256]{1,0:T(8,128)S(1)} %get-tuple-element.67.near, f32[256,256]{1,0:T(8,128)S(1)} %get-tuple-element.65.far, bf16[1,1536,256]{2,1,0:T(8,128)(2,1)S(1)} %get-tuple-element.68.h_ref, bf16[8,1536,256]{2,1,0:T(8,128)(2,1)S(1)} %get-tuple-element.57.weights, ...), custom_call_target="tpu_custom_call" | custom-call | flops 1107296256 | bytes 8134656 | tf_op jit(solution)/shard_map/pallas_call | solution.py:425
  36.6 1.3 %shard_map.102 = (f32[256,256]{1,0:T(8,128)S(1)}, f32[256,256]{1,0:T(8,128)S(1)}) custom-call(f32[256,256]{1,0:T(8,128)S(1)} %collective-permute-done.8.one, f32[256,256]{1,0:T(8,128)S(1)} %collective-permute-done.9.two, bf16[8,1536,256]{2,1,0:T(8,128)(2,1)S(1)} %get-tuple-element.57.weights, f32[256,256]{1,0:T(8,128)S(1)} %get-tuple-element.70.near, ...), custom_call_target="tpu_custom_call" | custom-call | flops 905969664 | bytes 7864320 | tf_op jit(solution)/shard_map/pallas_call | solution.py:425
  37.8 1.1 %collective-permute-done.7.source = f32[256,256]{1,0:T(8,128)S(1)} collective-permute-done((f32[256,256]{1,0:T(8,128)S(1)}, f32[256,256]{1,0:T(8,128)S(1)}, u32[]{:S(2)}, u32[]{:S(2)}) %collective-permute-start.7) | collective-permute-done | bytes 262176 | tf_op jit(solution)/shard_map/ppermute | solution.py:446
  39.9 1.8 %collective-permute-done.6.source = f32[256,256]{1,0:T(8,128)S(1)} collective-permute-done((f32[256,256]{1,0:T(8,128)S(1)}, f32[256,256]{1,0:T(8,128)S(1)}, u32[]{:S(2)}, u32[]{:S(2)}) %collective-permute-start.6) | collective-permute-done | bytes 262176 | tf_op jit(solution)/shard_map/ppermute | solution.py:446
  42.3 1.1 %collective-permute-start.14 = (f32[256,256]{1,0:T(8,128)S(1)}, f32[256,256]{1,0:T(8,128)S(1)}, u32[]{:S(2)}, u32[]{:S(2)}) collective-permute-start(f32[256,256]{1,0:T(8,128)S(1)} %get-tuple-element.77.far), channel_id=1, source_target_pairs={{0,4},{1,3},{2,10},{3,1},{4,0},{5,7},{6,14},{7,5},{8,16},{9,11},{1... | collective-permute-start | bytes 786440 | tf_op jit(solution)/shard_map/ppermute | solution.py:446
  44.4 1.7 %shard_map.106 = (f32[256,256]{1,0:T(8,128)S(1)}, f32[256,256]{1,0:T(8,128)S(1)}) custom-call(f32[256,256]{1,0:T(8,128)S(1)} %get-tuple-element.74.near, f32[256,256]{1,0:T(8,128)S(1)} %get-tuple-element.77.far, bf16[1,1536,256]{2,1,0:T(8,128)(2,1)S(1)} %get-tuple-element.68.h_ref, bf16[8,1536,256]{2,1,0:T(8,128)(2,1)S(1)} %get-tuple-element.57.weights, ...), custom_call_target="tpu_custom_call" | custom-call | flops 1107296256 | bytes 8134656 | tf_op jit(solution)/shard_map/pallas_call | solution.py:425
  46.1 1.3 %shard_map.107 = (f32[256,256]{1,0:T(8,128)S(1)}, f32[256,256]{1,0:T(8,128)S(1)}) custom-call(f32[256,256]{1,0:T(8,128)S(1)} %collective-permute-done.11.one, f32[256,256]{1,0:T(8,128)S(1)} %collective-permute-done.12.two, bf16[8,1536,256]{2,1,0:T(8,128)(2,1)S(1)} %get-tuple-element.57.weights, f32[256,256]{1,0:T(8,128)S(1)} %get-tuple-element.78.near, ...), custom_call_target="tpu_custom_call" | custom-call | flops 905969664 | bytes 7864320 | tf_op jit(solution)/shard_map/pallas_call | solution.py:425
  47.4 1.3 %collective-permute-done.14.source = f32[256,256]{1,0:T(8,128)S(1)} collective-permute-done((f32[256,256]{1,0:T(8,128)S(1)}, f32[256,256]{1,0:T(8,128)S(1)}, u32[]{:S(2)}, u32[]{:S(2)}) %collective-permute-start.14) | collective-permute-done | bytes 262176 | tf_op jit(solution)/shard_map/ppermute | solution.py:446
  49.2 2.4 %collective-permute-done.10.source = f32[256,256]{1,0:T(8,128)S(1)} collective-permute-done((f32[256,256]{1,0:T(8,128)S(1)}, f32[256,256]{1,0:T(8,128)S(1)}, u32[]{:S(2)}, u32[]{:S(2)}) %collective-permute-start.10) | collective-permute-done | bytes 262176 | tf_op jit(solution)/shard_map/ppermute | solution.py:446
  55.3 1.9 %shard_map.111 = (f32[256,256]{1,0:T(8,128)S(1)}, f32[256,256]{1,0:T(8,128)S(1)}) custom-call(f32[256,256]{1,0:T(8,128)S(1)} %get-tuple-element.85.near, f32[256,256]{1,0:T(8,128)S(1)} %get-tuple-element.82.far, bf16[1,1536,256]{2,1,0:T(8,128)(2,1)S(1)} %get-tuple-element.86.h_ref, bf16[8,1536,256]{2,1,0:T(8,128)(2,1)S(1)} %get-tuple-element.57.weights, ...), custom_call_target="tpu_custom_call" | custom-call | flops 1107296256 | bytes 8134656 | tf_op jit(solution)/shard_map/pallas_call | solution.py:425
  57.2 1.3 %shard_map.112 = (f32[256,256]{1,0:T(8,128)S(1)}, f32[256,256]{1,0:T(8,128)S(1)}) custom-call(f32[256,256]{1,0:T(8,128)S(1)} %collective-permute-done.16.one, f32[256,256]{1,0:T(8,128)S(1)} %collective-permute-done.17.two, bf16[8,1536,256]{2,1,0:T(8,128)(2,1)S(1)} %get-tuple-element.57.weights, f32[256,256]{1,0:T(8,128)S(1)} %get-tuple-element.87.near, ...), custom_call_target="tpu_custom_call" | custom-call | flops 905969664 | bytes 7864320 | tf_op jit(solution)/shard_map/pallas_call | solution.py:425
  58.5 1.1 %collective-permute-done.15.source = f32[256,256]{1,0:T(8,128)S(1)} collective-permute-done((f32[256,256]{1,0:T(8,128)S(1)}, f32[256,256]{1,0:T(8,128)S(1)}, u32[]{:S(2)}, u32[]{:S(2)}) %collective-permute-start.15) | collective-permute-done | bytes 262176 | tf_op jit(solution)/shard_map/ppermute | solution.py:446
  60.5 1.9 %collective-permute-done.13.source = f32[256,256]{1,0:T(8,128)S(1)} collective-permute-done((f32[256,256]{1,0:T(8,128)S(1)}, f32[256,256]{1,0:T(8,128)S(1)}, u32[]{:S(2)}, u32[]{:S(2)}) %collective-permute-start.13) | collective-permute-done | bytes 262176 | tf_op jit(solution)/shard_map/ppermute | solution.py:446
  62.9 2.4 %collective-permute-start.18 = (f32[256,256]{1,0:T(8,128)S(1)}, f32[256,256]{1,0:T(8,128)S(1)}, u32[]{:S(2)}, u32[]{:S(2)}) collective-permute-start(f32[256,256]{1,0:T(8,128)S(1)} %get-tuple-element.93.first_sent), channel_id=1, source_target_pairs={{0,16},{1,2},{2,6},{3,4},{4,1},{5,3},{6,7},{7,5},{8,14},{9,12},{10... | collective-permute-start | bytes 786440 | tf_op jit(solution)/shard_map/ppermute | solution.py:446
  65.2 4.1 %collective-permute-done.18.first = f32[256,256]{1,0:T(8,128)S(1)} collective-permute-done((f32[256,256]{1,0:T(8,128)S(1)}, f32[256,256]{1,0:T(8,128)S(1)}, u32[]{:S(2)}, u32[]{:S(2)}) %collective-permute-start.18) | collective-permute-done | bytes 262176 | tf_op jit(solution)/shard_map/ppermute | solution.py:446
  69.3 3.2 %collective-permute-done.19.second = f32[256,256]{1,0:T(8,128)S(1)} collective-permute-done((f32[256,256]{1,0:T(8,128)S(1)}, f32[256,256]{1,0:T(8,128)S(1)}, u32[]{:S(2)}, u32[]{:S(2)}) %collective-permute-start.19) | collective-permute-done | bytes 262176 | tf_op jit(solution)/shard_map/ppermute | solution.py:446
  72.5 1.0 %shard_map.116 = f32[1,2,256,256]{3,2,1,0:T(8,128)} custom-call(f32[256,256]{1,0:T(8,128)S(1)} %collective-permute-done.18.first, f32[256,256]{1,0:T(8,128)S(1)} %collective-permute-done.19.second, f32[256,256]{1,0:T(8,128)S(1)} %get-tuple-element.93.first_sent, f32[256,256]{1,0:T(8,128)S(1)} %get-tuple-element.94.second_sent), custom_call_target="tpu_custom_call" | custom-call | bytes 1572864 | tf_op jit(solution)/shard_map/pallas_call | solution.py:425
  (46 shorter events, 14.6 us)
Async XLA Ops:
  2.0 10.6 %collective-permute-start.2 = (f32[264,256]{1,0:T(8,128)}, f32[264,256]{1,0:T(8,128)S(1)}, u32[]{:S(2)}, u32[]{:S(2)}) collective-permute-start(f32[264,256]{1,0:T(8,128)} %shard_map.93), channel_id=1, source_target_pairs={{0,16},{1,4},{2,1},{3,5},{4,3},{5,7},{6,2},{7,6},{8,10},{9,14},{10... | collective-permute-start | bytes 811016 | tf_op jit(solution)/shard_map/ppermute | solution.py:446
  5.5 11.8 %collective-permute-start = (f32[264,256]{1,0:T(8,128)}, f32[264,256]{1,0:T(8,128)S(1)}, u32[]{:S(2)}, u32[]{:S(2)}) collective-permute-start(f32[264,256]{1,0:T(8,128)} %shard_map.91), channel_id=1, source_target_pairs={{0,4},{1,0},{2,5},{3,1},{4,7},{5,3},{6,22},{7,2},{8,14},{9,10},{10... | collective-permute-start | bytes 811016 | tf_op jit(solution)/shard_map/ppermute | solution.py:446
  12.6 16.1 %collective-permute-start.4 = (f32[264,256]{1,0:T(8,128)S(1)}, f32[264,256]{1,0:T(8,128)S(1)}, u32[]{:S(2)}, u32[]{:S(2)}) collective-permute-start(f32[264,256]{1,0:T(8,128)S(1)} %broadcast_select_fusion.array), channel_id=1, source_target_pairs={{0,1},{1,0},{2,3},{3,2},{4,5},{5,4},{6,7},{7,6},{8,9},{9,8},{10,11... | collective-permute-start | bytes 811016 | tf_op jit(solution)/shard_map/ppermute | solution.py:446
  17.3 11.4 %collective-permute-start.5 = (f32[264,256]{1,0:T(8,128)S(1)}, f32[264,256]{1,0:T(8,128)S(1)}, u32[]{:S(2)}, u32[]{:S(2)}) collective-permute-start(f32[264,256]{1,0:T(8,128)S(1)} %broadcast_select_fusion.1.array), channel_id=1, source_target_pairs={{0,1},{1,0},{2,3},{3,2},{4,5},{5,4},{6,7},{7,6},{8,9},{9,8},{10,11... | collective-permute-start | bytes 811016 | tf_op jit(solution)/shard_map/ppermute | solution.py:446
  17.4 12.6 %collective-permute-start.3 = (f32[264,256]{1,0:T(8,128)S(1)}, f32[264,256]{1,0:T(8,128)S(1)}, u32[]{:S(2)}, u32[]{:S(2)}) collective-permute-start(f32[264,256]{1,0:T(8,128)S(1)} %broadcast_select_fusion.array), channel_id=1, source_target_pairs={{0,4},{1,3},{2,10},{3,1},{4,0},{5,7},{6,14},{7,5},{8,16},{9,11},{1... | collective-permute-start | bytes 811016 | tf_op jit(solution)/shard_map/ppermute | solution.py:446
  18.4 12.6 %collective-permute-start.1 = (f32[264,256]{1,0:T(8,128)S(1)}, f32[264,256]{1,0:T(8,128)S(1)}, u32[]{:S(2)}, u32[]{:S(2)}) collective-permute-start(f32[264,256]{1,0:T(8,128)S(1)} %broadcast_select_fusion.1.array), channel_id=1, source_target_pairs={{0,4},{1,3},{2,10},{3,1},{4,0},{5,7},{6,14},{7,5},{8,16},{9,11},{1... | collective-permute-start | bytes 811016 | tf_op jit(solution)/shard_map/ppermute | solution.py:446
  19.5 1.1 %copy-start = (f32[3,256,256]{2,1,0:T(8,128)S(1)}, f32[3,256,256]{2,1,0:T(8,128)}, u32[]{:S(2)}) copy-start(f32[3,256,256]{2,1,0:T(8,128)} %couple.1) | copy-start | bytes 2359300
  20.6 1.0 %copy-start.1 = (f32[2,256,256]{2,1,0:T(8,128)S(1)}, f32[2,256,256]{2,1,0:T(8,128)}, u32[]{:S(2)}) copy-start(f32[2,256,256]{2,1,0:T(8,128)} %h_static.1) | copy-start | bytes 1572868
  21.7 1.0 %copy-start.2 = (f32[2,256,256]{2,1,0:T(8,128)S(1)}, f32[2,256,256]{2,1,0:T(8,128)}, u32[]{:S(2)}) copy-start(f32[2,256,256]{2,1,0:T(8,128)} %drive_op.1) | copy-start | bytes 1572868
  22.7 0.7 copy-start.3
  23.4 0.7 copy-start.4
  31.4 5.2 %collective-permute-start.8 = (f32[256,256]{1,0:T(8,128)S(1)}, f32[256,256]{1,0:T(8,128)S(1)}, u32[]{:S(2)}, u32[]{:S(2)}) collective-permute-start(f32[256,256]{1,0:T(8,128)S(1)} %get-tuple-element.67.near), channel_id=1, source_target_pairs={{0,1},{1,0},{2,3},{3,2},{4,5},{5,4},{6,7},{7,6},{8,9},{9,8},{10,11... | collective-permute-start | bytes 786440 | tf_op jit(solution)/shard_map/ppermute | solution.py:446
  31.6 5.0 %collective-permute-start.9 = (f32[256,256]{1,0:T(8,128)S(1)}, f32[256,256]{1,0:T(8,128)S(1)}, u32[]{:S(2)}, u32[]{:S(2)}) collective-permute-start(f32[256,256]{1,0:T(8,128)S(1)} %get-tuple-element.65.far), channel_id=1, source_target_pairs={{0,1},{1,0},{2,3},{3,2},{4,5},{5,4},{6,7},{7,6},{8,9},{9,8},{10,11... | collective-permute-start | bytes 786440 | tf_op jit(solution)/shard_map/ppermute | solution.py:446
  32.6 6.4 %collective-permute-start.7 = (f32[256,256]{1,0:T(8,128)S(1)}, f32[256,256]{1,0:T(8,128)S(1)}, u32[]{:S(2)}, u32[]{:S(2)}) collective-permute-start(f32[256,256]{1,0:T(8,128)S(1)} %get-tuple-element.67.near), channel_id=1, source_target_pairs={{0,4},{1,3},{2,10},{3,1},{4,0},{5,7},{6,14},{7,5},{8,16},{9,11},{1... | collective-permute-start | bytes 786440 | tf_op jit(solution)/shard_map/ppermute | solution.py:446
  33.5 8.3 %collective-permute-start.6 = (f32[256,256]{1,0:T(8,128)S(1)}, f32[256,256]{1,0:T(8,128)S(1)}, u32[]{:S(2)}, u32[]{:S(2)}) collective-permute-start(f32[256,256]{1,0:T(8,128)S(1)} %get-tuple-element.65.far), channel_id=1, source_target_pairs={{0,4},{1,3},{2,10},{3,1},{4,0},{5,7},{6,14},{7,5},{8,16},{9,11},{1... | collective-permute-start | bytes 786440 | tf_op jit(solution)/shard_map/ppermute | solution.py:446
  39.4 6.7 %collective-permute-start.12 = (f32[256,256]{1,0:T(8,128)S(1)}, f32[256,256]{1,0:T(8,128)S(1)}, u32[]{:S(2)}, u32[]{:S(2)}) collective-permute-start(f32[256,256]{1,0:T(8,128)S(1)} %get-tuple-element.77.far), channel_id=1, source_target_pairs={{0,1},{1,0},{2,3},{3,2},{4,5},{5,4},{6,7},{7,6},{8,9},{9,8},{10,11... | collective-permute-start | bytes 786440 | tf_op jit(solution)/shard_map/ppermute | solution.py:446
  42.2 3.9 %collective-permute-start.11 = (f32[256,256]{1,0:T(8,128)S(1)}, f32[256,256]{1,0:T(8,128)S(1)}, u32[]{:S(2)}, u32[]{:S(2)}) collective-permute-start(f32[256,256]{1,0:T(8,128)S(1)} %get-tuple-element.74.near), channel_id=1, source_target_pairs={{0,1},{1,0},{2,3},{3,2},{4,5},{5,4},{6,7},{7,6},{8,9},{9,8},{10,11... | collective-permute-start | bytes 786440 | tf_op jit(solution)/shard_map/ppermute | solution.py:446
  42.3 6.4 %collective-permute-start.14 = (f32[256,256]{1,0:T(8,128)S(1)}, f32[256,256]{1,0:T(8,128)S(1)}, u32[]{:S(2)}, u32[]{:S(2)}) collective-permute-start(f32[256,256]{1,0:T(8,128)S(1)} %get-tuple-element.77.far), channel_id=1, source_target_pairs={{0,4},{1,3},{2,10},{3,1},{4,0},{5,7},{6,14},{7,5},{8,16},{9,11},{1... | collective-permute-start | bytes 786440 | tf_op jit(solution)/shard_map/ppermute | solution.py:446
  43.4 8.2 %collective-permute-start.10 = (f32[256,256]{1,0:T(8,128)S(1)}, f32[256,256]{1,0:T(8,128)S(1)}, u32[]{:S(2)}, u32[]{:S(2)}) collective-permute-start(f32[256,256]{1,0:T(8,128)S(1)} %get-tuple-element.74.near), channel_id=1, source_target_pairs={{0,4},{1,3},{2,10},{3,1},{4,0},{5,7},{6,14},{7,5},{8,16},{9,11},{1... | collective-permute-start | bytes 786440 | tf_op jit(solution)/shard_map/ppermute | solution.py:446
  52.0 5.2 %collective-permute-start.16 = (f32[256,256]{1,0:T(8,128)S(1)}, f32[256,256]{1,0:T(8,128)S(1)}, u32[]{:S(2)}, u32[]{:S(2)}) collective-permute-start(f32[256,256]{1,0:T(8,128)S(1)} %get-tuple-element.85.near), channel_id=1, source_target_pairs={{0,1},{1,0},{2,3},{3,2},{4,5},{5,4},{6,7},{7,6},{8,9},{9,8},{10,11... | collective-permute-start | bytes 786440 | tf_op jit(solution)/shard_map/ppermute | solution.py:446
  52.5 4.7 %collective-permute-start.17 = (f32[256,256]{1,0:T(8,128)S(1)}, f32[256,256]{1,0:T(8,128)S(1)}, u32[]{:S(2)}, u32[]{:S(2)}) collective-permute-start(f32[256,256]{1,0:T(8,128)S(1)} %get-tuple-element.82.far), channel_id=1, source_target_pairs={{0,1},{1,0},{2,3},{3,2},{4,5},{5,4},{6,7},{7,6},{8,9},{9,8},{10,11... | collective-permute-start | bytes 786440 | tf_op jit(solution)/shard_map/ppermute | solution.py:446
  53.2 6.4 %collective-permute-start.15 = (f32[256,256]{1,0:T(8,128)S(1)}, f32[256,256]{1,0:T(8,128)S(1)}, u32[]{:S(2)}, u32[]{:S(2)}) collective-permute-start(f32[256,256]{1,0:T(8,128)S(1)} %get-tuple-element.85.near), channel_id=1, source_target_pairs={{0,4},{1,3},{2,10},{3,1},{4,0},{5,7},{6,14},{7,5},{8,16},{9,11},{1... | collective-permute-start | bytes 786440 | tf_op jit(solution)/shard_map/ppermute | solution.py:446
  54.2 8.2 %collective-permute-start.13 = (f32[256,256]{1,0:T(8,128)S(1)}, f32[256,256]{1,0:T(8,128)S(1)}, u32[]{:S(2)}, u32[]{:S(2)}) collective-permute-start(f32[256,256]{1,0:T(8,128)S(1)} %get-tuple-element.82.far), channel_id=1, source_target_pairs={{0,4},{1,3},{2,10},{3,1},{4,0},{5,7},{6,14},{7,5},{8,16},{9,11},{1... | collective-permute-start | bytes 786440 | tf_op jit(solution)/shard_map/ppermute | solution.py:446
  62.9 6.4 %collective-permute-start.18 = (f32[256,256]{1,0:T(8,128)S(1)}, f32[256,256]{1,0:T(8,128)S(1)}, u32[]{:S(2)}, u32[]{:S(2)}) collective-permute-start(f32[256,256]{1,0:T(8,128)S(1)} %get-tuple-element.93.first_sent), channel_id=1, source_target_pairs={{0,16},{1,2},{2,6},{3,4},{4,1},{5,3},{6,7},{7,5},{8,14},{9,12},{10... | collective-permute-start | bytes 786440 | tf_op jit(solution)/shard_map/ppermute | solution.py:446
  65.2 7.3 %collective-permute-start.19 = (f32[256,256]{1,0:T(8,128)S(1)}, f32[256,256]{1,0:T(8,128)S(1)}, u32[]{:S(2)}, u32[]{:S(2)}) collective-permute-start(f32[256,256]{1,0:T(8,128)S(1)} %get-tuple-element.94.second_sent), channel_id=1, source_target_pairs={{0,1},{1,3},{2,7},{3,5},{4,0},{5,2},{6,22},{7,4},{8,15},{9,13},{10... | collective-permute-start | bytes 786440 | tf_op jit(solution)/shard_map/ppermute | solution.py:446
